TPU v7x, 128 devices: a whole 4x4x4 slice. The times are simulated.
128 devices in a mesh: blk: 64 (over x, z, y_lo, core), rep: 2 (over y_hi).
Axes of the slice: x: 4, y: 4 (y_hi: 2, y_lo: 2; y = y_hi * 2 + y_lo), z: 4, core: 2. Of those that a mesh axis runs over, the one named last changes fastest.
Arguments:
- features: bfloat16 [16384, 128], P('blk'), may hold values from -6 to 6
- tile_values: bfloat16 [64, 64, 16, 128, 128], P('blk', 'rep'), may hold values from -0.046875 to 0.046875
- tile_target: int32 [64, 64, 16], P('blk', 'rep'), may hold values from 0 to 1
- tile_source: int32 [64, 64, 16], P('blk', 'rep'), may hold values from 0 to 1
- tile_count: int32 [64, 64], P('blk', 'rep'), may hold values from 0 to 16, as said below
- hub_list: int32 [64, 64, 16], P('blk'), may hold values from 0 to 255
- hub_count: int32 [64, 64], P('blk'), may hold values from 0 to 16, as said below
- hub_weight: bfloat16 [64, 16, 16384], P(None, None, 'blk'), may hold values from -0.1875 to 0.1875
- self_weight: bfloat16 [128, 256], P(None, 'rep'), may hold values from -0.5 to 0.5
- neighbor_weight: bfloat16 [128, 256], P(None, 'rep'), may hold values from -0.5 to 0.5
- bias: float32 [256], P('rep'), may hold values from -3 to 3
- cotangent: bfloat16 [16384, 256], P('blk', 'rep'), may hold values from -6 to 6
Outputs:
- output: bfloat16 [16384, 256], P('blk', 'rep')
- grad_input: bfloat16 [16384, 128], P('blk')
- grad_self: float32 [128, 256], P(None, 'rep')
- grad_neighbor: float32 [128, 256], P(None, 'rep')
- grad_bias: float32 [256], P('rep')
Inputs may be any that keep to these rules, and one draw needn't show every extreme that they name: Slots at or beyond tile_count of a pair of blocks carry values that no output reads. Offset 0 of every destination block has all 16 slots live; some destination blocks may have many slots live at every offset. Coordinates may repeat within a pair; their terms add. `hub_list`: entries may repeat within one list; slots at or beyond hub_count are unused. `hub_count`: every sending block s uses all 16 slots for the reading block (s + 1) mod 64.
All inputs are finite; a program needn't handle non-finite values.
Results may differ from a plain program's by a relative error of at most 0.0056.
Values may be sent and summed in bfloat16 or wider, within the bound.
No kernel may reach another device: no remote copies, remote signals or barrier semaphores. Data moves between devices by JAX's collectives and lax.ppermute only.
A program may use at most 64 MiB of HBM per device.

v0:
```python
import functools
import math

import jax
import jax.numpy as jnp
from jax import lax
from jax.experimental import pallas as pl
from jax.experimental.pallas import tpu as pltpu
from jax.sharding import PartitionSpec as P


AXES = ("blk", "rep")
COLS = 9
SLOTS = 4 * COLS
HEAD = 16
GROUP = 2 * (256 + HEAD)
BACK = 128 + 8
MIB = 2**20


def route(source_of):
    pairs = []
    for block in range(64):
        for r in range(2):
            q, l, c = block // 4, (block // 2) % 2, block % 2
            q2, l2, c2, r2 = source_of(q, l, c, r)
            pairs.append(((((q2 % 16) * 2 + l2 % 2) * 2 + c2 % 2) * 2 + r2 % 2, block * 2 + r))
    return pairs


def inverse(pairs):
    return [(d, s) for s, d in pairs]


def y_step(step):
    def source(q, l, c, r):
        y = (2 * r + l + step(c)) % 4
        return (q, y % 2, c, y // 2)

    return route(source)


SWAP_Y = y_step(lambda c: 1 if c else -1)
FROM_DOWN = y_step(lambda c: -1)
FROM_UP = y_step(lambda c: 1)
SWAP_C = route(lambda q, l, c, r: (q, l, c + 1, r))
SWAP_R = route(lambda q, l, c, r: (q, l, c, r + 1))
FROM_COL = [route(lambda q, l, c, r, k=k: (q + (k if r else -k), l, c, r)) for k in range(5)]


def permute(x, pairs):
    return lax.ppermute(x, AXES, pairs)


def as_bf16(x):
    return lax.reduce_precision(x, 8, 7)


def dot(a, b):
    return jnp.dot(a, b, preferred_element_type=jnp.float32)


def dot_nt(a, b):
    return lax.dot_general(a, b, (((1,), (1,)), ((), ())), preferred_element_type=jnp.float32)


def dot_tn(a, b):
    return lax.dot_general(a, b, (((0,), (0,)), ((), ())), preferred_element_type=jnp.float32)


def slot_source(ids_ref, cls, k, lr):
    block, r = ids_ref[0], ids_ref[1]
    q = lax.bitwise_and(block // 4 + jnp.where(r == 1, k, -k) + 16, 15)
    source = q * 4 + lax.bitwise_xor(lax.bitwise_and(block, 3), lr * 2 + cls)
    offset = lax.bitwise_and(block - source + 64, 63) - 32 * r
    return source, jnp.logical_and(offset >= 0, offset < 32)


def offset_slot(ids_ref, offset):
    block, r = ids_ref[0], ids_ref[1]
    source = lax.bitwise_and(block - offset - 32 * r + 128, 63)
    k = lax.bitwise_and((block // 4 - source // 4) * jnp.where(r == 1, -1, 1) + 16, 15)
    differ = lax.bitwise_xor(lax.bitwise_and(block, 3), lax.bitwise_and(source, 3))
    return (lax.bitwise_and(differ, 1) * COLS + k) * 2 + differ // 2


def vmem():
    return pl.BlockSpec(memory_space=pltpu.VMEM)


def smem():
    return pl.BlockSpec(memory_space=pltpu.SMEM)


def kernel_call(body, n_in, outs, scratch=(), limit=8 * MIB):
    single = not isinstance(outs, list)
    shapes = [jax.ShapeDtypeStruct(*o) for o in ([outs] if single else outs)]

    def call(*args):
        return pl.pallas_call(
            body,
            in_specs=[smem()] + [vmem()] * n_in,
            out_specs=vmem() if single else [vmem()] * len(shapes),
            out_shape=shapes[0] if single else shapes,
            scratch_shapes=list(scratch),
            compiler_params=pltpu.CompilerParams(vmem_limit_bytes=limit),
        )(*args)

    return call


STEP = 4


def densify_kernel(ids_ref, count_ref, code_ref, tiles_ref, out_ref, acc_ref):
    step = pl.program_id(0)

    @pl.when(step == 0)
    def _():
        for cls in range(2):
            for k in (0, COLS - 1):
                for lr in range(2):
                    _, valid = slot_source(ids_ref, cls, k, lr)

                    @pl.when(jnp.logical_not(valid))
                    def _():
                        out_ref[(cls * COLS + k) * 2 + lr] = jnp.zeros((256, 256), jnp.bfloat16)

    for u in range(STEP):
        offset = step * STEP + u
        acc_ref[...] = jnp.zeros_like(acc_ref)

        def add(j, carry):
            code = code_ref[offset * 16 + j]
            acc_ref[code] += tiles_ref[0, u, j].astype(jnp.float32)
            return carry

        lax.fori_loop(0, count_ref[offset], add, 0)
        slot = offset_slot(ids_ref, offset)
        for t in range(2):
            for s in range(2):
                out_ref[slot, t * 128 : (t + 1) * 128, s * 128 : (s + 1) * 128] = acc_ref[
                    t * 2 + s
                ].astype(jnp.bfloat16)


def densify(ids, tile_values, tile_target, tile_source, tile_count):
    offsets, slots = tile_target.shape[1:]
    code = (tile_target[0] * 2 + tile_source[0]).reshape(-1)
    return pl.pallas_call(
        densify_kernel,
        grid_spec=pltpu.PrefetchScalarGridSpec(
            num_scalar_prefetch=3,
            grid=(offsets // STEP,),
            in_specs=[pl.BlockSpec((1, STEP, slots, 128, 128), lambda o, i, n, c: (0, o, 0, 0, 0))],
            out_specs=pl.BlockSpec((SLOTS, 256, 256), lambda o, i, n, c: (0, 0, 0)),
            scratch_shapes=[pltpu.VMEM((4, 128, 128), jnp.float32)],
        ),
        out_shape=jax.ShapeDtypeStruct((SLOTS, 256, 256), jnp.bfloat16),
        compiler_params=pltpu.CompilerParams(vmem_limit_bytes=20 * MIB),
        name="densify",
    )(ids, tile_count[0], code, tile_values)


def forward_kernel(ids_ref, *refs):
    groups, (mats_ref, hub_ref, out_ref, hot_ref, pick_ref, wts_ref) = refs[:6], refs[6:]
    lane = lax.broadcasted_iota(jnp.int32, (2 * HEAD, 128), 1)
    column = lax.broadcasted_iota(jnp.int32, (2 * HEAD, 256), 1)
    total = None
    for cls in range(2):
        for k in range(COLS):
            part = 0 if k == 0 else (1 if k < 5 else 2)
            ref, base = groups[cls * 3 + part], (0 if k == 0 else (k - 1) % 4) * GROUP
            head = ref[base + 512 : base + GROUP, :].astype(jnp.float32)
            mine = jnp.sum(jnp.where(lane == ids_ref[0], head, 0.0), axis=1, keepdims=True)
            hot = (mine.astype(jnp.int32) == column).astype(jnp.float32).astype(jnp.bfloat16)
            for lr in range(2):
                slot = (cls * COLS + k) * 2 + lr
                source, valid = slot_source(ids_ref, cls, k, lr)
                at = slice(slot * HEAD, (slot + 1) * HEAD)
                one = hot[lr * HEAD : (lr + 1) * HEAD, :]
                block = ref[base + lr * 256 : base + (lr + 1) * 256, :]
                both = dot(jnp.concatenate([mats_ref[slot], one], axis=0), block)
                total = both[:256] if total is None else total + both[:256]
                hot_ref[at, :] = one
                pick_ref[at, :] = both[256:].astype(jnp.bfloat16)
                weights = hub_ref[source]
                wts_ref[at, :] = jnp.where(valid, weights, jnp.zeros_like(weights))
    out_ref[...] = total + dot_tn(wts_ref[...], pick_ref[...])


def forward(*args):
    return kernel_call(
        forward_kernel,
        8,
        [
            ((256, 128), jnp.float32),
            ((SLOTS * HEAD, 256), jnp.bfloat16),
            ((SLOTS * HEAD, 128), jnp.bfloat16),
            ((SLOTS * HEAD, 256), jnp.bfloat16),
        ],
        limit=24 * MIB,
    )(*args)


def middle_kernel(
    ids_ref, mine_ref, theirs_ref, feat_ref, sw_ref, nw_ref, ct_ref, bias_ref, other_ref, *outs
):
    out_ref, grad_ref, self_ref, wgrad_ref, bgrad_ref = outs
    first = ids_ref[1] == 0
    feats = feat_ref[...]
    agg = (mine_ref[...] + theirs_ref[...]).astype(jnp.bfloat16)

    def half(sw, nw, ct, bias):
        pre = dot(feats, sw) + dot(agg, nw) + bias
        gate = jax.nn.sigmoid(pre)
        act = ct.astype(jnp.float32) * gate * (1.0 + pre * (1.0 - gate))
        return pre * gate, act.astype(jnp.bfloat16)

    sw, nw = sw_ref[...], nw_ref[...]
    sw2, nw2 = other_ref[0:128, :], other_ref[128:256, :]
    extra = other_ref[512:528, :].astype(jnp.float32)
    bias2 = extra[0:1] + extra[1:2] + extra[2:3]
    value, act = half(sw, nw, ct_ref[...], bias_ref[...])
    _, act2 = half(sw2, nw2, other_ref[256:512, :], bias2)
    out_ref[...] = value.astype(jnp.bfloat16)
    grad_ref[...] = (dot_nt(nw, act) + dot_nt(nw2, act2)).astype(jnp.bfloat16)
    self_ref[...] = dot_nt(sw, act) + dot_nt(sw2, act2)
    bgrad_ref[...] = jnp.zeros_like(bgrad_ref)
    for h in range(2):
        now = jnp.where(first, act2, act) if h else jnp.where(first, act, act2)
        wgrad_ref[h * 256 : h * 256 + 128, :] = dot_tn(now, feats)
        wgrad_ref[h * 256 + 128 : h * 256 + 256, :] = dot_tn(now, agg)
        bgrad_ref[h : h + 1, :] = jnp.sum(now.astype(jnp.float32), axis=0, keepdims=True)


def middle(*args):
    return kernel_call(
        middle_kernel,
        8,
        [
            ((256, 128), jnp.bfloat16),
            ((128, 256), jnp.bfloat16),
            ((128, 256), jnp.float32),
            ((512, 128), jnp.float32),
            ((8, 128), jnp.float32),
        ],
    )(*args)


def backward_kernel(cls, columns, add, ids_ref, grad_ref, mats_ref, wts_ref, hot_ref, wg_ref, bg_ref, *refs):
    out_ref = refs[-1]
    grad = grad_ref[...]
    for i, k in enumerate(columns):
        for lr in range(2):
            slot = (cls * COLS + k) * 2 + lr
            at = slice(slot * HEAD, (slot + 1) * HEAD)
            lanes = slice(lr * 256, (lr + 1) * 256)
            source, valid = slot_source(ids_ref, cls, k, lr)
            back = dot_nt(grad, wts_ref[at, :]).astype(jnp.bfloat16)
            part = dot(grad, mats_ref[slot]) + dot(back, hot_ref[at, :])
            chunk = wg_ref[pl.ds(pl.multiple_of(source * 8, 8), 8), :]
            chunk = jnp.concatenate([chunk, bg_ref[...]], axis=1)
            chunk = jnp.where(valid, chunk, 0.0)
            if add:
                part += refs[0][i, 0:128, lanes].astype(jnp.float32)
                chunk += refs[0][i, 128:BACK, lanes].astype(jnp.float32)
            out_ref[i, 0:128, lanes] = part.astype(out_ref.dtype)
            out_ref[i, 128:BACK, lanes] = chunk.astype(out_ref.dtype)


def backward(cls, columns, dtype, ids, args, got=None):
    body = functools.partial(backward_kernel, cls, columns, got is not None)
    more = () if got is None else (got,)
    shape = (len(columns), BACK, 512)
    return kernel_call(body, 6 + len(more), (shape, dtype), limit=20 * MIB)(ids, *args, *more)


def near_kernel(ids_ref, keep_ref, far_ref, *outs):
    for i, out in enumerate(outs):
        out[...] = (keep_ref[i + 1] + far_ref[i].astype(jnp.float32)).astype(jnp.bfloat16)


def mine_kernel(ids_ref, keep_ref, *refs):
    got, (same_ref, cross_ref) = refs[:4], refs[4:]
    total = keep_ref[0]
    for ref in got:
        total += ref[...].astype(jnp.float32)
    same_ref[...] = total[:, :256].astype(jnp.bfloat16)
    cross_ref[...] = total[:, 256:].astype(jnp.bfloat16)


def finish_kernel(ids_ref, same_ref, rep_ref, down_ref, up_ref, self_ref, grad_ref, pay_ref):
    f32 = jnp.float32
    total = (same_ref[...].astype(f32) + rep_ref[...].astype(f32)) + (
        down_ref[...].astype(f32) + up_ref[...].astype(f32)
    )
    grad_ref[...] = (total[:128] + self_ref[...]).T.astype(jnp.bfloat16)
    useful = ids_ref[0] // 32 == ids_ref[1]
    pay = jnp.where(useful, total[128:, :128], total[128:, 128:])
    pay_ref[...] = jnp.broadcast_to(pay[None], pay_ref.shape)


def weights_kernel(scale, ids_ref, got_ref, self_ref, neighbor_ref, bias_ref):
    r = ids_ref[1]
    start = pl.multiple_of(r * 256, 256)
    self_ref[...] = got_ref[pl.ds(start, 128), :].T * scale
    neighbor_ref[...] = got_ref[pl.ds(start + 128, 128), :].T * scale
    rows = got_ref[pl.ds(pl.multiple_of(256 - start, 256), 8), :]
    row = lax.broadcasted_iota(jnp.int32, rows.shape, 0)
    bias_ref[...] = jnp.sum(jnp.where(row == r, rows, 0.0), axis=0, keepdims=True) * scale


def layer(
    features,
    tile_values,
    tile_target,
    tile_source,
    tile_count,
    hub_list,
    hub_count,
    hub_weight,
    self_weight,
    neighbor_weight,
    bias,
    cotangent,
):
    f32, bf16 = jnp.float32, jnp.bfloat16
    blocks = lax.axis_size("blk")
    ids = jnp.stack([lax.axis_index("blk"), lax.axis_index("rep")]).astype(jnp.int32)

    live = jnp.arange(HEAD, dtype=jnp.int32)[None, :] < hub_count[0][:, None]
    lists = jnp.where(live, hub_list[0], -1).astype(bf16).T
    lists = jnp.pad(lists, ((0, 0), (0, 128 - blocks)), constant_values=-1)
    block = jnp.concatenate([features, lists], axis=0)
    theirs = permute(block, SWAP_Y)

    bias_hi = as_bf16(bias)
    bias_mid = as_bf16(bias - bias_hi)
    bias_lo = bias - bias_hi - bias_mid
    bias_rows = jnp.stack([bias_hi, bias_mid, bias_lo]).astype(bf16)
    bias_rows = jnp.pad(bias_rows, ((0, 13), (0, 0)))
    packed = jnp.concatenate([self_weight, neighbor_weight, cotangent, bias_rows], axis=0)
    other = permute(packed, SWAP_R)

    col0 = jnp.concatenate([features, theirs[:256], lists, theirs[256:]], axis=0)
    cols = [permute(col0, FROM_COL[k]) for k in range(1, 5)]
    oth0 = permute(col0, SWAP_C)
    cols = jnp.concatenate(cols, axis=0)
    far = permute(cols, FROM_COL[4])
    oth1 = permute(cols, SWAP_C)
    mats = densify(ids, tile_values, tile_target, tile_source, tile_count)
    oth2 = permute(far, SWAP_C)

    partial, hot, _, wts = forward(ids, col0, cols, far, oth0, oth1, oth2, mats, hub_weight)
    theirs = permute(partial, SWAP_R)
    output, grad, self_grad, wgrad, bgrad = middle(
        ids,
        partial,
        theirs,
        features,
        self_weight,
        neighbor_weight,
        cotangent,
        bias[None, :],
        other,
    )

    shared = (grad, mats, wts, hot, wgrad, bgrad)
    near_cols, far_cols = tuple(range(5)), tuple(range(5, 9))
    got_far = permute(backward(1, far_cols, bf16, ids, shared), SWAP_C)
    got_near = permute(backward(1, near_cols, bf16, ids, shared), SWAP_C)
    sent = backward(0, far_cols, bf16, ids, shared, got_far)
    far_sums = permute(sent, inverse(FROM_COL[4]))
    keep = backward(0, near_cols, f32, ids, shared, got_near)
    piece = ((BACK, 512), bf16)
    near = kernel_call(near_kernel, 2, [piece] * 4)(ids, keep, far_sums)
    got = [permute(near[k - 1], inverse(FROM_COL[k])) for k in range(1, 5)]
    piece = ((BACK, 256), bf16)
    same, cross = kernel_call(mine_kernel, 5, [piece] * 2)(ids, keep, *got)
    over = permute(same, SWAP_R)
    down = permute(cross, FROM_DOWN)
    up = permute(cross, FROM_UP)
    grad_input, pay = kernel_call(
        finish_kernel, 5, [((256, 128), bf16), ((blocks, 8, 128), f32)]
    )(ids, same, over, down, up, self_grad)
    whole = lax.all_to_all(pay, "blk", 0, 0, tiled=True).reshape(blocks * 8, 128)
    scale = 1.0 / math.sqrt(256 * blocks)
    grad_self, grad_neighbor, grad_bias = kernel_call(
        functools.partial(weights_kernel, scale),
        1,
        [((128, 128), f32), ((128, 128), f32), ((1, 128), f32)],
    )(ids, whole)
    return output, grad_input, grad_self, grad_neighbor, grad_bias[0]


def solution(mesh):
    in_specs = (
        P("blk", None),
        P("blk", "rep", None, None, None),
        P("blk", "rep", None),
        P("blk", "rep", None),
        P("blk", "rep"),
        P("blk", None, None),
        P("blk", None),
        P(None, None, "blk"),
        P(None, "rep"),
        P(None, "rep"),
        P("rep"),
        P("blk", "rep"),
    )
    out_specs = (P("blk", "rep"), P("blk", None), P(None, "rep"), P(None, "rep"), P("rep"))
    return jax.shard_map(layer, mesh=mesh, in_specs=in_specs, out_specs=out_specs, check_vma=False)
```

profile of v0, /device:TPU:0, one launch (start us, length us, event | category | flops | bytes accessed | tf_op | source)
XLA Modules:
  0.0 129.9 jit_solution(13280894841517848774)
XLA Ops:
  0.6 0.7 fusion.4
  1.3 0.8 pad_maximum_fusion.2
  2.2 1.7 %collective-permute-start = (bf16[272,128]{1,0:T(8,128)(2,1)S(1)}, bf16[272,128]{1,0:T(8,128)(2,1)S(1)}, u32[]{:S(2)}, u32[]{:S(2)}) collective-permute-start(bf16[272,128]{1,0:T(8,128)(2,1)S(1)} %pad_maximum_fusion.2), channel_id=1, source_target_pairs={{5,0},{4,1},{6,2},{7,3},{0,4},{1,5},{3,6},{2,7},{13,8},{12,9},{14,... | collective-permute-start | bytes 208904 | tf_op jit(solution)/shard_map/ppermute | solution.py:52
  3.9 3.8 %collective-permute-done = bf16[272,128]{1,0:T(8,128)(2,1)S(1)} collective-permute-done((bf16[272,128]{1,0:T(8,128)(2,1)S(1)}, bf16[272,128]{1,0:T(8,128)(2,1)S(1)}, u32[]{:S(2)}, u32[]{:S(2)}) %collective-permute-start) | collective-permute-done | bytes 69664 | tf_op jit(solution)/shard_map/ppermute | solution.py:52
  7.7 0.9 pad_maximum_fusion.refs_0_
  8.6 2.1 %collective-permute-start.1 = (bf16[544,128]{1,0:T(8,128)(2,1)S(1)}, bf16[544,128]{1,0:T(8,128)(2,1)S(1)}, u32[]{:S(2)}, u32[]{:S(2)}) collective-permute-start(bf16[544,128]{1,0:T(8,128)(2,1)S(1)} %pad_maximum_fusion.refs_0_), channel_id=1, source_target_pairs={{120,0},{9,1},{122,2},{11,3},{124,4},{13,5},{126,6},{15,7},{0,8},{... | collective-permute-start | bytes 417800 | tf_op jit(solution)/shard_map/ppermute | solution.py:52
  10.7 3.6 %collective-permute-start.2 = (bf16[544,128]{1,0:T(8,128)(2,1)S(1)}, bf16[544,128]{1,0:T(8,128)(2,1)S(1)}, u32[]{:S(2)}, u32[]{:S(2)}) collective-permute-start(bf16[544,128]{1,0:T(8,128)(2,1)S(1)} %pad_maximum_fusion.refs_0_), channel_id=1, source_target_pairs={{112,0},{17,1},{114,2},{19,3},{116,4},{21,5},{118,6},{23,7},{120,8... | collective-permute-start | bytes 417800 | tf_op jit(solution)/shard_map/ppermute | solution.py:52
  14.3 1.9 %collective-permute-start.3 = (bf16[544,128]{1,0:T(8,128)(2,1)S(1)}, bf16[544,128]{1,0:T(8,128)(2,1)S(1)}, u32[]{:S(2)}, u32[]{:S(2)}) collective-permute-start(bf16[544,128]{1,0:T(8,128)(2,1)S(1)} %pad_maximum_fusion.refs_0_), channel_id=1, source_target_pairs={{104,0},{25,1},{106,2},{27,3},{108,4},{29,5},{110,6},{31,7},{112,8... | collective-permute-start | bytes 417800 | tf_op jit(solution)/shard_map/ppermute | solution.py:52
  16.2 1.5 %collective-permute-start.4 = (bf16[544,128]{1,0:T(8,128)(2,1)S(1)}, bf16[544,128]{1,0:T(8,128)(2,1)S(1)}, u32[]{:S(2)}, u32[]{:S(2)}) collective-permute-start(bf16[544,128]{1,0:T(8,128)(2,1)S(1)} %pad_maximum_fusion.refs_0_), channel_id=1, source_target_pairs={{96,0},{33,1},{98,2},{35,3},{100,4},{37,5},{102,6},{39,7},{104,8},... | collective-permute-start | bytes 417800 | tf_op jit(solution)/shard_map/ppermute | solution.py:52
  17.7 1.8 %collective-permute-done.1 = bf16[544,128]{1,0:T(8,128)(2,1)S(1)} collective-permute-done((bf16[544,128]{1,0:T(8,128)(2,1)S(1)}, bf16[544,128]{1,0:T(8,128)(2,1)S(1)}, u32[]{:S(2)}, u32[]{:S(2)}) %collective-permute-start.1) | collective-permute-done | bytes 139296 | tf_op jit(solution)/shard_map/ppermute | solution.py:52
  19.5 1.4 %collective-permute-done.2 = bf16[544,128]{1,0:T(8,128)(2,1)S(1)} collective-permute-done((bf16[544,128]{1,0:T(8,128)(2,1)S(1)}, bf16[544,128]{1,0:T(8,128)(2,1)S(1)}, u32[]{:S(2)}, u32[]{:S(2)}) %collective-permute-start.2) | collective-permute-done | bytes 139296 | tf_op jit(solution)/shard_map/ppermute | solution.py:52
  21.0 0.4 collective-permute-done.3
  21.4 1.0 collective-permute-done.4
  22.5 0.9 collective-permute-start.5
  23.4 0.7 fusion.7
  24.1 0.0 collective-permute-start.7
  24.1 10.9 %collective-permute-done.5.refs_2_ = bf16[2176,128]{1,0:T(8,128)(2,1)S(1)} collective-permute-done((bf16[2176,128]{1,0:T(8,128)(2,1)S(1)}, bf16[2176,128]{1,0:T(8,128)(2,1)S(1)}, u32[]{:S(2)}, u32[]{:S(2)}) %collective-permute-start.5) | collective-permute-done | bytes 557088 | tf_op jit(solution)/shard_map/ppermute | solution.py:52
  35.0 0.0 collective-permute-start.8
  35.0 0.9 pad_maximum_fusion.1
  35.9 6.1 %collective-permute-start.10 = (bf16[528,128]{1,0:T(8,128)(2,1)S(1)}, bf16[528,128]{1,0:T(8,128)(2,1)S(1)}, u32[]{:S(2)}, u32[]{:S(2)}) collective-permute-start(bf16[528,128]{1,0:T(8,128)(2,1)S(1)} %pad_maximum_fusion.1), channel_id=1, source_target_pairs={{1,0},{0,1},{3,2},{2,3},{5,4},{4,5},{7,6},{6,7},{9,8},{8,9},{11,10... | collective-permute-start | bytes 405512 | tf_op jit(solution)/shard_map/ppermute | solution.py:52
  42.0 0.2 collective-permute-start.6
  42.3 0.7 multiply_add_fusion
  43.0 0.1 pad_add_fusion.ids_ref
  43.1 0.1 copy.17
  43.1 0.1 add.12.code_ref
  43.2 5.8 %copy-done = bf16[1,32,16,128,128]{4,3,2,1,0:T(8,128)(2,1)S(1)} copy-done((bf16[1,32,16,128,128]{4,3,2,1,0:T(8,128)(2,1)S(1)}, bf16[1,32,16,128,128]{4,3,2,1,0:T(8,128)(2,1)}, u32[]{:S(2)}) %copy-start) | copy-done | bytes 16777240
  49.0 0.7 copy-done.7
  49.6 3.1 %densify.1.refs_6_.mats_ref = bf16[36,256,256]{2,1,0:T(8,128)(2,1)S(1)} custom-call(s32[2]{0:T(128)S(1)} %pad_add_fusion.ids_ref, s32[32]{0:T(128)S(1)} %bitcast.23, s32[512]{0:T(512)S(1)} %add.12.code_ref, bf16[1,32,16,128,128]{4,3,2,1,0:T(8,128)(2,1)S(1)} %copy-done), custom_call_target="tpu_custom_call" | custom-call | tf_op jit(solution)/shard_map/densify/pallas_call | solution.py:150
  52.8 0.0 copy-start.1
  52.8 0.0 copy-start.3
  52.8 0.0 copy-start.4
  52.8 0.0 copy-start.5
  52.8 0.0 copy-start.6
  52.8 0.0 collective-permute-done.7.refs_4_
  52.9 0.0 collective-permute-done.8.refs_5_
  52.9 2.8 %shard_map.155 = (f32[256,128]{1,0:T(8,128)S(1)}, bf16[576,256]{1,0:T(8,128)(2,1)S(1)}, bf16[576,128]{1,0:T(8,128)(2,1)}, bf16[576,256]{1,0:T(8,128)(2,1)S(1)}) custom-call(s32[2]{0:T(128)S(1)} %pad_add_fusion.ids_ref, bf16[544,128]{1,0:T(8,128)(2,1)S(1)} %pad_maximum_fusion.refs_0_, bf16[2176,128]{1,0:T(8,128)(2,1)S(1)} %constant_dynamic-update-slice_fusion.refs_1_, ...), custom_call_target="tpu_custom_call" | custom-call | tf_op jit(solution)/shard_map/pallas_call | solution.py:100
  55.7 0.3 collective-permute-start.9
  56.0 7.0 %collective-permute-done.9.theirs_ref = f32[256,128]{1,0:T(8,128)S(1)} collective-permute-done((f32[256,128]{1,0:T(8,128)S(1)}, f32[256,128]{1,0:T(8,128)S(1)}, u32[]{:S(2)}, u32[]{:S(2)}) %collective-permute-start.9) | collective-permute-done | bytes 131104 | tf_op jit(solution)/shard_map/ppermute | solution.py:52
  63.0 1.5 %shard_map.156 = (bf16[256,128]{1,0:T(8,128)(2,1)}, bf16[128,256]{1,0:T(8,128)(2,1)S(1)}, f32[128,256]{1,0:T(8,128)S(1)}, f32[512,128]{1,0:T(8,128)S(1)}, f32[8,128]{1,0:T(8,128)S(1)}) custom-call(s32[2]{0:T(128)S(1)} %pad_add_fusion.ids_ref, f32[256,128]{1,0:T(8,128)S(1)} %get-tuple-element.24.mine_ref, f32[256,128]{1,0:T(8,128)S(1)} %collective-permute-done.9.theirs_ref, ...), custom_call_target="tpu_custom_call" | custom-call | tf_op jit(solution)/shard_map/pallas_call | solution.py:100
  64.6 1.5 %shard_map.159 = bf16[4,136,512]{2,1,0:T(8,128)(2,1)S(1)} custom-call(s32[2]{0:T(128)S(1)} %pad_add_fusion.ids_ref, bf16[128,256]{1,0:T(8,128)(2,1)S(1)} %get-tuple-element.26.grad_ref, bf16[36,256,256]{2,1,0:T(8,128)(2,1)S(1)} %densify.1.refs_6_.mats_ref, bf16[576,256]{1,0:T(8,128)(2,1)S(1)} %get-tuple-element.27.wts_ref, ...), custom_call_target="tpu_custom_call" | custom-call | tf_op jit(solution)/shard_map/pallas_call | solution.py:100
  66.0 0.1 collective-permute-start.12
  66.1 1.7 %shard_map.157 = bf16[5,136,512]{2,1,0:T(8,128)(2,1)S(1)} custom-call(s32[2]{0:T(128)S(1)} %pad_add_fusion.ids_ref, bf16[128,256]{1,0:T(8,128)(2,1)S(1)} %get-tuple-element.26.grad_ref, bf16[36,256,256]{2,1,0:T(8,128)(2,1)S(1)} %densify.1.refs_6_.mats_ref, bf16[576,256]{1,0:T(8,128)(2,1)S(1)} %get-tuple-element.27.wts_ref, ...), custom_call_target="tpu_custom_call" | custom-call | tf_op jit(solution)/shard_map/pallas_call | solution.py:100
  67.8 0.6 collective-permute-start.11
  68.4 0.0 collective-permute-done.12.refs_0_
  68.4 1.5 %shard_map.160 = bf16[4,136,512]{2,1,0:T(8,128)(2,1)S(1)} custom-call(s32[2]{0:T(128)S(1)} %pad_add_fusion.ids_ref, bf16[128,256]{1,0:T(8,128)(2,1)S(1)} %get-tuple-element.26.grad_ref, bf16[36,256,256]{2,1,0:T(8,128)(2,1)S(1)} %densify.1.refs_6_.mats_ref, bf16[576,256]{1,0:T(8,128)(2,1)S(1)} %get-tuple-element.27.wts_ref, ...), custom_call_target="tpu_custom_call" | custom-call | tf_op jit(solution)/shard_map/pallas_call | solution.py:100
  69.8 3.6 %collective-permute-start.13 = (bf16[4,136,512]{2,1,0:T(8,128)(2,1)S(1)}, bf16[4,136,512]{2,1,0:T(8,128)(2,1)S(1)}, u32[]{:S(2)}, u32[]{:S(2)}) collective-permute-start(bf16[4,136,512]{2,1,0:T(8,128)(2,1)S(1)} %shard_map.160), channel_id=1, source_target_pairs={{0,96},{1,33},{2,98},{3,35},{4,100},{5,37},{6,102},{7,39},{8,104},... | collective-permute-start | bytes 1671176 | tf_op jit(solution)/shard_map/ppermute | solution.py:52
  73.5 1.7 %shard_map.158.keep_ref = f32[5,136,512]{2,1,0:T(8,128)S(1)} custom-call(s32[2]{0:T(128)S(1)} %pad_add_fusion.ids_ref, bf16[128,256]{1,0:T(8,128)(2,1)S(1)} %get-tuple-element.26.grad_ref, bf16[36,256,256]{2,1,0:T(8,128)(2,1)S(1)} %densify.1.refs_6_.mats_ref, bf16[576,256]{1,0:T(8,128)(2,1)S(1)} %get-tuple-element.27.wts_ref, ...), custom_call_target="tpu_custom_call" | custom-call | tf_op jit(solution)/shard_map/pallas_call | solution.py:100
  75.2 10.4 %collective-permute-done.13.far_ref = bf16[4,136,512]{2,1,0:T(8,128)(2,1)S(1)} collective-permute-done((bf16[4,136,512]{2,1,0:T(8,128)(2,1)S(1)}, bf16[4,136,512]{2,1,0:T(8,128)(2,1)S(1)}, u32[]{:S(2)}, u32[]{:S(2)}) %collective-permute-start.13) | collective-permute-done | bytes 557088 | tf_op jit(solution)/shard_map/ppermute | solution.py:52
  85.6 0.7 shard_map.161
  86.2 0.1 collective-permute-start.14
  86.3 4.5 %collective-permute-start.15 = (bf16[136,512]{1,0:T(8,128)(2,1)S(1)}, bf16[136,512]{1,0:T(8,128)(2,1)S(1)}, u32[]{:S(2)}, u32[]{:S(2)}) collective-permute-start(bf16[136,512]{1,0:T(8,128)(2,1)S(1)} %get-tuple-element.32), channel_id=1, source_target_pairs={{0,112},{1,17},{2,114},{3,19},{4,116},{5,21},{6,118},{7,23},{8,120... | collective-permute-start | bytes 417800 | tf_op jit(solution)/shard_map/ppermute | solution.py:52
  90.8 0.7 collective-permute-start.16
  91.5 2.6 %collective-permute-done.14.refs_0_ = bf16[136,512]{1,0:T(8,128)(2,1)S(1)} collective-permute-done((bf16[136,512]{1,0:T(8,128)(2,1)S(1)}, bf16[136,512]{1,0:T(8,128)(2,1)S(1)}, u32[]{:S(2)}, u32[]{:S(2)}) %collective-permute-start.14) | collective-permute-done | bytes 139296 | tf_op jit(solution)/shard_map/ppermute | solution.py:52
  94.0 0.8 collective-permute-done.15.refs_1_
  94.8 2.4 %collective-permute-done.16.refs_2_ = bf16[136,512]{1,0:T(8,128)(2,1)S(1)} collective-permute-done((bf16[136,512]{1,0:T(8,128)(2,1)S(1)}, bf16[136,512]{1,0:T(8,128)(2,1)S(1)}, u32[]{:S(2)}, u32[]{:S(2)}) %collective-permute-start.16) | collective-permute-done | bytes 139296 | tf_op jit(solution)/shard_map/ppermute | solution.py:52
  97.2 2.3 %collective-permute-done.17.refs_3_ = bf16[136,512]{1,0:T(8,128)(2,1)S(1)} collective-permute-done((bf16[136,512]{1,0:T(8,128)(2,1)S(1)}, bf16[136,512]{1,0:T(8,128)(2,1)S(1)}, u32[]{:S(2)}, u32[]{:S(2)}) %collective-permute-start.17) | collective-permute-done | bytes 139296 | tf_op jit(solution)/shard_map/ppermute | solution.py:52
  99.5 0.6 shard_map.162
  100.2 0.1 collective-permute-start.18
  100.3 5.0 %collective-permute-start.19 = (bf16[136,256]{1,0:T(8,128)(2,1)S(1)}, bf16[136,256]{1,0:T(8,128)(2,1)S(1)}, u32[]{:S(2)}, u32[]{:S(2)}) collective-permute-start(bf16[136,256]{1,0:T(8,128)(2,1)S(1)} %get-tuple-element.36), channel_id=1, source_target_pairs={{5,0},{4,1},{7,2},{6,3},{0,4},{1,5},{2,6},{3,7},{13,8},{12,9},{15,... | collective-permute-start | bytes 208904 | tf_op jit(solution)/shard_map/ppermute | solution.py:52
  105.3 2.6 %collective-permute-start.20 = (bf16[136,256]{1,0:T(8,128)(2,1)S(1)}, bf16[136,256]{1,0:T(8,128)(2,1)S(1)}, u32[]{:S(2)}, u32[]{:S(2)}) collective-permute-start(bf16[136,256]{1,0:T(8,128)(2,1)S(1)} %get-tuple-element.36), channel_id=1, source_target_pairs={{4,0},{5,1},{6,2},{7,3},{1,4},{0,5},{3,6},{2,7},{12,8},{13,9},{14,... | collective-permute-start | bytes 208904 | tf_op jit(solution)/shard_map/ppermute | solution.py:52
  107.9 2.3 %collective-permute-done.19.down_ref = bf16[136,256]{1,0:T(8,128)(2,1)S(1)} collective-permute-done((bf16[136,256]{1,0:T(8,128)(2,1)S(1)}, bf16[136,256]{1,0:T(8,128)(2,1)S(1)}, u32[]{:S(2)}, u32[]{:S(2)}) %collective-permute-start.19) | collective-permute-done | bytes 69664 | tf_op jit(solution)/shard_map/ppermute | solution.py:52
  110.1 1.3 shard_map.163
  111.4 17.2 %all_to_all.5 = f32[64,8,128]{2,1,0:T(8,128)S(1)} all-to-all(f32[64,8,128]{2,1,0:T(8,128)S(1)} %get-tuple-element.39), channel_id=1, replica_groups=mesh['blk'=64,'rep'=2] {'blk'}, dimensions={0} | all-to-all | bytes 524288 | tf_op jit(solution)/shard_map/all_to_all | solution.py:387
  128.6 1.3 shard_map.164
  (23 shorter events, 0.1 us)
Async XLA Ops:
  2.2 5.5 %collective-permute-start = (bf16[272,128]{1,0:T(8,128)(2,1)S(1)}, bf16[272,128]{1,0:T(8,128)(2,1)S(1)}, u32[]{:S(2)}, u32[]{:S(2)}) collective-permute-start(bf16[272,128]{1,0:T(8,128)(2,1)S(1)} %pad_maximum_fusion.2), channel_id=1, source_target_pairs={{5,0},{4,1},{6,2},{7,3},{0,4},{1,5},{3,6},{2,7},{13,8},{12,9},{14,... | collective-permute-start | bytes 208904 | tf_op jit(solution)/shard_map/ppermute | solution.py:52
  8.6 10.9 %collective-permute-start.1 = (bf16[544,128]{1,0:T(8,128)(2,1)S(1)}, bf16[544,128]{1,0:T(8,128)(2,1)S(1)}, u32[]{:S(2)}, u32[]{:S(2)}) collective-permute-start(bf16[544,128]{1,0:T(8,128)(2,1)S(1)} %pad_maximum_fusion.refs_0_), channel_id=1, source_target_pairs={{120,0},{9,1},{122,2},{11,3},{124,4},{13,5},{126,6},{15,7},{0,8},{... | collective-permute-start | bytes 417800 | tf_op jit(solution)/shard_map/ppermute | solution.py:52
  10.7 10.3 %collective-permute-start.2 = (bf16[544,128]{1,0:T(8,128)(2,1)S(1)}, bf16[544,128]{1,0:T(8,128)(2,1)S(1)}, u32[]{:S(2)}, u32[]{:S(2)}) collective-permute-start(bf16[544,128]{1,0:T(8,128)(2,1)S(1)} %pad_maximum_fusion.refs_0_), channel_id=1, source_target_pairs={{112,0},{17,1},{114,2},{19,3},{116,4},{21,5},{118,6},{23,7},{120,8... | collective-permute-start | bytes 417800 | tf_op jit(solution)/shard_map/ppermute | solution.py:52
  14.3 7.2 %collective-permute-start.3 = (bf16[544,128]{1,0:T(8,128)(2,1)S(1)}, bf16[544,128]{1,0:T(8,128)(2,1)S(1)}, u32[]{:S(2)}, u32[]{:S(2)}) collective-permute-start(bf16[544,128]{1,0:T(8,128)(2,1)S(1)} %pad_maximum_fusion.refs_0_), channel_id=1, source_target_pairs={{104,0},{25,1},{106,2},{27,3},{108,4},{29,5},{110,6},{31,7},{112,8... | collective-permute-start | bytes 417800 | tf_op jit(solution)/shard_map/ppermute | solution.py:52
  16.2 6.3 %collective-permute-start.4 = (bf16[544,128]{1,0:T(8,128)(2,1)S(1)}, bf16[544,128]{1,0:T(8,128)(2,1)S(1)}, u32[]{:S(2)}, u32[]{:S(2)}) collective-permute-start(bf16[544,128]{1,0:T(8,128)(2,1)S(1)} %pad_maximum_fusion.refs_0_), channel_id=1, source_target_pairs={{96,0},{33,1},{98,2},{35,3},{100,4},{37,5},{102,6},{39,7},{104,8},... | collective-permute-start | bytes 417800 | tf_op jit(solution)/shard_map/ppermute | solution.py:52
  22.5 12.5 %collective-permute-start.5 = (bf16[2176,128]{1,0:T(8,128)(2,1)S(1)}, bf16[2176,128]{1,0:T(8,128)(2,1)S(1)}, u32[]{:S(2)}, u32[]{:S(2)}) collective-permute-start(bf16[2176,128]{1,0:T(8,128)(2,1)S(1)} %constant_dynamic-update-slice_fusion.refs_1_), channel_id=1, source_target_pairs={{96,0},{33,1},{98,2},{35,3},{100,4},{37,5},{102,6},{39,7},{104,8},... | collective-permute-start | bytes 1671176 | tf_op jit(solution)/shard_map/ppermute | solution.py:52
  24.1 28.8 %collective-permute-start.7 = (bf16[2176,128]{1,0:T(8,128)(2,1)S(1)}, bf16[2176,128]{1,0:T(8,128)(2,1)S(1)}, u32[]{:S(2)}, u32[]{:S(2)}) collective-permute-start(bf16[2176,128]{1,0:T(8,128)(2,1)S(1)} %constant_dynamic-update-slice_fusion.refs_1_), channel_id=1, source_target_pairs={{2,0},{3,1},{0,2},{1,3},{6,4},{7,5},{4,6},{5,7},{10,8},{11,9},{8,1... | collective-permute-start | bytes 1671176 | tf_op jit(solution)/shard_map/ppermute | solution.py:52
  35.0 17.8 %collective-permute-start.8 = (bf16[2176,128]{1,0:T(8,128)(2,1)S(1)}, bf16[2176,128]{1,0:T(8,128)(2,1)S(1)}, u32[]{:S(2)}, u32[]{:S(2)}) collective-permute-start(bf16[2176,128]{1,0:T(8,128)(2,1)S(1)} %collective-permute-done.5.refs_2_), channel_id=1, source_target_pairs={{2,0},{3,1},{0,2},{1,3},{6,4},{7,5},{4,6},{5,7},{10,8},{11,9},{8,1... | collective-permute-start | bytes 1671176 | tf_op jit(solution)/shard_map/ppermute | solution.py:52
  35.9 20.1 %collective-permute-start.10 = (bf16[528,128]{1,0:T(8,128)(2,1)S(1)}, bf16[528,128]{1,0:T(8,128)(2,1)S(1)}, u32[]{:S(2)}, u32[]{:S(2)}) collective-permute-start(bf16[528,128]{1,0:T(8,128)(2,1)S(1)} %pad_maximum_fusion.1), channel_id=1, source_target_pairs={{1,0},{0,1},{3,2},{2,3},{5,4},{4,5},{7,6},{6,7},{9,8},{8,9},{11,10... | collective-permute-start | bytes 405512 | tf_op jit(solution)/shard_map/ppermute | solution.py:52
  42.0 10.8 %collective-permute-start.6 = (bf16[544,128]{1,0:T(8,128)(2,1)S(1)}, bf16[544,128]{1,0:T(8,128)(2,1)S(1)}, u32[]{:S(2)}, u32[]{:S(2)}) collective-permute-start(bf16[544,128]{1,0:T(8,128)(2,1)S(1)} %pad_maximum_fusion.refs_0_), channel_id=1, source_target_pairs={{2,0},{3,1},{0,2},{1,3},{6,4},{7,5},{4,6},{5,7},{10,8},{11,9},{8,1... | collective-permute-start | bytes 417800 | tf_op jit(solution)/shard_map/ppermute | solution.py:52
  43.2 5.8 %copy-start = (bf16[1,32,16,128,128]{4,3,2,1,0:T(8,128)(2,1)S(1)}, bf16[1,32,16,128,128]{4,3,2,1,0:T(8,128)(2,1)}, u32[]{:S(2)}) copy-start(bf16[1,32,16,128,128]{4,3,2,1,0:T(8,128)(2,1)} %tiles_ref.1) | copy-start | bytes 50331652
  49.0 0.7 copy-start.7
  49.6 3.2 %copy-start.2 = (bf16[64,16,256]{2,1,0:T(8,128)(2,1)S(1)}, bf16[64,16,256]{2,1,0:T(8,128)(2,1)}, u32[]{:S(2)}) copy-start(bf16[64,16,256]{2,1,0:T(8,128)(2,1)} %refs_7_.1) | copy-start | bytes 1572868
  52.8 10.2 %copy-start.1 = (bf16[256,128]{1,0:T(8,128)(2,1)S(1)}, bf16[256,128]{1,0:T(8,128)(2,1)}, u32[]{:S(2)}) copy-start(bf16[256,128]{1,0:T(8,128)(2,1)} %feat_ref.1) | copy-start | bytes 196612
  52.8 10.2 %copy-start.3 = (bf16[256,128]{1,0:T(8,128)(2,1)S(1)}, bf16[256,128]{1,0:T(8,128)(2,1)}, u32[]{:S(2)}) copy-start(bf16[256,128]{1,0:T(8,128)(2,1)} %ct_ref.1) | copy-start | bytes 196612
  52.8 10.2 %copy-start.4 = (bf16[128,128]{1,0:T(8,128)(2,1)S(1)}, bf16[128,128]{1,0:T(8,128)(2,1)}, u32[]{:S(2)}) copy-start(bf16[128,128]{1,0:T(8,128)(2,1)} %sw_ref.1) | copy-start | bytes 98308
  52.8 10.2 %copy-start.5 = (bf16[128,128]{1,0:T(8,128)(2,1)S(1)}, bf16[128,128]{1,0:T(8,128)(2,1)}, u32[]{:S(2)}) copy-start(bf16[128,128]{1,0:T(8,128)(2,1)} %nw_ref.1) | copy-start | bytes 98308
  52.8 10.2 %copy-start.6 = (f32[128]{0:T(128)S(1)}, f32[128]{0:T(128)}, u32[]{:S(2)}) copy-start(f32[128]{0:T(128)} %param.22) | copy-start | bytes 1540
  55.7 7.3 %collective-permute-start.9 = (f32[256,128]{1,0:T(8,128)S(1)}, f32[256,128]{1,0:T(8,128)S(1)}, u32[]{:S(2)}, u32[]{:S(2)}) collective-permute-start(f32[256,128]{1,0:T(8,128)S(1)} %get-tuple-element.24.mine_ref), channel_id=1, source_target_pairs={{1,0},{0,1},{3,2},{2,3},{5,4},{4,5},{7,6},{6,7},{9,8},{8,9},{11,10... | collective-permute-start | bytes 393224 | tf_op jit(solution)/shard_map/ppermute | solution.py:52
  66.0 2.3 %collective-permute-start.12 = (bf16[4,136,512]{2,1,0:T(8,128)(2,1)S(1)}, bf16[4,136,512]{2,1,0:T(8,128)(2,1)S(1)}, u32[]{:S(2)}, u32[]{:S(2)}) collective-permute-start(bf16[4,136,512]{2,1,0:T(8,128)(2,1)S(1)} %shard_map.159), channel_id=1, source_target_pairs={{2,0},{3,1},{0,2},{1,3},{6,4},{7,5},{4,6},{5,7},{10,8},{11,9},{8,1... | collective-permute-start | bytes 1671176 | tf_op jit(solution)/shard_map/ppermute | solution.py:52
  67.8 5.7 %collective-permute-start.11 = (bf16[5,136,512]{2,1,0:T(8,128)(2,1)S(1)}, bf16[5,136,512]{2,1,0:T(8,128)(2,1)S(1)}, u32[]{:S(2)}, u32[]{:S(2)}) collective-permute-start(bf16[5,136,512]{2,1,0:T(8,128)(2,1)S(1)} %shard_map.157), channel_id=1, source_target_pairs={{2,0},{3,1},{0,2},{1,3},{6,4},{7,5},{4,6},{5,7},{10,8},{11,9},{8,1... | collective-permute-start | bytes 2088968 | tf_op jit(solution)/shard_map/ppermute | solution.py:52
  69.8 15.7 %collective-permute-start.13 = (bf16[4,136,512]{2,1,0:T(8,128)(2,1)S(1)}, bf16[4,136,512]{2,1,0:T(8,128)(2,1)S(1)}, u32[]{:S(2)}, u32[]{:S(2)}) collective-permute-start(bf16[4,136,512]{2,1,0:T(8,128)(2,1)S(1)} %shard_map.160), channel_id=1, source_target_pairs={{0,96},{1,33},{2,98},{3,35},{4,100},{5,37},{6,102},{7,39},{8,104},... | collective-permute-start | bytes 1671176 | tf_op jit(solution)/shard_map/ppermute | solution.py:52
  86.2 7.8 %collective-permute-start.14 = (bf16[136,512]{1,0:T(8,128)(2,1)S(1)}, bf16[136,512]{1,0:T(8,128)(2,1)S(1)}, u32[]{:S(2)}, u32[]{:S(2)}) collective-permute-start(bf16[136,512]{1,0:T(8,128)(2,1)S(1)} %get-tuple-element.31), channel_id=1, source_target_pairs={{0,120},{1,9},{2,122},{3,11},{4,124},{5,13},{6,126},{7,15},{8,0},{... | collective-permute-start | bytes 417800 | tf_op jit(solution)/shard_map/ppermute | solution.py:52
  86.3 8.5 %collective-permute-start.15 = (bf16[136,512]{1,0:T(8,128)(2,1)S(1)}, bf16[136,512]{1,0:T(8,128)(2,1)S(1)}, u32[]{:S(2)}, u32[]{:S(2)}) collective-permute-start(bf16[136,512]{1,0:T(8,128)(2,1)S(1)} %get-tuple-element.32), channel_id=1, source_target_pairs={{0,112},{1,17},{2,114},{3,19},{4,116},{5,21},{6,118},{7,23},{8,120... | collective-permute-start | bytes 417800 | tf_op jit(solution)/shard_map/ppermute | solution.py:52
  90.8 6.5 %collective-permute-start.16 = (bf16[136,512]{1,0:T(8,128)(2,1)S(1)}, bf16[136,512]{1,0:T(8,128)(2,1)S(1)}, u32[]{:S(2)}, u32[]{:S(2)}) collective-permute-start(bf16[136,512]{1,0:T(8,128)(2,1)S(1)} %get-tuple-element.33), channel_id=1, source_target_pairs={{0,104},{1,25},{2,106},{3,27},{4,108},{5,29},{6,110},{7,31},{8,112... | collective-permute-start | bytes 417800 | tf_op jit(solution)/shard_map/ppermute | solution.py:52
  91.4 8.1 %collective-permute-start.17 = (bf16[136,512]{1,0:T(8,128)(2,1)S(1)}, bf16[136,512]{1,0:T(8,128)(2,1)S(1)}, u32[]{:S(2)}, u32[]{:S(2)}) collective-permute-start(bf16[136,512]{1,0:T(8,128)(2,1)S(1)} %get-tuple-element.34), channel_id=1, source_target_pairs={{0,96},{1,33},{2,98},{3,35},{4,100},{5,37},{6,102},{7,39},{8,104},... | collective-permute-start | bytes 417800 | tf_op jit(solution)/shard_map/ppermute | solution.py:52
  100.2 7.7 %collective-permute-start.18 = (bf16[136,256]{1,0:T(8,128)(2,1)S(1)}, bf16[136,256]{1,0:T(8,128)(2,1)S(1)}, u32[]{:S(2)}, u32[]{:S(2)}) collective-permute-start(bf16[136,256]{1,0:T(8,128)(2,1)S(1)} %get-tuple-element.35.same_ref), channel_id=1, source_target_pairs={{1,0},{0,1},{3,2},{2,3},{5,4},{4,5},{7,6},{6,7},{9,8},{8,9},{11,10... | collective-permute-start | bytes 208904 | tf_op jit(solution)/shard_map/ppermute | solution.py:52
  100.3 9.9 %collective-permute-start.19 = (bf16[136,256]{1,0:T(8,128)(2,1)S(1)}, bf16[136,256]{1,0:T(8,128)(2,1)S(1)}, u32[]{:S(2)}, u32[]{:S(2)}) collective-permute-start(bf16[136,256]{1,0:T(8,128)(2,1)S(1)} %get-tuple-element.36), channel_id=1, source_target_pairs={{5,0},{4,1},{7,2},{6,3},{0,4},{1,5},{2,6},{3,7},{13,8},{12,9},{15,... | collective-permute-start | bytes 208904 | tf_op jit(solution)/shard_map/ppermute | solution.py:52
  105.3 4.9 %collective-permute-start.20 = (bf16[136,256]{1,0:T(8,128)(2,1)S(1)}, bf16[136,256]{1,0:T(8,128)(2,1)S(1)}, u32[]{:S(2)}, u32[]{:S(2)}) collective-permute-start(bf16[136,256]{1,0:T(8,128)(2,1)S(1)} %get-tuple-element.36), channel_id=1, source_target_pairs={{4,0},{5,1},{6,2},{7,3},{1,4},{0,5},{3,6},{2,7},{12,8},{13,9},{14,... | collective-permute-start | bytes 208904 | tf_op jit(solution)/shard_map/ppermute | solution.py:52
where the time goes:
time: 131 us; the launch traced here: 130 us
  waiting for transfers between devices  47.2 us (36%)
  starting transfers between devices  35.6 us (27%)
  Pallas kernels  17.6 us (13%)
  blocking collectives  17.2 us (13%)
  local copies, waits for them, and re-layouts  6.7 us (5%)
  other arithmetic  4.72 us (4%)
    ppermute x21, waiting for transfers between devices, permute(): return lax.ppermute(x, AXES, pairs)  47.2 us
    ppermute x21, starting transfers between devices, permute(): return lax.ppermute(x, AXES, pairs)  35.6 us
    all_to_all x1, blocking collectives, layer(): lax.all_to_all(pay, 'blk', 0, 0, tiled=True).reshape(blocks * 8, 128)  17.2 us
    pallas_call x10, Pallas kernels, call(): pl.pallas_call(body, in_specs=[smem()] + [vmem()] * n_in, out_specs=vmem(...  14.5 us
    unnamed x19, local copies, waits for them, and re-layouts  6.51 us
    pallas_call x1, Pallas kernels, densify(): pl.pallas_call(densify_kernel, grid_spec=pltpu.PrefetchScalarGridSpec(num...  3.12 us
  transfers between devices with their start and end apart: 21, of which 13 were waited for; matrix products, arithmetic and copies ran while one was open for 2% of the time, Pallas kernels for 8%

commit v1 on v0

v1 whole, which is shorter than its diff:
```python
import functools
import math

import jax
import jax.numpy as jnp
from jax import lax
from jax.experimental import pallas as pl
from jax.experimental.pallas import tpu as pltpu
from jax.sharding import PartitionSpec as P


AXES = ("blk", "rep")
COLS = 9
HEAD = 16
PART = 64 + 8
GROUP = 2 * (256 + HEAD)
MIB = 2**20


def route(source_of):
    pairs = []
    for block in range(64):
        for r in range(2):
            q, l, c = block // 4, (block // 2) % 2, block % 2
            q2, l2, c2, r2 = source_of(q, l, c, r)
            pairs.append(((((q2 % 16) * 2 + l2 % 2) * 2 + c2 % 2) * 2 + r2 % 2, block * 2 + r))
    return pairs


def inverse(pairs):
    return [(d, s) for s, d in pairs]


def y_step(step):
    def source(q, l, c, r):
        y = (2 * r + l + step(c)) % 4
        return (q, y % 2, c, y // 2)

    return route(source)


SWAP_Y = y_step(lambda c: 1 if c else -1)
FROM_DOWN = y_step(lambda c: -1)
FROM_UP = y_step(lambda c: 1)
SWAP_C = route(lambda q, l, c, r: (q, l, c + 1, r))
SWAP_L = route(lambda q, l, c, r: (q, l + 1, c, r))
SWAP_R = route(lambda q, l, c, r: (q, l, c, r + 1))
SAME_X, SAME_Z = (
    [route(lambda q, l, c, r, m=m: (q ^ m, l, c, r)) for m in masks]
    for masks in ((1, 3, 2), (4, 12, 8))
)
FROM_COL = [route(lambda q, l, c, r, k=k: (q + (k if r else -k), l, c, r)) for k in range(5)]


def permute(x, pairs):
    return lax.ppermute(x, AXES, pairs)


def as_bf16(x):
    return lax.reduce_precision(x, 8, 7)


def dot(a, b):
    return jnp.dot(a, b, preferred_element_type=jnp.float32)


def dot_nt(a, b):
    return lax.dot_general(a, b, (((1,), (1,)), ((), ())), preferred_element_type=jnp.float32)


def dot_tn(a, b):
    return lax.dot_general(a, b, (((0,), (0,)), ((), ())), preferred_element_type=jnp.float32)


def slot_source(ids_ref, cls, k, lr):
    block, r = ids_ref[0], ids_ref[1]
    q = lax.bitwise_and(block // 4 + jnp.where(r == 1, k, -k) + 16, 15)
    source = q * 4 + lax.bitwise_xor(lax.bitwise_and(block, 3), lr * 2 + cls)
    offset = lax.bitwise_and(block - source + 64, 63) - 32 * r
    return source, jnp.logical_and(offset >= 0, offset < 32)


def vmem():
    return pl.BlockSpec(memory_space=pltpu.VMEM)


def smem():
    return pl.BlockSpec(memory_space=pltpu.SMEM)


def kernel_call(body, n_in, outs, scratch=(), limit=8 * MIB):
    single = not isinstance(outs, list)
    shapes = [jax.ShapeDtypeStruct(*o) for o in ([outs] if single else outs)]

    def call(*args):
        return pl.pallas_call(
            body,
            in_specs=[smem()] + [vmem()] * n_in,
            out_specs=vmem() if single else [vmem()] * len(shapes),
            out_shape=shapes[0] if single else shapes,
            scratch_shapes=list(scratch),
            compiler_params=pltpu.CompilerParams(vmem_limit_bytes=limit),
        )(*args)

    return call


DEPTH = 8
NEAR, FAR = tuple(range(5)), tuple(range(5, COLS))


def densify_kernel(columns, ids_ref, table_ref, tiles_ref, out_ref, *scratch):
    acc_ref, buf_ref, sem_ref = scratch
    slots = 4 * len(columns)
    counts_at, width = tiles_ref.shape[1] * tiles_ref.shape[2], tiles_ref.shape[2]

    def place(slot):
        cls = slot // (2 * len(columns))
        k = columns[0] + lax.rem(slot // 2, len(columns))
        source, valid = slot_source(ids_ref, cls, k, lax.rem(slot, 2))
        offset = lax.bitwise_and(ids_ref[0] - source + 64, 63) - 32 * ids_ref[1]
        return jnp.where(valid, offset, 0), valid

    def fetch(slot, at):
        offset, _ = place(slot)
        return pltpu.make_async_copy(tiles_ref.at[0, offset], buf_ref.at[at], sem_ref.at[at])

    for u in range(DEPTH):
        fetch(u, u).start()

    def body(slot, carry):
        at = lax.rem(slot, DEPTH)
        offset, valid = place(slot)
        acc_ref[...] = jnp.zeros_like(acc_ref)
        fetch(slot, at).wait()

        def add(j, inner):
            code = table_ref[offset * width + j]
            acc_ref[code] += buf_ref[at, j].astype(jnp.float32)
            return inner

        lax.fori_loop(0, jnp.where(valid, table_ref[counts_at + offset], 0), add, 0)

        @pl.when(slot + DEPTH < slots)
        def _():
            fetch(slot + DEPTH, at).start()

        for t in range(2):
            for s in range(2):
                out_ref[slot, t * 128 : (t + 1) * 128, s * 128 : (s + 1) * 128] = acc_ref[
                    t * 2 + s
                ].astype(jnp.bfloat16)
        return carry

    lax.fori_loop(0, slots, body, 0)


def densify(columns, ids, table, tile_values):
    return pl.pallas_call(
        functools.partial(densify_kernel, columns),
        in_specs=[smem()] * 2 + [pl.BlockSpec(memory_space=pltpu.HBM)],
        out_specs=vmem(),
        scratch_shapes=[
            pltpu.VMEM((4, 128, 128), jnp.float32),
            pltpu.VMEM((DEPTH,) + tile_values.shape[2:], jnp.bfloat16),
            pltpu.SemaphoreType.DMA((DEPTH,)),
        ],
        out_shape=jax.ShapeDtypeStruct((4 * len(columns), 256, 256), jnp.bfloat16),
        compiler_params=pltpu.CompilerParams(vmem_limit_bytes=48 * MIB),
    )(ids, table, tile_values)


def forward_kernel(columns, first, ids_ref, *refs):
    groups, (mats_ref, hub_ref), refs = refs[: 4 if first else 2], refs[4 if first else 2 :][:2], refs[6 if first else 4 :]
    before_ref, (out_ref, hot_ref, wts_ref, pick_ref) = (None, refs) if first else (refs[0], refs[1:])
    lane = lax.broadcasted_iota(jnp.int32, (2 * HEAD, 128), 1)
    column = lax.broadcasted_iota(jnp.int32, (2 * HEAD, 256), 1)
    total = None if first else before_ref[...]
    for cls in range(2):
        for i, k in enumerate(columns):
            if first:
                ref, base = groups[cls * 2 + min(k, 1)], max(k - 1, 0) * GROUP
            else:
                ref, base = groups[cls], i * GROUP
            head = ref[base + 512 : base + GROUP, :].astype(jnp.float32)
            mine = jnp.sum(jnp.where(lane == ids_ref[0], head, 0.0), axis=1, keepdims=True)
            hot = (mine.astype(jnp.int32) == column).astype(jnp.float32).astype(jnp.bfloat16)
            for lr in range(2):
                slot = (cls * len(columns) + i) * 2 + lr
                source, valid = slot_source(ids_ref, cls, k, lr)
                at = slice(slot * HEAD, (slot + 1) * HEAD)
                one = hot[lr * HEAD : (lr + 1) * HEAD, :]
                block = ref[base + lr * 256 : base + (lr + 1) * 256, :]
                both = dot(jnp.concatenate([mats_ref[slot], one], axis=0), block)
                total = both[:256] if total is None else total + both[:256]
                hot_ref[at, :] = one
                pick_ref[at, :] = both[256:].astype(jnp.bfloat16)
                weights = hub_ref[source]
                wts_ref[at, :] = jnp.where(valid, weights, jnp.zeros_like(weights))
    out_ref[...] = (total + dot_tn(wts_ref[...], pick_ref[...])).astype(out_ref.dtype)


def forward(columns, first, *args):
    rows = 4 * len(columns) * HEAD
    return kernel_call(
        functools.partial(forward_kernel, columns, first),
        len(args) - 1,
        [
            ((256, 128), jnp.float32 if first else jnp.bfloat16),
            ((rows, 256), jnp.bfloat16),
            ((rows, 256), jnp.bfloat16),
        ],
        scratch=[pltpu.VMEM((rows, 128), jnp.bfloat16)],
        limit=20 * MIB,
    )(*args)


def middle_kernel(
    ids_ref, mine_ref, theirs_ref, feat_ref, sw_ref, nw_ref, ct_ref, bias_ref, other_ref, *outs
):
    out_ref, grad_ref, self_ref, keep_ref, give_ref, sums_ref = outs
    feats = feat_ref[...]
    agg = mine_ref[...].astype(jnp.float32) + theirs_ref[...].astype(jnp.float32)
    agg = agg.astype(jnp.bfloat16)

    def half(sw, nw, ct, bias):
        pre = dot(feats, sw) + dot(agg, nw) + bias
        gate = jax.nn.sigmoid(pre)
        act = ct.astype(jnp.float32) * gate * (1.0 + pre * (1.0 - gate))
        return pre * gate, act.astype(jnp.bfloat16)

    sw, nw = sw_ref[...], nw_ref[...]
    sw2, nw2 = other_ref[0:128, :], other_ref[128:256, :]
    extra = other_ref[512:528, :].astype(jnp.float32)
    bias2 = extra[0:1] + extra[1:2] + extra[2:3]
    value, act = half(sw, nw, ct_ref[...], bias_ref[...])
    _, act2 = half(sw2, nw2, other_ref[256:512, :], bias2)
    out_ref[...] = value.astype(jnp.bfloat16)
    grad_ref[...] = (dot_nt(nw, act) + dot_nt(nw2, act2)).astype(jnp.bfloat16)
    self_ref[...] = dot_nt(sw, act) + dot_nt(sw2, act2)
    sums_ref[0:128, :] = dot_tn(act, feats)
    sums_ref[128:256, :] = dot_tn(act, agg)
    bias_sum = jnp.sum(act.astype(jnp.float32), axis=0, keepdims=True)
    low = lax.bitwise_and(ids_ref[0], 3)
    for lr in range(2):
        for cls, ref in enumerate((keep_ref, give_ref)):
            quarter = lax.bitwise_xor(low, 2 * lr + cls)
            ref[lr, 0:64, :] = sums_ref[pl.ds(pl.multiple_of(quarter * 64, 64), 64), :]
            ref[lr, 64:PART, :] = jnp.broadcast_to(bias_sum, (PART - 64, 128))


def middle(*args):
    return kernel_call(
        middle_kernel,
        8,
        [
            ((256, 128), jnp.bfloat16),
            ((128, 256), jnp.bfloat16),
            ((128, 256), jnp.float32),
            ((2, PART, 128), jnp.float32),
            ((2, PART, 128), jnp.float32),
        ],
        scratch=[pltpu.VMEM((256, 128), jnp.float32)],
    )(*args)


def backward_kernel(cls, columns, add, ids_ref, grad_ref, mats_ref, hot_ref, wts_ref, *refs):
    out_ref = refs[-1]
    grad = grad_ref[...]
    for i in range(len(columns)):
        for lr in range(2):
            slot = (cls * len(columns) + i) * 2 + lr
            at = slice(slot * HEAD, (slot + 1) * HEAD)
            lanes = slice(lr * 256, (lr + 1) * 256)
            back = dot_nt(grad, wts_ref[at, :]).astype(jnp.bfloat16)
            part = dot(grad, mats_ref[slot]) + dot(back, hot_ref[at, :])
            if add:
                part += refs[0][i, :, lanes].astype(jnp.float32)
            out_ref[i, :, lanes] = part.astype(out_ref.dtype)


def backward(cls, columns, dtype, *args):
    body = functools.partial(backward_kernel, cls, columns, len(args) > 5)
    return kernel_call(body, len(args) - 1, ((len(columns), 128, 512), dtype), limit=20 * MIB)(
        *args
    )


def near_kernel(ids_ref, keep_ref, far_ref, *outs):
    for i, out in enumerate(outs):
        out[...] = (keep_ref[i + 1] + far_ref[i].astype(jnp.float32)).astype(jnp.bfloat16)


def mine_kernel(ids_ref, keep_ref, *refs):
    got, (same_ref, cross_ref) = refs[:4], refs[4:]
    total = keep_ref[0]
    for ref in got:
        total += ref[...].astype(jnp.float32)
    same_ref[...] = total[:, :256].astype(jnp.bfloat16)
    cross_ref[...] = total[:, 256:].astype(jnp.bfloat16)


def finish_kernel(ids_ref, same_ref, rep_ref, down_ref, up_ref, self_ref, grad_ref):
    f32 = jnp.float32
    total = (same_ref[...].astype(f32) + rep_ref[...].astype(f32)) + (
        down_ref[...].astype(f32) + up_ref[...].astype(f32)
    )
    grad_ref[...] = (total + self_ref[...]).T.astype(jnp.bfloat16)


def weights_kernel(scale, ids_ref, mine_ref, line_ref, core_ref, *refs):
    self_ref, neighbor_ref, bias_ref, sums_ref, bias_sums_ref = refs
    low = lax.bitwise_and(ids_ref[0], 3)
    for lr in range(2):
        for cls in range(2):
            part = core_ref.at[lr] if cls else (line_ref if lr else mine_ref)
            quarter = lax.bitwise_xor(low, 2 * lr + cls)
            sums_ref[pl.ds(pl.multiple_of(quarter * 64, 64), 64), :] = part[0:64, :]
            bias_sums_ref[quarter] = part[64:PART, :]
    self_ref[...] = sums_ref[0:128, :].T * scale
    neighbor_ref[...] = sums_ref[128:256, :].T * scale
    bias_ref[...] = bias_sums_ref[0][0:1] * scale


def layer(
    features,
    tile_values,
    tile_target,
    tile_source,
    tile_count,
    hub_list,
    hub_count,
    hub_weight,
    self_weight,
    neighbor_weight,
    bias,
    cotangent,
):
    f32, bf16 = jnp.float32, jnp.bfloat16
    blocks = lax.axis_size("blk")
    ids = jnp.stack([lax.axis_index("blk"), lax.axis_index("rep")]).astype(jnp.int32)

    live = jnp.arange(HEAD, dtype=jnp.int32)[None, :] < hub_count[0][:, None]
    lists = jnp.where(live, hub_list[0], -1).astype(bf16).T
    lists = jnp.pad(lists, ((0, 0), (0, 128 - blocks)), constant_values=-1)
    theirs = permute(features, SWAP_Y)
    their_lists = permute(lists, SWAP_Y)

    bias_hi = as_bf16(bias)
    bias_mid = as_bf16(bias - bias_hi)
    bias_lo = bias - bias_hi - bias_mid
    bias_rows = jnp.stack([bias_hi, bias_mid, bias_lo]).astype(bf16)
    bias_rows = jnp.pad(bias_rows, ((0, 13), (0, 0)))
    packed = jnp.concatenate([self_weight, neighbor_weight, cotangent, bias_rows], axis=0)

    col0 = jnp.concatenate([features, theirs, lists, their_lists], axis=0)
    code = (tile_target[0] * 2 + tile_source[0]).reshape(-1)
    table = jnp.concatenate([code, tile_count[0]])
    col0, table, ids, packed = lax.optimization_barrier((col0, table, ids, packed))
    other = permute(packed, SWAP_R)
    cols = [permute(col0, FROM_COL[k]) for k in range(1, 5)]
    oth0 = permute(col0, SWAP_C)
    cols = jnp.concatenate(cols, axis=0)
    far = permute(cols, FROM_COL[4])
    oth1 = permute(cols, SWAP_C)
    mats_near = densify(NEAR, ids, table, tile_values)
    mats_far = densify(FAR, ids, table, tile_values)
    oth2 = permute(far, SWAP_C)

    partial, hot_near, wts_near = forward(
        NEAR, True, ids, col0, cols, oth0, oth1, mats_near, hub_weight
    )
    partial, hot_far, wts_far = forward(FAR, False, ids, far, oth2, mats_far, hub_weight, partial)
    theirs = permute(partial, SWAP_R)
    output, grad, self_grad, parts, give_parts = middle(
        ids,
        partial,
        theirs,
        features,
        self_weight,
        neighbor_weight,
        cotangent,
        bias[None, :],
        other,
    )

    with_far = (grad, mats_far, hot_far, wts_far)
    with_near = (grad, mats_near, hot_near, wts_near)
    got_far = permute(backward(1, FAR, bf16, ids, *with_far), SWAP_C)
    got_near = permute(backward(1, NEAR, bf16, ids, *with_near), SWAP_C)
    got_parts = permute(give_parts, SWAP_C)
    sent = backward(0, FAR, bf16, ids, *with_far, got_far)
    far_sums = permute(sent, inverse(FROM_COL[4]))
    keep = backward(0, NEAR, f32, ids, *with_near, got_near)

    def added(*terms):
        while len(terms) > 1:
            terms = [a + b for a, b in zip(terms[::2], terms[1::2])]
        return terms[0]

    def over_columns(value, routes):
        return added(value, *(permute(value, p) for p in routes))

    parts = added(parts, got_parts)
    quarter = added(parts[0], permute(parts[1], SWAP_L))
    quarter = over_columns(quarter, SAME_X)
    far_sums, _ = lax.optimization_barrier((far_sums, quarter))

    piece = ((128, 512), bf16)
    near = kernel_call(near_kernel, 2, [piece] * 4)(ids, keep, far_sums)
    got = [permute(near[k - 1], inverse(FROM_COL[k])) for k in range(1, 5)]
    quarter = over_columns(quarter, SAME_Z)
    line = permute(quarter, SWAP_L)
    core = permute(jnp.stack([quarter, line]), SWAP_C)
    piece = ((128, 256), bf16)
    same, cross = kernel_call(mine_kernel, 5, [piece] * 2)(ids, keep, *got)
    over = permute(same, SWAP_R)
    down = permute(cross, FROM_DOWN)
    up = permute(cross, FROM_UP)
    grad_input = kernel_call(finish_kernel, 5, ((256, 128), bf16))(
        ids, same, over, down, up, self_grad
    )
    grad_self, grad_neighbor, grad_bias = kernel_call(
        functools.partial(weights_kernel, 1.0 / math.sqrt(256 * blocks)),
        3,
        [((128, 128), f32), ((128, 128), f32), ((1, 128), f32)],
        scratch=[pltpu.VMEM((256, 128), f32), pltpu.VMEM((4, PART - 64, 128), f32)],
    )(ids, quarter, line, core)
    return output, grad_input, grad_self, grad_neighbor, grad_bias[0]


def solution(mesh):
    in_specs = (
        P("blk", None),
        P("blk", "rep", None, None, None),
        P("blk", "rep", None),
        P("blk", "rep", None),
        P("blk", "rep"),
        P("blk", None, None),
        P("blk", None),
        P(None, None, "blk"),
        P(None, "rep"),
        P(None, "rep"),
        P("rep"),
        P("blk", "rep"),
    )
    out_specs = (P("blk", "rep"), P("blk", None), P(None, "rep"), P(None, "rep"), P("rep"))
    return jax.shard_map(layer, mesh=mesh, in_specs=in_specs, out_specs=out_specs, check_vma=False)
```

time: 131 us -> 118 us (0.901)
  blocking collectives: 17.2 us -> 0 us
  starting transfers between devices: 35.6 us -> 44.7 us
  Pallas kernels: 17.6 us -> 24.6 us
  local copies, waits for them, and re-layouts: 6.7 us -> 0.27 us
  waiting for transfers between devices: 47.2 us -> 41.5 us
    all_to_all x1 -> x0, blocking collectives: 17.2 us -> none  [layer(): lax.all_to_all(pay, 'blk', 0, 0, tiled=True).reshape(blocks * 8, 128)]
    ppermute x21 -> x32, starting transfers between devices: 35.6 us -> 44.7 us  [permute(): return lax.ppermute(x, AXES, pairs)]
    pallas_call x1 -> x2, Pallas kernels: 3.12 us -> 9.76 us  [densify(): pl.pallas_call(functools.partial(densify_kernel, columns), in_specs=[smem...]
    unnamed x19 -> x15, local copies, waits for them, and re-layouts: 6.51 us -> 0.09 us
    ppermute x21 -> x32, waiting for transfers between devices: 47.2 us -> 41.5 us  [permute(): return lax.ppermute(x, AXES, pairs)]
    pallas_call x10 -> x11, Pallas kernels: 14.5 us -> 14.8 us  [call(): pl.pallas_call(body, in_specs=[smem()] + [vmem()] * n_in, out_specs=vmem(...]
  transfers between devices with their start and end apart: 21 -> 32, of which waited for: 13 -> 16; matrix products, arithmetic and copies ran while one was open for 2% -> 3% of each run, Pallas kernels for 8% -> 19%
where the time goes in v1:
time: 118 us; the launch traced here: 117 us
  starting transfers between devices  44.7 us (38%)
  waiting for transfers between devices  41.5 us (35%)
  Pallas kernels  24.6 us (21%)
  other arithmetic  4.6 us (4%)
    ppermute x32, starting transfers between devices, permute(): return lax.ppermute(x, AXES, pairs)  44.7 us
    ppermute x32, waiting for transfers between devices, permute(): return lax.ppermute(x, AXES, pairs)  41.5 us
    pallas_call x11, Pallas kernels, call(): pl.pallas_call(body, in_specs=[smem()] + [vmem()] * n_in, out_specs=vmem(...  14.8 us
    pallas_call x2, Pallas kernels, densify(): pl.pallas_call(functools.partial(densify_kernel, columns), in_specs=[smem...  9.76 us
  transfers between devices with their start and end apart: 32, of which 16 were waited for; matrix products, arithmetic and copies ran while one was open for 3% of the time, Pallas kernels for 19%

profile of v1, /device:TPU:0, one launch (start us, length us, event | category | flops | bytes accessed | tf_op | source)
XLA Modules:
  0.0 116.7 jit_solution(3571624384915506834)
XLA Ops:
  0.6 0.7 fusion.5
  1.3 1.8 %collective-permute-start.1 = (bf16[16,128]{1,0:T(8,128)(2,1)S(1)}, bf16[16,128]{1,0:T(8,128)(2,1)S(1)}, u32[]{:S(2)}, u32[]{:S(2)}) collective-permute-start(bf16[16,128]{1,0:T(8,128)(2,1)S(1)} %pad.8), channel_id=1, source_target_pairs={{5,0},{4,1},{6,2},{7,3},{0,4},{1,5},{3,6},{2,7},{13,8},{12,9},{14,... | collective-permute-start | bytes 12296 | tf_op jit(solution)/shard_map/ppermute | solution.py:56
  3.1 1.6 %collective-permute-start = (bf16[256,128]{1,0:T(8,128)(2,1)}, bf16[256,128]{1,0:T(8,128)(2,1)S(1)}, u32[]{:S(2)}, u32[]{:S(2)}) collective-permute-start(bf16[256,128]{1,0:T(8,128)(2,1)} %feat_ref.1), channel_id=1, source_target_pairs={{5,0},{4,1},{6,2},{7,3},{0,4},{1,5},{3,6},{2,7},{13,8},{12,9},{14,... | collective-permute-start | bytes 196616 | tf_op jit(solution)/shard_map/ppermute | solution.py:56
  4.7 0.7 fusion.8
  5.3 0.7 multiply_add_fusion
  6.1 0.1 copy.17
  6.1 0.1 add.36
  6.2 0.7 pad_add_fusion.table_ref
  6.9 0.9 pad_maximum_fusion.1
  7.8 0.1 pad_add_fusion.1.ids_ref
  7.8 1.0 collective-permute-done
  8.8 0.8 pad_maximum_fusion.refs_0_
  9.6 2.0 %collective-permute-start.2 = (bf16[544,128]{1,0:T(8,128)(2,1)S(1)}, bf16[544,128]{1,0:T(8,128)(2,1)S(1)}, u32[]{:S(2)}, u32[]{:S(2)}) collective-permute-start(bf16[544,128]{1,0:T(8,128)(2,1)S(1)} %pad_maximum_fusion.refs_0_), channel_id=1, source_target_pairs={{120,0},{9,1},{122,2},{11,3},{124,4},{13,5},{126,6},{15,7},{0,8},{... | collective-permute-start | bytes 417800 | tf_op jit(solution)/shard_map/ppermute | solution.py:56
  11.6 3.6 %collective-permute-start.3 = (bf16[544,128]{1,0:T(8,128)(2,1)S(1)}, bf16[544,128]{1,0:T(8,128)(2,1)S(1)}, u32[]{:S(2)}, u32[]{:S(2)}) collective-permute-start(bf16[544,128]{1,0:T(8,128)(2,1)S(1)} %pad_maximum_fusion.refs_0_), channel_id=1, source_target_pairs={{112,0},{17,1},{114,2},{19,3},{116,4},{21,5},{118,6},{23,7},{120,8... | collective-permute-start | bytes 417800 | tf_op jit(solution)/shard_map/ppermute | solution.py:56
  15.2 1.9 %collective-permute-start.4 = (bf16[544,128]{1,0:T(8,128)(2,1)S(1)}, bf16[544,128]{1,0:T(8,128)(2,1)S(1)}, u32[]{:S(2)}, u32[]{:S(2)}) collective-permute-start(bf16[544,128]{1,0:T(8,128)(2,1)S(1)} %pad_maximum_fusion.refs_0_), channel_id=1, source_target_pairs={{104,0},{25,1},{106,2},{27,3},{108,4},{29,5},{110,6},{31,7},{112,8... | collective-permute-start | bytes 417800 | tf_op jit(solution)/shard_map/ppermute | solution.py:56
  17.1 1.5 %collective-permute-start.5 = (bf16[544,128]{1,0:T(8,128)(2,1)S(1)}, bf16[544,128]{1,0:T(8,128)(2,1)S(1)}, u32[]{:S(2)}, u32[]{:S(2)}) collective-permute-start(bf16[544,128]{1,0:T(8,128)(2,1)S(1)} %pad_maximum_fusion.refs_0_), channel_id=1, source_target_pairs={{96,0},{33,1},{98,2},{35,3},{100,4},{37,5},{102,6},{39,7},{104,8},... | collective-permute-start | bytes 417800 | tf_op jit(solution)/shard_map/ppermute | solution.py:56
  18.6 2.3 %collective-permute-done.2 = bf16[544,128]{1,0:T(8,128)(2,1)S(1)} collective-permute-done((bf16[544,128]{1,0:T(8,128)(2,1)S(1)}, bf16[544,128]{1,0:T(8,128)(2,1)S(1)}, u32[]{:S(2)}, u32[]{:S(2)}) %collective-permute-start.2) | collective-permute-done | bytes 139296 | tf_op jit(solution)/shard_map/ppermute | solution.py:56
  20.9 1.0 collective-permute-done.3
  21.9 0.8 collective-permute-done.4
  22.8 0.6 collective-permute-done.5
  23.4 0.4 collective-permute-start.6
  23.9 12.6 %collective-permute-done.6.refs_0_ = bf16[2176,128]{1,0:T(8,128)(2,1)S(1)} collective-permute-done((bf16[2176,128]{1,0:T(8,128)(2,1)S(1)}, bf16[2176,128]{1,0:T(8,128)(2,1)S(1)}, u32[]{:S(2)}, u32[]{:S(2)}) %collective-permute-start.6) | collective-permute-done | bytes 557088 | tf_op jit(solution)/shard_map/ppermute | solution.py:56
  36.5 0.5 collective-permute-start.8
  37.0 3.0 %collective-permute-start.11 = (bf16[528,128]{1,0:T(8,128)(2,1)S(1)}, bf16[528,128]{1,0:T(8,128)(2,1)S(1)}, u32[]{:S(2)}, u32[]{:S(2)}) collective-permute-start(bf16[528,128]{1,0:T(8,128)(2,1)S(1)} %pad_maximum_fusion.1), channel_id=1, source_target_pairs={{1,0},{0,1},{3,2},{2,3},{5,4},{4,5},{7,6},{6,7},{9,8},{8,9},{11,10... | collective-permute-start | bytes 405512 | tf_op jit(solution)/shard_map/ppermute | solution.py:56
  40.0 5.5 %shard_map.156.refs_4_.mats_ref = bf16[20,256,256]{2,1,0:T(8,128)(2,1)S(1)} custom-call(s32[2]{0:T(128)S(1)} %pad_add_fusion.1.ids_ref, s32[544]{0:T(1024)S(1)} %pad_add_fusion.table_ref, bf16[1,32,16,128,128]{4,3,2,1,0:T(8,128)(2,1)} %tiles_ref.3), custom_call_target="tpu_custom_call" | custom-call | tf_op jit(solution)/shard_map/pallas_call | solution.py:159
  45.5 4.3 %shard_map.155.refs_2_.mats_ref = bf16[16,256,256]{2,1,0:T(8,128)(2,1)S(1)} custom-call(s32[2]{0:T(128)S(1)} %pad_add_fusion.1.ids_ref, s32[544]{0:T(1024)S(1)} %pad_add_fusion.table_ref, bf16[1,32,16,128,128]{4,3,2,1,0:T(8,128)(2,1)} %tiles_ref.3), custom_call_target="tpu_custom_call" | custom-call | tf_op jit(solution)/shard_map/pallas_call | solution.py:159
  49.9 1.7 %shard_map.157 = (f32[256,128]{1,0:T(8,128)S(1)}, bf16[320,256]{1,0:T(8,128)(2,1)S(1)}, bf16[320,256]{1,0:T(8,128)(2,1)S(1)}) custom-call(s32[2]{0:T(128)S(1)} %pad_add_fusion.1.ids_ref, bf16[544,128]{1,0:T(8,128)(2,1)S(1)} %pad_maximum_fusion.refs_0_, bf16[2176,128]{1,0:T(8,128)(2,1)S(1)} %constant_dynamic-update-slice_fusion.refs_1_, ...), custom_call_target="tpu_custom_call" | custom-call | tf_op jit(solution)/shard_map/pallas_call | solution.py:96
  51.6 1.6 %shard_map.158 = (bf16[256,128]{1,0:T(8,128)(2,1)S(1)}, bf16[256,256]{1,0:T(8,128)(2,1)S(1)}, bf16[256,256]{1,0:T(8,128)(2,1)S(1)}) custom-call(s32[2]{0:T(128)S(1)} %pad_add_fusion.1.ids_ref, bf16[2176,128]{1,0:T(8,128)(2,1)S(1)} %collective-permute-done.6.refs_0_, bf16[2176,128]{1,0:T(8,128)(2,1)S(1)} %collective-permute-done.7.refs_1_, ...), custom_call_target="tpu_custom_call" | custom-call | tf_op jit(solution)/shard_map/pallas_call | solution.py:96
  53.2 0.2 collective-permute-start.10
  53.4 5.6 %collective-permute-done.10.theirs_ref = bf16[256,128]{1,0:T(8,128)(2,1)S(1)} collective-permute-done((bf16[256,128]{1,0:T(8,128)(2,1)S(1)}, bf16[256,128]{1,0:T(8,128)(2,1)S(1)}, u32[]{:S(2)}, u32[]{:S(2)}) %collective-permute-start.10) | collective-permute-done | bytes 65568 | tf_op jit(solution)/shard_map/ppermute | solution.py:56
  59.1 1.5 %shard_map.159 = (bf16[256,128]{1,0:T(8,128)(2,1)}, bf16[128,256]{1,0:T(8,128)(2,1)S(1)}, f32[128,256]{1,0:T(8,128)S(1)}, f32[2,72,128]{2,1,0:T(8,128)S(1)}, f32[2,72,128]{2,1,0:T(8,128)S(1)}) custom-call(s32[2]{0:T(128)S(1)} %pad_add_fusion.1.ids_ref, bf16[256,128]{1,0:T(8,128)(2,1)S(1)} %get-tuple-element.34.mine_ref, ...), custom_call_target="tpu_custom_call" | custom-call | tf_op jit(solution)/shard_map/pallas_call | solution.py:96
  60.5 1.5 %shard_map.162 = bf16[4,128,512]{2,1,0:T(8,128)(2,1)S(1)} custom-call(s32[2]{0:T(128)S(1)} %pad_add_fusion.1.ids_ref, bf16[128,256]{1,0:T(8,128)(2,1)S(1)} %get-tuple-element.37.grad_ref, bf16[16,256,256]{2,1,0:T(8,128)(2,1)S(1)} %shard_map.155.refs_2_.mats_ref, bf16[256,256]{1,0:T(8,128)(2,1)S(1)} %get-tuple-element.40.hot_ref, ...), custom_call_target="tpu_custom_call" | custom-call | tf_op jit(solution)/shard_map/pallas_call | solution.py:96
  62.0 0.6 collective-permute-start.13
  62.6 4.9 %collective-permute-start.16 = (f32[72,128]{1,0:T(8,128)S(1)}, f32[72,128]{1,0:T(8,128)S(1)}, u32[]{:S(2)}, u32[]{:S(2)}) collective-permute-start(f32[72,128]{1,0:T(8,128)S(1)} %slice_bitcast_fusion), channel_id=1, source_target_pairs={{4,0},{5,1},{6,2},{7,3},{0,4},{1,5},{2,6},{3,7},{12,8},{13,9},{14,... | collective-permute-start | bytes 110600 | tf_op jit(solution)/shard_map/ppermute | solution.py:56
  67.5 1.7 %shard_map.160 = bf16[5,128,512]{2,1,0:T(8,128)(2,1)S(1)} custom-call(s32[2]{0:T(128)S(1)} %pad_add_fusion.1.ids_ref, bf16[128,256]{1,0:T(8,128)(2,1)S(1)} %get-tuple-element.37.grad_ref, bf16[20,256,256]{2,1,0:T(8,128)(2,1)S(1)} %shard_map.156.refs_4_.mats_ref, bf16[320,256]{1,0:T(8,128)(2,1)S(1)} %get-tuple-element.38.hot_ref, ...), custom_call_target="tpu_custom_call" | custom-call | tf_op jit(solution)/shard_map/pallas_call | solution.py:96
  69.2 0.1 collective-permute-start.12
  69.3 0.2 collective-permute-done.16
  69.5 0.8 collective-permute-start.18
  70.3 3.3 %collective-permute-start.19 = (f32[72,128]{1,0:T(8,128)S(1)}, f32[72,128]{1,0:T(8,128)S(1)}, u32[]{:S(2)}, u32[]{:S(2)}) collective-permute-start(f32[72,128]{1,0:T(8,128)S(1)} %fusion), channel_id=1, source_target_pairs={{16,0},{17,1},{18,2},{19,3},{20,4},{21,5},{22,6},{23,7},{24,8},{25... | collective-permute-start | bytes 110600 | tf_op jit(solution)/shard_map/ppermute | solution.py:56
  73.6 1.5 %shard_map.163 = bf16[4,128,512]{2,1,0:T(8,128)(2,1)S(1)} custom-call(s32[2]{0:T(128)S(1)} %pad_add_fusion.1.ids_ref, bf16[128,256]{1,0:T(8,128)(2,1)S(1)} %get-tuple-element.37.grad_ref, bf16[16,256,256]{2,1,0:T(8,128)(2,1)S(1)} %shard_map.155.refs_2_.mats_ref, bf16[256,256]{1,0:T(8,128)(2,1)S(1)} %get-tuple-element.40.hot_ref, ...), custom_call_target="tpu_custom_call" | custom-call | tf_op jit(solution)/shard_map/pallas_call | solution.py:96
  75.1 3.6 %collective-permute-start.14 = (bf16[4,128,512]{2,1,0:T(8,128)(2,1)S(1)}, bf16[4,128,512]{2,1,0:T(8,128)(2,1)S(1)}, u32[]{:S(2)}, u32[]{:S(2)}) collective-permute-start(bf16[4,128,512]{2,1,0:T(8,128)(2,1)S(1)} %shard_map.163), channel_id=1, source_target_pairs={{0,96},{1,33},{2,98},{3,35},{4,100},{5,37},{6,102},{7,39},{8,104},... | collective-permute-start | bytes 1572872 | tf_op jit(solution)/shard_map/ppermute | solution.py:56
  78.7 0.1 collective-permute-start.27
  78.8 0.4 collective-permute-start.28
  79.3 3.6 %collective-permute-start.29 = (f32[72,128]{1,0:T(8,128)S(1)}, f32[72,128]{1,0:T(8,128)S(1)}, u32[]{:S(2)}, u32[]{:S(2)}) collective-permute-start(f32[72,128]{1,0:T(8,128)S(1)} %add_add_fusion.1), channel_id=1, source_target_pairs={{64,0},{65,1},{66,2},{67,3},{68,4},{69,5},{70,6},{71,7},{72,8},{73... | collective-permute-start | bytes 110600 | tf_op jit(solution)/shard_map/ppermute | solution.py:56
  82.9 6.8 %collective-permute-done.27 = f32[72,128]{1,0:T(8,128)S(1)} collective-permute-done((f32[72,128]{1,0:T(8,128)S(1)}, f32[72,128]{1,0:T(8,128)S(1)}, u32[]{:S(2)}, u32[]{:S(2)}) %collective-permute-start.27) | collective-permute-done | bytes 36896 | tf_op jit(solution)/shard_map/ppermute | solution.py:56
  89.7 1.5 %collective-permute-done.28 = f32[72,128]{1,0:T(8,128)S(1)} collective-permute-done((f32[72,128]{1,0:T(8,128)S(1)}, f32[72,128]{1,0:T(8,128)S(1)}, u32[]{:S(2)}, u32[]{:S(2)}) %collective-permute-start.28) | collective-permute-done | bytes 36896 | tf_op jit(solution)/shard_map/ppermute | solution.py:56
  91.2 0.6 collective-permute-start.30
  91.8 1.7 %shard_map.161.keep_ref = f32[5,128,512]{2,1,0:T(8,128)S(1)} custom-call(s32[2]{0:T(128)S(1)} %pad_add_fusion.1.ids_ref, bf16[128,256]{1,0:T(8,128)(2,1)S(1)} %get-tuple-element.37.grad_ref, bf16[20,256,256]{2,1,0:T(8,128)(2,1)S(1)} %shard_map.156.refs_4_.mats_ref, bf16[320,256]{1,0:T(8,128)(2,1)S(1)} %get-tuple-element.38.hot_ref, ...), custom_call_target="tpu_custom_call" | custom-call | tf_op jit(solution)/shard_map/pallas_call | solution.py:96
  93.5 0.6 shard_map.164
  94.1 4.1 %collective-permute-start.20 = (bf16[128,512]{1,0:T(8,128)(2,1)S(1)}, bf16[128,512]{1,0:T(8,128)(2,1)S(1)}, u32[]{:S(2)}, u32[]{:S(2)}) collective-permute-start(bf16[128,512]{1,0:T(8,128)(2,1)S(1)} %get-tuple-element.45), channel_id=1, source_target_pairs={{0,120},{1,9},{2,122},{3,11},{4,124},{5,13},{6,126},{7,15},{8,0},{... | collective-permute-start | bytes 393224 | tf_op jit(solution)/shard_map/ppermute | solution.py:56
  98.2 1.6 %collective-permute-start.21 = (bf16[128,512]{1,0:T(8,128)(2,1)S(1)}, bf16[128,512]{1,0:T(8,128)(2,1)S(1)}, u32[]{:S(2)}, u32[]{:S(2)}) collective-permute-start(bf16[128,512]{1,0:T(8,128)(2,1)S(1)} %get-tuple-element.46), channel_id=1, source_target_pairs={{0,112},{1,17},{2,114},{3,19},{4,116},{5,21},{6,118},{7,23},{8,120... | collective-permute-start | bytes 393224 | tf_op jit(solution)/shard_map/ppermute | solution.py:56
  99.8 0.1 collective-permute-start.31
  99.8 2.2 %collective-permute-done.20.refs_0_ = bf16[128,512]{1,0:T(8,128)(2,1)S(1)} collective-permute-done((bf16[128,512]{1,0:T(8,128)(2,1)S(1)}, bf16[128,512]{1,0:T(8,128)(2,1)S(1)}, u32[]{:S(2)}, u32[]{:S(2)}) %collective-permute-start.20) | collective-permute-done | bytes 131104 | tf_op jit(solution)/shard_map/ppermute | solution.py:56
  102.1 3.7 %collective-permute-done.21.refs_1_ = bf16[128,512]{1,0:T(8,128)(2,1)S(1)} collective-permute-done((bf16[128,512]{1,0:T(8,128)(2,1)S(1)}, bf16[128,512]{1,0:T(8,128)(2,1)S(1)}, u32[]{:S(2)}, u32[]{:S(2)}) %collective-permute-start.21) | collective-permute-done | bytes 131104 | tf_op jit(solution)/shard_map/ppermute | solution.py:56
  105.8 0.9 collective-permute-done.22.refs_2_
  106.7 1.4 %collective-permute-done.23.refs_3_ = bf16[128,512]{1,0:T(8,128)(2,1)S(1)} collective-permute-done((bf16[128,512]{1,0:T(8,128)(2,1)S(1)}, bf16[128,512]{1,0:T(8,128)(2,1)S(1)}, u32[]{:S(2)}, u32[]{:S(2)}) %collective-permute-start.23) | collective-permute-done | bytes 131104 | tf_op jit(solution)/shard_map/ppermute | solution.py:56
  108.0 0.6 shard_map.165
  108.7 0.1 collective-permute-start.24
  108.8 1.8 %collective-permute-start.25 = (bf16[128,256]{1,0:T(8,128)(2,1)S(1)}, bf16[128,256]{1,0:T(8,128)(2,1)S(1)}, u32[]{:S(2)}, u32[]{:S(2)}) collective-permute-start(bf16[128,256]{1,0:T(8,128)(2,1)S(1)} %get-tuple-element.50), channel_id=1, source_target_pairs={{5,0},{4,1},{7,2},{6,3},{0,4},{1,5},{2,6},{3,7},{13,8},{12,9},{15,... | collective-permute-start | bytes 196616 | tf_op jit(solution)/shard_map/ppermute | solution.py:56
  110.5 2.6 %collective-permute-start.26 = (bf16[128,256]{1,0:T(8,128)(2,1)S(1)}, bf16[128,256]{1,0:T(8,128)(2,1)S(1)}, u32[]{:S(2)}, u32[]{:S(2)}) collective-permute-start(bf16[128,256]{1,0:T(8,128)(2,1)S(1)} %get-tuple-element.50), channel_id=1, source_target_pairs={{4,0},{5,1},{6,2},{7,3},{1,4},{0,5},{3,6},{2,7},{12,8},{13,9},{14,... | collective-permute-start | bytes 196616 | tf_op jit(solution)/shard_map/ppermute | solution.py:56
  113.1 1.3 %shard_map.167 = (f32[128,128]{1,0:T(8,128)}, f32[128,128]{1,0:T(8,128)}, f32[1,128]{1,0:T(1,128)}) custom-call(s32[2]{0:T(128)S(1)} %pad_add_fusion.1.ids_ref, f32[72,128]{1,0:T(8,128)S(1)} %add_add_fusion.mine_ref, f32[72,128]{1,0:T(8,128)S(1)} %collective-permute-done.30.line_ref, f32[2,72,128]{2,1,0:T(8,128)S(1)} %collective-permute-done.31.core_ref), custom_call_target="tpu_custom_call" | custom-call | tf_op jit(solution)/shard_map/pallas_call | solution.py:96
  114.5 0.1 collective-permute-done.24.rep_ref
  114.5 0.9 collective-permute-done.25.down_ref
  115.4 1.3 %shard_map.166 = bf16[256,128]{1,0:T(8,128)(2,1)} custom-call(s32[2]{0:T(128)S(1)} %pad_add_fusion.1.ids_ref, bf16[128,256]{1,0:T(8,128)(2,1)S(1)} %get-tuple-element.49.same_ref, bf16[128,256]{1,0:T(8,128)(2,1)S(1)} %collective-permute-done.24.rep_ref, bf16[128,256]{1,0:T(8,128)(2,1)S(1)} %collective-permute-done.25.down_ref, ...), custom_call_target="tpu_custom_call" | custom-call | tf_op jit(solution)/shard_map/pallas_call | solution.py:96
  (46 shorter events, 0.2 us)
Async XLA Ops:
  1.3 6.5 %collective-permute-start.1 = (bf16[16,128]{1,0:T(8,128)(2,1)S(1)}, bf16[16,128]{1,0:T(8,128)(2,1)S(1)}, u32[]{:S(2)}, u32[]{:S(2)}) collective-permute-start(bf16[16,128]{1,0:T(8,128)(2,1)S(1)} %pad.8), channel_id=1, source_target_pairs={{5,0},{4,1},{6,2},{7,3},{0,4},{1,5},{3,6},{2,7},{13,8},{12,9},{14,... | collective-permute-start | bytes 12296 | tf_op jit(solution)/shard_map/ppermute | solution.py:56
  3.1 5.7 %collective-permute-start = (bf16[256,128]{1,0:T(8,128)(2,1)}, bf16[256,128]{1,0:T(8,128)(2,1)S(1)}, u32[]{:S(2)}, u32[]{:S(2)}) collective-permute-start(bf16[256,128]{1,0:T(8,128)(2,1)} %feat_ref.1), channel_id=1, source_target_pairs={{5,0},{4,1},{6,2},{7,3},{0,4},{1,5},{3,6},{2,7},{13,8},{12,9},{14,... | collective-permute-start | bytes 196616 | tf_op jit(solution)/shard_map/ppermute | solution.py:56
  9.6 11.3 %collective-permute-start.2 = (bf16[544,128]{1,0:T(8,128)(2,1)S(1)}, bf16[544,128]{1,0:T(8,128)(2,1)S(1)}, u32[]{:S(2)}, u32[]{:S(2)}) collective-permute-start(bf16[544,128]{1,0:T(8,128)(2,1)S(1)} %pad_maximum_fusion.refs_0_), channel_id=1, source_target_pairs={{120,0},{9,1},{122,2},{11,3},{124,4},{13,5},{126,6},{15,7},{0,8},{... | collective-permute-start | bytes 417800 | tf_op jit(solution)/shard_map/ppermute | solution.py:56
  11.6 10.3 %collective-permute-start.3 = (bf16[544,128]{1,0:T(8,128)(2,1)S(1)}, bf16[544,128]{1,0:T(8,128)(2,1)S(1)}, u32[]{:S(2)}, u32[]{:S(2)}) collective-permute-start(bf16[544,128]{1,0:T(8,128)(2,1)S(1)} %pad_maximum_fusion.refs_0_), channel_id=1, source_target_pairs={{112,0},{17,1},{114,2},{19,3},{116,4},{21,5},{118,6},{23,7},{120,8... | collective-permute-start | bytes 417800 | tf_op jit(solution)/shard_map/ppermute | solution.py:56
  15.2 7.5 %collective-permute-start.4 = (bf16[544,128]{1,0:T(8,128)(2,1)S(1)}, bf16[544,128]{1,0:T(8,128)(2,1)S(1)}, u32[]{:S(2)}, u32[]{:S(2)}) collective-permute-start(bf16[544,128]{1,0:T(8,128)(2,1)S(1)} %pad_maximum_fusion.refs_0_), channel_id=1, source_target_pairs={{104,0},{25,1},{106,2},{27,3},{108,4},{29,5},{110,6},{31,7},{112,8... | collective-permute-start | bytes 417800 | tf_op jit(solution)/shard_map/ppermute | solution.py:56
  17.1 6.3 %collective-permute-start.5 = (bf16[544,128]{1,0:T(8,128)(2,1)S(1)}, bf16[544,128]{1,0:T(8,128)(2,1)S(1)}, u32[]{:S(2)}, u32[]{:S(2)}) collective-permute-start(bf16[544,128]{1,0:T(8,128)(2,1)S(1)} %pad_maximum_fusion.refs_0_), channel_id=1, source_target_pairs={{96,0},{33,1},{98,2},{35,3},{100,4},{37,5},{102,6},{39,7},{104,8},... | collective-permute-start | bytes 417800 | tf_op jit(solution)/shard_map/ppermute | solution.py:56
  23.4 13.0 %collective-permute-start.6 = (bf16[2176,128]{1,0:T(8,128)(2,1)S(1)}, bf16[2176,128]{1,0:T(8,128)(2,1)S(1)}, u32[]{:S(2)}, u32[]{:S(2)}) collective-permute-start(bf16[2176,128]{1,0:T(8,128)(2,1)S(1)} %constant_dynamic-update-slice_fusion.refs_1_), channel_id=1, source_target_pairs={{96,0},{33,1},{98,2},{35,3},{100,4},{37,5},{102,6},{39,7},{104,8},... | collective-permute-start | bytes 1671176 | tf_op jit(solution)/shard_map/ppermute | solution.py:56
  23.9 26.0 %collective-permute-start.9 = (bf16[2176,128]{1,0:T(8,128)(2,1)S(1)}, bf16[2176,128]{1,0:T(8,128)(2,1)S(1)}, u32[]{:S(2)}, u32[]{:S(2)}) collective-permute-start(bf16[2176,128]{1,0:T(8,128)(2,1)S(1)} %constant_dynamic-update-slice_fusion.refs_1_), channel_id=1, source_target_pairs={{2,0},{3,1},{0,2},{1,3},{6,4},{7,5},{4,6},{5,7},{10,8},{11,9},{8,1... | collective-permute-start | bytes 1671176 | tf_op jit(solution)/shard_map/ppermute | solution.py:56
  36.5 15.1 %collective-permute-start.7 = (bf16[2176,128]{1,0:T(8,128)(2,1)S(1)}, bf16[2176,128]{1,0:T(8,128)(2,1)S(1)}, u32[]{:S(2)}, u32[]{:S(2)}) collective-permute-start(bf16[2176,128]{1,0:T(8,128)(2,1)S(1)} %collective-permute-done.6.refs_0_), channel_id=1, source_target_pairs={{2,0},{3,1},{0,2},{1,3},{6,4},{7,5},{4,6},{5,7},{10,8},{11,9},{8,1... | collective-permute-start | bytes 1671176 | tf_op jit(solution)/shard_map/ppermute | solution.py:56
  36.5 13.3 %collective-permute-start.8 = (bf16[544,128]{1,0:T(8,128)(2,1)S(1)}, bf16[544,128]{1,0:T(8,128)(2,1)S(1)}, u32[]{:S(2)}, u32[]{:S(2)}) collective-permute-start(bf16[544,128]{1,0:T(8,128)(2,1)S(1)} %pad_maximum_fusion.refs_0_), channel_id=1, source_target_pairs={{2,0},{3,1},{0,2},{1,3},{6,4},{7,5},{4,6},{5,7},{10,8},{11,9},{8,1... | collective-permute-start | bytes 417800 | tf_op jit(solution)/shard_map/ppermute | solution.py:56
  37.0 16.4 %collective-permute-start.11 = (bf16[528,128]{1,0:T(8,128)(2,1)S(1)}, bf16[528,128]{1,0:T(8,128)(2,1)S(1)}, u32[]{:S(2)}, u32[]{:S(2)}) collective-permute-start(bf16[528,128]{1,0:T(8,128)(2,1)S(1)} %pad_maximum_fusion.1), channel_id=1, source_target_pairs={{1,0},{0,1},{3,2},{2,3},{5,4},{4,5},{7,6},{6,7},{9,8},{8,9},{11,10... | collective-permute-start | bytes 405512 | tf_op jit(solution)/shard_map/ppermute | solution.py:56
  45.5 4.3 %copy-start = (bf16[64,16,256]{2,1,0:T(8,128)(2,1)S(1)}, bf16[64,16,256]{2,1,0:T(8,128)(2,1)}, u32[]{:S(2)}) copy-start(bf16[64,16,256]{2,1,0:T(8,128)(2,1)} %refs_3_.1) | copy-start | bytes 1572868
  51.5 7.5 %copy-start.1 = (bf16[256,128]{1,0:T(8,128)(2,1)S(1)}, bf16[256,128]{1,0:T(8,128)(2,1)}, u32[]{:S(2)}) copy-start(bf16[256,128]{1,0:T(8,128)(2,1)} %feat_ref.1) | copy-start | bytes 196612
  51.5 7.5 %copy-start.2 = (bf16[256,128]{1,0:T(8,128)(2,1)S(1)}, bf16[256,128]{1,0:T(8,128)(2,1)}, u32[]{:S(2)}) copy-start(bf16[256,128]{1,0:T(8,128)(2,1)} %ct_ref.1) | copy-start | bytes 196612
  51.5 7.5 %copy-start.3 = (bf16[128,128]{1,0:T(8,128)(2,1)S(1)}, bf16[128,128]{1,0:T(8,128)(2,1)}, u32[]{:S(2)}) copy-start(bf16[128,128]{1,0:T(8,128)(2,1)} %sw_ref.1) | copy-start | bytes 98308
  51.6 7.5 %copy-start.4 = (bf16[128,128]{1,0:T(8,128)(2,1)S(1)}, bf16[128,128]{1,0:T(8,128)(2,1)}, u32[]{:S(2)}) copy-start(bf16[128,128]{1,0:T(8,128)(2,1)} %nw_ref.1) | copy-start | bytes 98308
  51.6 7.5 %copy-start.5 = (f32[128]{0:T(128)S(1)}, f32[128]{0:T(128)}, u32[]{:S(2)}) copy-start(f32[128]{0:T(128)} %param.22) | copy-start | bytes 1540
  53.2 5.8 %collective-permute-start.10 = (bf16[256,128]{1,0:T(8,128)(2,1)S(1)}, bf16[256,128]{1,0:T(8,128)(2,1)S(1)}, u32[]{:S(2)}, u32[]{:S(2)}) collective-permute-start(bf16[256,128]{1,0:T(8,128)(2,1)S(1)} %get-tuple-element.34.mine_ref), channel_id=1, source_target_pairs={{1,0},{0,1},{3,2},{2,3},{5,4},{4,5},{7,6},{6,7},{9,8},{8,9},{11,10... | collective-permute-start | bytes 196616 | tf_op jit(solution)/shard_map/ppermute | solution.py:56
  60.5 2.1 %collective-permute-start.15 = (f32[2,72,128]{2,1,0:T(8,128)S(1)}, f32[2,72,128]{2,1,0:T(8,128)S(1)}, u32[]{:S(2)}, u32[]{:S(2)}) collective-permute-start(f32[2,72,128]{2,1,0:T(8,128)S(1)} %get-tuple-element.43), channel_id=1, source_target_pairs={{2,0},{3,1},{0,2},{1,3},{6,4},{7,5},{4,6},{5,7},{10,8},{11,9},{8,1... | collective-permute-start | bytes 221192 | tf_op jit(solution)/shard_map/ppermute | solution.py:56
  62.0 11.6 %collective-permute-start.13 = (bf16[4,128,512]{2,1,0:T(8,128)(2,1)S(1)}, bf16[4,128,512]{2,1,0:T(8,128)(2,1)S(1)}, u32[]{:S(2)}, u32[]{:S(2)}) collective-permute-start(bf16[4,128,512]{2,1,0:T(8,128)(2,1)S(1)} %shard_map.162), channel_id=1, source_target_pairs={{2,0},{3,1},{0,2},{1,3},{6,4},{7,5},{4,6},{5,7},{10,8},{11,9},{8,1... | collective-permute-start | bytes 1572872 | tf_op jit(solution)/shard_map/ppermute | solution.py:56
  62.6 6.8 %collective-permute-start.16 = (f32[72,128]{1,0:T(8,128)S(1)}, f32[72,128]{1,0:T(8,128)S(1)}, u32[]{:S(2)}, u32[]{:S(2)}) collective-permute-start(f32[72,128]{1,0:T(8,128)S(1)} %slice_bitcast_fusion), channel_id=1, source_target_pairs={{4,0},{5,1},{6,2},{7,3},{0,4},{1,5},{2,6},{3,7},{12,8},{13,9},{14,... | collective-permute-start | bytes 110600 | tf_op jit(solution)/shard_map/ppermute | solution.py:56
  69.2 22.6 %collective-permute-start.12 = (bf16[5,128,512]{2,1,0:T(8,128)(2,1)S(1)}, bf16[5,128,512]{2,1,0:T(8,128)(2,1)S(1)}, u32[]{:S(2)}, u32[]{:S(2)}) collective-permute-start(bf16[5,128,512]{2,1,0:T(8,128)(2,1)S(1)} %shard_map.160), channel_id=1, source_target_pairs={{2,0},{3,1},{0,2},{1,3},{6,4},{7,5},{4,6},{5,7},{10,8},{11,9},{8,1... | collective-permute-start | bytes 1966088 | tf_op jit(solution)/shard_map/ppermute | solution.py:56
  69.5 9.2 %collective-permute-start.17 = (f32[72,128]{1,0:T(8,128)S(1)}, f32[72,128]{1,0:T(8,128)S(1)}, u32[]{:S(2)}, u32[]{:S(2)}) collective-permute-start(f32[72,128]{1,0:T(8,128)S(1)} %fusion), channel_id=1, source_target_pairs={{8,0},{9,1},{10,2},{11,3},{12,4},{13,5},{14,6},{15,7},{0,8},{1,9},... | collective-permute-start | bytes 110600 | tf_op jit(solution)/shard_map/ppermute | solution.py:56
  69.5 9.2 %collective-permute-start.18 = (f32[72,128]{1,0:T(8,128)S(1)}, f32[72,128]{1,0:T(8,128)S(1)}, u32[]{:S(2)}, u32[]{:S(2)}) collective-permute-start(f32[72,128]{1,0:T(8,128)S(1)} %fusion), channel_id=1, source_target_pairs={{24,0},{25,1},{26,2},{27,3},{28,4},{29,5},{30,6},{31,7},{16,8},{17... | collective-permute-start | bytes 110600 | tf_op jit(solution)/shard_map/ppermute | solution.py:56
  70.3 8.4 %collective-permute-start.19 = (f32[72,128]{1,0:T(8,128)S(1)}, f32[72,128]{1,0:T(8,128)S(1)}, u32[]{:S(2)}, u32[]{:S(2)}) collective-permute-start(f32[72,128]{1,0:T(8,128)S(1)} %fusion), channel_id=1, source_target_pairs={{16,0},{17,1},{18,2},{19,3},{20,4},{21,5},{22,6},{23,7},{24,8},{25... | collective-permute-start | bytes 110600 | tf_op jit(solution)/shard_map/ppermute | solution.py:56
  75.1 18.4 %collective-permute-start.14 = (bf16[4,128,512]{2,1,0:T(8,128)(2,1)S(1)}, bf16[4,128,512]{2,1,0:T(8,128)(2,1)S(1)}, u32[]{:S(2)}, u32[]{:S(2)}) collective-permute-start(bf16[4,128,512]{2,1,0:T(8,128)(2,1)S(1)} %shard_map.163), channel_id=1, source_target_pairs={{0,96},{1,33},{2,98},{3,35},{4,100},{5,37},{6,102},{7,39},{8,104},... | collective-permute-start | bytes 1572872 | tf_op jit(solution)/shard_map/ppermute | solution.py:56
  78.7 11.0 %collective-permute-start.27 = (f32[72,128]{1,0:T(8,128)S(1)}, f32[72,128]{1,0:T(8,128)S(1)}, u32[]{:S(2)}, u32[]{:S(2)}) collective-permute-start(f32[72,128]{1,0:T(8,128)S(1)} %add_add_fusion.1), channel_id=1, source_target_pairs={{32,0},{33,1},{34,2},{35,3},{36,4},{37,5},{38,6},{39,7},{40,8},{41... | collective-permute-start | bytes 110600 | tf_op jit(solution)/shard_map/ppermute | solution.py:56
  78.8 12.4 %collective-permute-start.28 = (f32[72,128]{1,0:T(8,128)S(1)}, f32[72,128]{1,0:T(8,128)S(1)}, u32[]{:S(2)}, u32[]{:S(2)}) collective-permute-start(f32[72,128]{1,0:T(8,128)S(1)} %add_add_fusion.1), channel_id=1, source_target_pairs={{96,0},{97,1},{98,2},{99,3},{100,4},{101,5},{102,6},{103,7},{104,8... | collective-permute-start | bytes 110600 | tf_op jit(solution)/shard_map/ppermute | solution.py:56
  79.3 11.9 %collective-permute-start.29 = (f32[72,128]{1,0:T(8,128)S(1)}, f32[72,128]{1,0:T(8,128)S(1)}, u32[]{:S(2)}, u32[]{:S(2)}) collective-permute-start(f32[72,128]{1,0:T(8,128)S(1)} %add_add_fusion.1), channel_id=1, source_target_pairs={{64,0},{65,1},{66,2},{67,3},{68,4},{69,5},{70,6},{71,7},{72,8},{73... | collective-permute-start | bytes 110600 | tf_op jit(solution)/shard_map/ppermute | solution.py:56
  91.2 8.5 %collective-permute-start.30 = (f32[72,128]{1,0:T(8,128)S(1)}, f32[72,128]{1,0:T(8,128)S(1)}, u32[]{:S(2)}, u32[]{:S(2)}) collective-permute-start(f32[72,128]{1,0:T(8,128)S(1)} %add_add_fusion.mine_ref), channel_id=1, source_target_pairs={{4,0},{5,1},{6,2},{7,3},{0,4},{1,5},{2,6},{3,7},{12,8},{13,9},{14,... | collective-permute-start | bytes 110600 | tf_op jit(solution)/shard_map/ppermute | solution.py:56
  94.1 8.0 %collective-permute-start.20 = (bf16[128,512]{1,0:T(8,128)(2,1)S(1)}, bf16[128,512]{1,0:T(8,128)(2,1)S(1)}, u32[]{:S(2)}, u32[]{:S(2)}) collective-permute-start(bf16[128,512]{1,0:T(8,128)(2,1)S(1)} %get-tuple-element.45), channel_id=1, source_target_pairs={{0,120},{1,9},{2,122},{3,11},{4,124},{5,13},{6,126},{7,15},{8,0},{... | collective-permute-start | bytes 393224 | tf_op jit(solution)/shard_map/ppermute | solution.py:56
  98.2 7.6 %collective-permute-start.21 = (bf16[128,512]{1,0:T(8,128)(2,1)S(1)}, bf16[128,512]{1,0:T(8,128)(2,1)S(1)}, u32[]{:S(2)}, u32[]{:S(2)}) collective-permute-start(bf16[128,512]{1,0:T(8,128)(2,1)S(1)} %get-tuple-element.46), channel_id=1, source_target_pairs={{0,112},{1,17},{2,114},{3,19},{4,116},{5,21},{6,118},{7,23},{8,120... | collective-permute-start | bytes 393224 | tf_op jit(solution)/shard_map/ppermute | solution.py:56
  99.7 7.0 %collective-permute-start.22 = (bf16[128,512]{1,0:T(8,128)(2,1)S(1)}, bf16[128,512]{1,0:T(8,128)(2,1)S(1)}, u32[]{:S(2)}, u32[]{:S(2)}) collective-permute-start(bf16[128,512]{1,0:T(8,128)(2,1)S(1)} %get-tuple-element.47), channel_id=1, source_target_pairs={{0,104},{1,25},{2,106},{3,27},{4,108},{5,29},{6,110},{7,31},{8,112... | collective-permute-start | bytes 393224 | tf_op jit(solution)/shard_map/ppermute | solution.py:56
  99.7 8.3 %collective-permute-start.23 = (bf16[128,512]{1,0:T(8,128)(2,1)S(1)}, bf16[128,512]{1,0:T(8,128)(2,1)S(1)}, u32[]{:S(2)}, u32[]{:S(2)}) collective-permute-start(bf16[128,512]{1,0:T(8,128)(2,1)S(1)} %get-tuple-element.48), channel_id=1, source_target_pairs={{0,96},{1,33},{2,98},{3,35},{4,100},{5,37},{6,102},{7,39},{8,104},... | collective-permute-start | bytes 393224 | tf_op jit(solution)/shard_map/ppermute | solution.py:56
  99.8 13.4 %collective-permute-start.31 = (f32[2,72,128]{2,1,0:T(8,128)S(1)}, f32[2,72,128]{2,1,0:T(8,128)S(1)}, u32[]{:S(2)}, u32[]{:S(2)}) collective-permute-start(f32[2,72,128]{2,1,0:T(8,128)S(1)} %pad_maximum_fusion.2), channel_id=1, source_target_pairs={{2,0},{3,1},{0,2},{1,3},{6,4},{7,5},{4,6},{5,7},{10,8},{11,9},{8,1... | collective-permute-start | bytes 221192 | tf_op jit(solution)/shard_map/ppermute | solution.py:56
  108.7 5.8 %collective-permute-start.24 = (bf16[128,256]{1,0:T(8,128)(2,1)S(1)}, bf16[128,256]{1,0:T(8,128)(2,1)S(1)}, u32[]{:S(2)}, u32[]{:S(2)}) collective-permute-start(bf16[128,256]{1,0:T(8,128)(2,1)S(1)} %get-tuple-element.49.same_ref), channel_id=1, source_target_pairs={{1,0},{0,1},{3,2},{2,3},{5,4},{4,5},{7,6},{6,7},{9,8},{8,9},{11,10... | collective-permute-start | bytes 196616 | tf_op jit(solution)/shard_map/ppermute | solution.py:56
  108.8 6.6 %collective-permute-start.25 = (bf16[128,256]{1,0:T(8,128)(2,1)S(1)}, bf16[128,256]{1,0:T(8,128)(2,1)S(1)}, u32[]{:S(2)}, u32[]{:S(2)}) collective-permute-start(bf16[128,256]{1,0:T(8,128)(2,1)S(1)} %get-tuple-element.50), channel_id=1, source_target_pairs={{5,0},{4,1},{7,2},{6,3},{0,4},{1,5},{2,6},{3,7},{13,8},{12,9},{15,... | collective-permute-start | bytes 196616 | tf_op jit(solution)/shard_map/ppermute | solution.py:56
  110.5 4.8 %collective-permute-start.26 = (bf16[128,256]{1,0:T(8,128)(2,1)S(1)}, bf16[128,256]{1,0:T(8,128)(2,1)S(1)}, u32[]{:S(2)}, u32[]{:S(2)}) collective-permute-start(bf16[128,256]{1,0:T(8,128)(2,1)S(1)} %get-tuple-element.50), channel_id=1, source_target_pairs={{4,0},{5,1},{6,2},{7,3},{1,4},{0,5},{3,6},{2,7},{12,8},{13,9},{14,... | collective-permute-start | bytes 196616 | tf_op jit(solution)/shard_map/ppermute | solution.py:56

commit v2 on v1

--- a/solution.py
+++ b/solution.py
@@ -105,7 +105,8 @@
     return call
 
 
-DEPTH = 8
+DEPTH = 12
+QUAD = 4
 NEAR, FAR = tuple(range(5)), tuple(range(5, COLS))
 
 
@@ -119,31 +120,49 @@
         k = columns[0] + lax.rem(slot // 2, len(columns))
         source, valid = slot_source(ids_ref, cls, k, lax.rem(slot, 2))
         offset = lax.bitwise_and(ids_ref[0] - source + 64, 63) - 32 * ids_ref[1]
-        return jnp.where(valid, offset, 0), valid
-
-    def fetch(slot, at):
-        offset, _ = place(slot)
-        return pltpu.make_async_copy(tiles_ref.at[0, offset], buf_ref.at[at], sem_ref.at[at])
+        offset = jnp.where(valid, offset, 0)
+        return offset, jnp.where(valid, table_ref[counts_at + offset], 0)
+
+    def fetch(slot, act):
+        offset, live = place(slot)
+        at = lax.rem(slot, DEPTH)
+        for i in range(0, width, QUAD):
+
+            @pl.when(live > i)
+            def _():
+                act(
+                    pltpu.make_async_copy(
+                        tiles_ref.at[0, offset, pl.ds(i, QUAD)],
+                        buf_ref.at[at, pl.ds(i, QUAD)],
+                        sem_ref.at[at, i // QUAD],
+                    )
+                )
+
+    def start(copy):
+        copy.start()
+
+    def wait(copy):
+        copy.wait()
 
     for u in range(DEPTH):
-        fetch(u, u).start()
+        fetch(u, start)
 
     def body(slot, carry):
         at = lax.rem(slot, DEPTH)
-        offset, valid = place(slot)
+        offset, live = place(slot)
         acc_ref[...] = jnp.zeros_like(acc_ref)
-        fetch(slot, at).wait()
+        fetch(slot, wait)
 
         def add(j, inner):
             code = table_ref[offset * width + j]
             acc_ref[code] += buf_ref[at, j].astype(jnp.float32)
             return inner
 
-        lax.fori_loop(0, jnp.where(valid, table_ref[counts_at + offset], 0), add, 0)
+        lax.fori_loop(0, live, add, 0)
 
         @pl.when(slot + DEPTH < slots)
         def _():
-            fetch(slot + DEPTH, at).start()
+            fetch(slot + DEPTH, start)
 
         for t in range(2):
             for s in range(2):
@@ -163,11 +182,16 @@
         scratch_shapes=[
             pltpu.VMEM((4, 128, 128), jnp.float32),
             pltpu.VMEM((DEPTH,) + tile_values.shape[2:], jnp.bfloat16),
-            pltpu.SemaphoreType.DMA((DEPTH,)),
+            pltpu.SemaphoreType.DMA((DEPTH, tile_values.shape[2] // QUAD)),
         ],
         out_shape=jax.ShapeDtypeStruct((4 * len(columns), 256, 256), jnp.bfloat16),
         compiler_params=pltpu.CompilerParams(vmem_limit_bytes=48 * MIB),
     )(ids, table, tile_values)
+
+
+def join_kernel(ids_ref, *refs):
+    for i, ref in enumerate(refs[:-1]):
+        refs[-1][i * GROUP : (i + 1) * GROUP, :] = ref[...]
 
 
 def forward_kernel(columns, first, ids_ref, *refs):
@@ -267,13 +291,15 @@
 def backward_kernel(cls, columns, add, ids_ref, grad_ref, mats_ref, hot_ref, wts_ref, *refs):
     out_ref = refs[-1]
     grad = grad_ref[...]
+    count = 2 * len(columns) * HEAD
+    backs = dot_nt(wts_ref[cls * count : (cls + 1) * count, :], grad).astype(jnp.bfloat16)
     for i in range(len(columns)):
         for lr in range(2):
             slot = (cls * len(columns) + i) * 2 + lr
             at = slice(slot * HEAD, (slot + 1) * HEAD)
             lanes = slice(lr * 256, (lr + 1) * 256)
-            back = dot_nt(grad, wts_ref[at, :]).astype(jnp.bfloat16)
-            part = dot(grad, mats_ref[slot]) + dot(back, hot_ref[at, :])
+            back = backs[(2 * i + lr) * HEAD : (2 * i + lr + 1) * HEAD]
+            part = dot(grad, mats_ref[slot]) + dot_tn(back, hot_ref[at, :])
             if add:
                 part += refs[0][i, :, lanes].astype(jnp.float32)
             out_ref[i, :, lanes] = part.astype(out_ref.dtype)
@@ -300,20 +326,18 @@
     cross_ref[...] = total[:, 256:].astype(jnp.bfloat16)
 
 
-def finish_kernel(ids_ref, same_ref, rep_ref, down_ref, up_ref, self_ref, grad_ref):
+def finish_kernel(scale, ids_ref, *refs):
     f32 = jnp.float32
+    same_ref, rep_ref, down_ref, up_ref, add_ref = refs[:5]
+    parts, (grad_ref, self_ref, neighbor_ref, bias_ref, sums_ref, bias_sums_ref) = refs[5:9], refs[9:]
     total = (same_ref[...].astype(f32) + rep_ref[...].astype(f32)) + (
         down_ref[...].astype(f32) + up_ref[...].astype(f32)
     )
-    grad_ref[...] = (total + self_ref[...]).T.astype(jnp.bfloat16)
-
-
-def weights_kernel(scale, ids_ref, mine_ref, line_ref, core_ref, *refs):
-    self_ref, neighbor_ref, bias_ref, sums_ref, bias_sums_ref = refs
+    grad_ref[...] = (total + add_ref[...]).T.astype(jnp.bfloat16)
     low = lax.bitwise_and(ids_ref[0], 3)
     for lr in range(2):
         for cls in range(2):
-            part = core_ref.at[lr] if cls else (line_ref if lr else mine_ref)
+            part = parts[2 * cls + lr]
             quarter = lax.bitwise_xor(low, 2 * lr + cls)
             sums_ref[pl.ds(pl.multiple_of(quarter * 64, 64), 64), :] = part[0:64, :]
             bias_sums_ref[quarter] = part[64:PART, :]
@@ -360,7 +384,7 @@
     other = permute(packed, SWAP_R)
     cols = [permute(col0, FROM_COL[k]) for k in range(1, 5)]
     oth0 = permute(col0, SWAP_C)
-    cols = jnp.concatenate(cols, axis=0)
+    cols = kernel_call(join_kernel, 4, ((4 * GROUP, 128), bf16))(ids, *cols)
     far = permute(cols, FROM_COL[4])
     oth1 = permute(cols, SWAP_C)
     mats_near = densify(NEAR, ids, table, tile_values)
@@ -411,21 +435,18 @@
     got = [permute(near[k - 1], inverse(FROM_COL[k])) for k in range(1, 5)]
     quarter = over_columns(quarter, SAME_Z)
     line = permute(quarter, SWAP_L)
-    core = permute(jnp.stack([quarter, line]), SWAP_C)
+    core0, core1 = permute(quarter, SWAP_C), permute(line, SWAP_C)
     piece = ((128, 256), bf16)
     same, cross = kernel_call(mine_kernel, 5, [piece] * 2)(ids, keep, *got)
     over = permute(same, SWAP_R)
     down = permute(cross, FROM_DOWN)
     up = permute(cross, FROM_UP)
-    grad_input = kernel_call(finish_kernel, 5, ((256, 128), bf16))(
-        ids, same, over, down, up, self_grad
-    )
-    grad_self, grad_neighbor, grad_bias = kernel_call(
-        functools.partial(weights_kernel, 1.0 / math.sqrt(256 * blocks)),
-        3,
-        [((128, 128), f32), ((128, 128), f32), ((1, 128), f32)],
+    grad_input, grad_self, grad_neighbor, grad_bias = kernel_call(
+        functools.partial(finish_kernel, 1.0 / math.sqrt(256 * blocks)),
+        9,
+        [((256, 128), bf16), ((128, 128), f32), ((128, 128), f32), ((1, 128), f32)],
         scratch=[pltpu.VMEM((256, 128), f32), pltpu.VMEM((4, PART - 64, 128), f32)],
-    )(ids, quarter, line, core)
+    )(ids, same, over, down, up, self_grad, quarter, line, core0, core1)
     return output, grad_input, grad_self, grad_neighbor, grad_bias[0]
 
 

time: 118 us -> 108 us (0.915)
  waiting for transfers between devices: 41.5 us -> 36.4 us
  Pallas kernels: 24.6 us -> 20.2 us
    ppermute x32 -> x33, waiting for transfers between devices: 41.5 us -> 36.4 us  [permute(): return lax.ppermute(x, AXES, pairs)]
    pallas_call x2, Pallas kernels: 9.76 us -> 7.4 us  [densify(): pl.pallas_call(functools.partial(densify_kernel, columns), in_specs=[smem...]
    pallas_call x11, Pallas kernels: 14.8 us -> 12.8 us  [call(): pl.pallas_call(body, in_specs=[smem()] + [vmem()] * n_in, out_specs=vmem(...]
    ppermute x32 -> x33, starting transfers between devices: 44.7 us -> 44.7 us  [permute(): return lax.ppermute(x, AXES, pairs)]
  transfers between devices with their start and end apart: 32 -> 33, of which waited for: 16 -> 18; matrix products, arithmetic and copies ran while one was open for 3% -> 3% of each run, Pallas kernels for 19% -> 15%
where the time goes in v2:
time: 108 us; the launch traced here: 107 us
  starting transfers between devices  44.7 us (41%)
  waiting for transfers between devices  36.4 us (34%)
  Pallas kernels  20.2 us (19%)
  other arithmetic  4.58 us (4%)
    ppermute x33, starting transfers between devices, permute(): return lax.ppermute(x, AXES, pairs)  44.7 us
    ppermute x33, waiting for transfers between devices, permute(): return lax.ppermute(x, AXES, pairs)  36.4 us
    pallas_call x11, Pallas kernels, call(): pl.pallas_call(body, in_specs=[smem()] + [vmem()] * n_in, out_specs=vmem(...  12.8 us
    pallas_call x2, Pallas kernels, densify(): pl.pallas_call(functools.partial(densify_kernel, columns), in_specs=[smem...  7.4 us
  transfers between devices with their start and end apart: 33, of which 18 were waited for; matrix products, arithmetic and copies ran while one was open for 3% of the time, Pallas kernels for 15%

profile of v2, /device:TPU:0, one launch (start us, length us, event | category | flops | bytes accessed | tf_op | source)
XLA Modules:
  0.0 106.9 jit_solution(12067502797100113026)
XLA Ops:
  0.6 0.7 fusion.5
  1.3 1.8 %collective-permute-start.1 = (bf16[16,128]{1,0:T(8,128)(2,1)S(1)}, bf16[16,128]{1,0:T(8,128)(2,1)S(1)}, u32[]{:S(2)}, u32[]{:S(2)}) collective-permute-start(bf16[16,128]{1,0:T(8,128)(2,1)S(1)} %pad.8), channel_id=1, source_target_pairs={{5,0},{4,1},{6,2},{7,3},{0,4},{1,5},{3,6},{2,7},{13,8},{12,9},{14,... | collective-permute-start | bytes 12296 | tf_op jit(solution)/shard_map/ppermute | solution.py:56
  3.1 1.6 %collective-permute-start = (bf16[256,128]{1,0:T(8,128)(2,1)}, bf16[256,128]{1,0:T(8,128)(2,1)S(1)}, u32[]{:S(2)}, u32[]{:S(2)}) collective-permute-start(bf16[256,128]{1,0:T(8,128)(2,1)} %feat_ref.1), channel_id=1, source_target_pairs={{5,0},{4,1},{6,2},{7,3},{0,4},{1,5},{3,6},{2,7},{13,8},{12,9},{14,... | collective-permute-start | bytes 196616 | tf_op jit(solution)/shard_map/ppermute | solution.py:56
  4.7 0.7 fusion.8
  5.3 0.7 multiply_add_fusion
  6.2 0.7 pad_add_fusion.table_ref
  6.9 0.9 pad_maximum_fusion.1
  7.8 1.0 collective-permute-done
  8.8 0.8 pad_maximum_fusion.refs_0_
  9.6 2.0 %collective-permute-start.2 = (bf16[544,128]{1,0:T(8,128)(2,1)S(1)}, bf16[544,128]{1,0:T(8,128)(2,1)S(1)}, u32[]{:S(2)}, u32[]{:S(2)}) collective-permute-start(bf16[544,128]{1,0:T(8,128)(2,1)S(1)} %pad_maximum_fusion.refs_0_), channel_id=1, source_target_pairs={{120,0},{9,1},{122,2},{11,3},{124,4},{13,5},{126,6},{15,7},{0,8},{... | collective-permute-start | bytes 417800 | tf_op jit(solution)/shard_map/ppermute | solution.py:56
  11.6 3.6 %collective-permute-start.3 = (bf16[544,128]{1,0:T(8,128)(2,1)S(1)}, bf16[544,128]{1,0:T(8,128)(2,1)S(1)}, u32[]{:S(2)}, u32[]{:S(2)}) collective-permute-start(bf16[544,128]{1,0:T(8,128)(2,1)S(1)} %pad_maximum_fusion.refs_0_), channel_id=1, source_target_pairs={{112,0},{17,1},{114,2},{19,3},{116,4},{21,5},{118,6},{23,7},{120,8... | collective-permute-start | bytes 417800 | tf_op jit(solution)/shard_map/ppermute | solution.py:56
  15.2 1.9 %collective-permute-start.4 = (bf16[544,128]{1,0:T(8,128)(2,1)S(1)}, bf16[544,128]{1,0:T(8,128)(2,1)S(1)}, u32[]{:S(2)}, u32[]{:S(2)}) collective-permute-start(bf16[544,128]{1,0:T(8,128)(2,1)S(1)} %pad_maximum_fusion.refs_0_), channel_id=1, source_target_pairs={{104,0},{25,1},{106,2},{27,3},{108,4},{29,5},{110,6},{31,7},{112,8... | collective-permute-start | bytes 417800 | tf_op jit(solution)/shard_map/ppermute | solution.py:56
  17.1 1.5 %collective-permute-start.5 = (bf16[544,128]{1,0:T(8,128)(2,1)S(1)}, bf16[544,128]{1,0:T(8,128)(2,1)S(1)}, u32[]{:S(2)}, u32[]{:S(2)}) collective-permute-start(bf16[544,128]{1,0:T(8,128)(2,1)S(1)} %pad_maximum_fusion.refs_0_), channel_id=1, source_target_pairs={{96,0},{33,1},{98,2},{35,3},{100,4},{37,5},{102,6},{39,7},{104,8},... | collective-permute-start | bytes 417800 | tf_op jit(solution)/shard_map/ppermute | solution.py:56
  18.6 2.3 %collective-permute-done.2.refs_0_ = bf16[544,128]{1,0:T(8,128)(2,1)S(1)} collective-permute-done((bf16[544,128]{1,0:T(8,128)(2,1)S(1)}, bf16[544,128]{1,0:T(8,128)(2,1)S(1)}, u32[]{:S(2)}, u32[]{:S(2)}) %collective-permute-start.2) | collective-permute-done | bytes 139296 | tf_op jit(solution)/shard_map/ppermute | solution.py:56
  20.9 1.0 collective-permute-done.3.refs_1_
  21.9 0.8 collective-permute-done.4.refs_2_
  22.8 0.7 collective-permute-done.5.refs_3_
  23.4 0.6 shard_map.155.refs_1_
  24.0 0.3 collective-permute-start.6
  24.4 12.7 %collective-permute-done.6.refs_0_ = bf16[2176,128]{1,0:T(8,128)(2,1)S(1)} collective-permute-done((bf16[2176,128]{1,0:T(8,128)(2,1)S(1)}, bf16[2176,128]{1,0:T(8,128)(2,1)S(1)}, u32[]{:S(2)}, u32[]{:S(2)}) %collective-permute-start.6) | collective-permute-done | bytes 557088 | tf_op jit(solution)/shard_map/ppermute | solution.py:56
  37.0 0.5 collective-permute-start.8
  37.6 3.0 %collective-permute-start.11 = (bf16[528,128]{1,0:T(8,128)(2,1)S(1)}, bf16[528,128]{1,0:T(8,128)(2,1)S(1)}, u32[]{:S(2)}, u32[]{:S(2)}) collective-permute-start(bf16[528,128]{1,0:T(8,128)(2,1)S(1)} %pad_maximum_fusion.1), channel_id=1, source_target_pairs={{1,0},{0,1},{3,2},{2,3},{5,4},{4,5},{7,6},{6,7},{9,8},{8,9},{11,10... | collective-permute-start | bytes 405512 | tf_op jit(solution)/shard_map/ppermute | solution.py:56
  40.6 4.1 %shard_map.157.refs_4_.mats_ref = bf16[20,256,256]{2,1,0:T(8,128)(2,1)S(1)} custom-call(s32[2]{0:T(128)S(1)} %pad_add_fusion.1.ids_ref, s32[544]{0:T(1024)S(1)} %pad_add_fusion.table_ref, bf16[1,32,16,128,128]{4,3,2,1,0:T(8,128)(2,1)} %tiles_ref.3), custom_call_target="tpu_custom_call" | custom-call | tf_op jit(solution)/shard_map/pallas_call | solution.py:178
  44.7 3.3 %shard_map.156.refs_2_.mats_ref = bf16[16,256,256]{2,1,0:T(8,128)(2,1)S(1)} custom-call(s32[2]{0:T(128)S(1)} %pad_add_fusion.1.ids_ref, s32[544]{0:T(1024)S(1)} %pad_add_fusion.table_ref, bf16[1,32,16,128,128]{4,3,2,1,0:T(8,128)(2,1)} %tiles_ref.3), custom_call_target="tpu_custom_call" | custom-call | tf_op jit(solution)/shard_map/pallas_call | solution.py:178
  48.1 1.7 %shard_map.158 = (f32[256,128]{1,0:T(8,128)S(1)}, bf16[320,256]{1,0:T(8,128)(2,1)S(1)}, bf16[320,256]{1,0:T(8,128)(2,1)S(1)}) custom-call(s32[2]{0:T(128)S(1)} %pad_add_fusion.1.ids_ref, bf16[544,128]{1,0:T(8,128)(2,1)S(1)} %pad_maximum_fusion.refs_0_, bf16[2176,128]{1,0:T(8,128)(2,1)S(1)} %shard_map.155.refs_1_, ...), custom_call_target="tpu_custom_call" | custom-call | tf_op jit(solution)/shard_map/pallas_call | solution.py:96
  49.8 1.6 %shard_map.159 = (bf16[256,128]{1,0:T(8,128)(2,1)S(1)}, bf16[256,256]{1,0:T(8,128)(2,1)S(1)}, bf16[256,256]{1,0:T(8,128)(2,1)S(1)}) custom-call(s32[2]{0:T(128)S(1)} %pad_add_fusion.1.ids_ref, bf16[2176,128]{1,0:T(8,128)(2,1)S(1)} %collective-permute-done.6.refs_0_, bf16[2176,128]{1,0:T(8,128)(2,1)S(1)} %collective-permute-done.7.refs_1_, ...), custom_call_target="tpu_custom_call" | custom-call | tf_op jit(solution)/shard_map/pallas_call | solution.py:96
  51.4 0.1 collective-permute-start.10
  51.6 5.7 %collective-permute-done.10.theirs_ref = bf16[256,128]{1,0:T(8,128)(2,1)S(1)} collective-permute-done((bf16[256,128]{1,0:T(8,128)(2,1)S(1)}, bf16[256,128]{1,0:T(8,128)(2,1)S(1)}, u32[]{:S(2)}, u32[]{:S(2)}) %collective-permute-start.10) | collective-permute-done | bytes 65568 | tf_op jit(solution)/shard_map/ppermute | solution.py:56
  57.3 1.5 %shard_map.160 = (bf16[256,128]{1,0:T(8,128)(2,1)}, bf16[128,256]{1,0:T(8,128)(2,1)S(1)}, f32[128,256]{1,0:T(8,128)S(1)}, f32[2,72,128]{2,1,0:T(8,128)S(1)}, f32[2,72,128]{2,1,0:T(8,128)S(1)}) custom-call(s32[2]{0:T(128)S(1)} %pad_add_fusion.1.ids_ref, bf16[256,128]{1,0:T(8,128)(2,1)S(1)} %get-tuple-element.35.mine_ref, ...), custom_call_target="tpu_custom_call" | custom-call | tf_op jit(solution)/shard_map/pallas_call | solution.py:96
  58.8 1.2 %shard_map.163 = bf16[4,128,512]{2,1,0:T(8,128)(2,1)S(1)} custom-call(s32[2]{0:T(128)S(1)} %pad_add_fusion.1.ids_ref, bf16[128,256]{1,0:T(8,128)(2,1)S(1)} %get-tuple-element.38.grad_ref, bf16[16,256,256]{2,1,0:T(8,128)(2,1)S(1)} %shard_map.156.refs_2_.mats_ref, bf16[256,256]{1,0:T(8,128)(2,1)S(1)} %get-tuple-element.41.hot_ref, ...), custom_call_target="tpu_custom_call" | custom-call | tf_op jit(solution)/shard_map/pallas_call | solution.py:96
  59.9 0.1 collective-permute-start.13
  60.0 0.5 collective-permute-start.15
  60.5 1.3 %shard_map.161 = bf16[5,128,512]{2,1,0:T(8,128)(2,1)S(1)} custom-call(s32[2]{0:T(128)S(1)} %pad_add_fusion.1.ids_ref, bf16[128,256]{1,0:T(8,128)(2,1)S(1)} %get-tuple-element.38.grad_ref, bf16[20,256,256]{2,1,0:T(8,128)(2,1)S(1)} %shard_map.157.refs_4_.mats_ref, bf16[320,256]{1,0:T(8,128)(2,1)S(1)} %get-tuple-element.39.hot_ref, ...), custom_call_target="tpu_custom_call" | custom-call | tf_op jit(solution)/shard_map/pallas_call | solution.py:96
  61.8 0.2 collective-permute-start.12
  62.0 7.2 %collective-permute-start.16 = (f32[72,128]{1,0:T(8,128)S(1)}, f32[72,128]{1,0:T(8,128)S(1)}, u32[]{:S(2)}, u32[]{:S(2)}) collective-permute-start(f32[72,128]{1,0:T(8,128)S(1)} %slice_bitcast_fusion), channel_id=1, source_target_pairs={{4,0},{5,1},{6,2},{7,3},{0,4},{1,5},{2,6},{3,7},{12,8},{13,9},{14,... | collective-permute-start | bytes 110600 | tf_op jit(solution)/shard_map/ppermute | solution.py:56
  69.2 1.2 %shard_map.164 = bf16[4,128,512]{2,1,0:T(8,128)(2,1)S(1)} custom-call(s32[2]{0:T(128)S(1)} %pad_add_fusion.1.ids_ref, bf16[128,256]{1,0:T(8,128)(2,1)S(1)} %get-tuple-element.38.grad_ref, bf16[16,256,256]{2,1,0:T(8,128)(2,1)S(1)} %shard_map.156.refs_2_.mats_ref, bf16[256,256]{1,0:T(8,128)(2,1)S(1)} %get-tuple-element.41.hot_ref, ...), custom_call_target="tpu_custom_call" | custom-call | tf_op jit(solution)/shard_map/pallas_call | solution.py:96
  70.4 1.5 %collective-permute-start.14 = (bf16[4,128,512]{2,1,0:T(8,128)(2,1)S(1)}, bf16[4,128,512]{2,1,0:T(8,128)(2,1)S(1)}, u32[]{:S(2)}, u32[]{:S(2)}) collective-permute-start(bf16[4,128,512]{2,1,0:T(8,128)(2,1)S(1)} %shard_map.164), channel_id=1, source_target_pairs={{0,96},{1,33},{2,98},{3,35},{4,100},{5,37},{6,102},{7,39},{8,104},... | collective-permute-start | bytes 1572872 | tf_op jit(solution)/shard_map/ppermute | solution.py:56
  72.0 0.6 collective-permute-start.17
  72.6 3.5 %collective-permute-start.19 = (f32[72,128]{1,0:T(8,128)S(1)}, f32[72,128]{1,0:T(8,128)S(1)}, u32[]{:S(2)}, u32[]{:S(2)}) collective-permute-start(f32[72,128]{1,0:T(8,128)S(1)} %fusion), channel_id=1, source_target_pairs={{16,0},{17,1},{18,2},{19,3},{20,4},{21,5},{22,6},{23,7},{24,8},{25... | collective-permute-start | bytes 110600 | tf_op jit(solution)/shard_map/ppermute | solution.py:56
  76.1 1.6 %collective-permute-done.18 = f32[72,128]{1,0:T(8,128)S(1)} collective-permute-done((f32[72,128]{1,0:T(8,128)S(1)}, f32[72,128]{1,0:T(8,128)S(1)}, u32[]{:S(2)}, u32[]{:S(2)}) %collective-permute-start.18) | collective-permute-done | bytes 36896 | tf_op jit(solution)/shard_map/ppermute | solution.py:56
  77.8 0.4 collective-permute-done.19
  78.2 0.6 collective-permute-start.27
  78.7 0.2 collective-permute-start.28
  78.9 3.4 %collective-permute-start.29 = (f32[72,128]{1,0:T(8,128)S(1)}, f32[72,128]{1,0:T(8,128)S(1)}, u32[]{:S(2)}, u32[]{:S(2)}) collective-permute-start(f32[72,128]{1,0:T(8,128)S(1)} %add_add_fusion.1), channel_id=1, source_target_pairs={{64,0},{65,1},{66,2},{67,3},{68,4},{69,5},{70,6},{71,7},{72,8},{73... | collective-permute-start | bytes 110600 | tf_op jit(solution)/shard_map/ppermute | solution.py:56
  82.3 1.3 %shard_map.162.keep_ref = f32[5,128,512]{2,1,0:T(8,128)S(1)} custom-call(s32[2]{0:T(128)S(1)} %pad_add_fusion.1.ids_ref, bf16[128,256]{1,0:T(8,128)(2,1)S(1)} %get-tuple-element.38.grad_ref, bf16[20,256,256]{2,1,0:T(8,128)(2,1)S(1)} %shard_map.157.refs_4_.mats_ref, bf16[320,256]{1,0:T(8,128)(2,1)S(1)} %get-tuple-element.39.hot_ref, ...), custom_call_target="tpu_custom_call" | custom-call | tf_op jit(solution)/shard_map/pallas_call | solution.py:96
  83.6 1.4 %collective-permute-done.14.far_ref = bf16[4,128,512]{2,1,0:T(8,128)(2,1)S(1)} collective-permute-done((bf16[4,128,512]{2,1,0:T(8,128)(2,1)S(1)}, bf16[4,128,512]{2,1,0:T(8,128)(2,1)S(1)}, u32[]{:S(2)}, u32[]{:S(2)}) %collective-permute-start.14) | collective-permute-done | bytes 524320 | tf_op jit(solution)/shard_map/ppermute | solution.py:56
  85.0 0.6 shard_map.165
  85.6 1.9 %collective-permute-start.20 = (bf16[128,512]{1,0:T(8,128)(2,1)S(1)}, bf16[128,512]{1,0:T(8,128)(2,1)S(1)}, u32[]{:S(2)}, u32[]{:S(2)}) collective-permute-start(bf16[128,512]{1,0:T(8,128)(2,1)S(1)} %get-tuple-element.46), channel_id=1, source_target_pairs={{0,120},{1,9},{2,122},{3,11},{4,124},{5,13},{6,126},{7,15},{8,0},{... | collective-permute-start | bytes 393224 | tf_op jit(solution)/shard_map/ppermute | solution.py:56
  87.5 2.9 %collective-permute-start.21 = (bf16[128,512]{1,0:T(8,128)(2,1)S(1)}, bf16[128,512]{1,0:T(8,128)(2,1)S(1)}, u32[]{:S(2)}, u32[]{:S(2)}) collective-permute-start(bf16[128,512]{1,0:T(8,128)(2,1)S(1)} %get-tuple-element.47), channel_id=1, source_target_pairs={{0,112},{1,17},{2,114},{3,19},{4,116},{5,21},{6,118},{7,23},{8,120... | collective-permute-start | bytes 393224 | tf_op jit(solution)/shard_map/ppermute | solution.py:56
  90.4 0.9 collective-permute-start.23
  91.3 0.8 collective-permute-start.30
  92.1 2.2 %collective-permute-done.21.refs_1_ = bf16[128,512]{1,0:T(8,128)(2,1)S(1)} collective-permute-done((bf16[128,512]{1,0:T(8,128)(2,1)S(1)}, bf16[128,512]{1,0:T(8,128)(2,1)S(1)}, u32[]{:S(2)}, u32[]{:S(2)}) %collective-permute-start.21) | collective-permute-done | bytes 131104 | tf_op jit(solution)/shard_map/ppermute | solution.py:56
  94.3 2.7 %collective-permute-done.22.refs_2_ = bf16[128,512]{1,0:T(8,128)(2,1)S(1)} collective-permute-done((bf16[128,512]{1,0:T(8,128)(2,1)S(1)}, bf16[128,512]{1,0:T(8,128)(2,1)S(1)}, u32[]{:S(2)}, u32[]{:S(2)}) %collective-permute-start.22) | collective-permute-done | bytes 131104 | tf_op jit(solution)/shard_map/ppermute | solution.py:56
  97.0 1.4 %collective-permute-done.23.refs_3_ = bf16[128,512]{1,0:T(8,128)(2,1)S(1)} collective-permute-done((bf16[128,512]{1,0:T(8,128)(2,1)S(1)}, bf16[128,512]{1,0:T(8,128)(2,1)S(1)}, u32[]{:S(2)}, u32[]{:S(2)}) %collective-permute-start.23) | collective-permute-done | bytes 131104 | tf_op jit(solution)/shard_map/ppermute | solution.py:56
  98.4 0.6 shard_map.166
  99.1 0.1 collective-permute-start.24
  99.1 0.9 collective-permute-start.25
  100.1 2.6 %collective-permute-start.26 = (bf16[128,256]{1,0:T(8,128)(2,1)S(1)}, bf16[128,256]{1,0:T(8,128)(2,1)S(1)}, u32[]{:S(2)}, u32[]{:S(2)}) collective-permute-start(bf16[128,256]{1,0:T(8,128)(2,1)S(1)} %get-tuple-element.51), channel_id=1, source_target_pairs={{4,0},{5,1},{6,2},{7,3},{1,4},{0,5},{3,6},{2,7},{12,8},{13,9},{14,... | collective-permute-start | bytes 196616 | tf_op jit(solution)/shard_map/ppermute | solution.py:56
  102.7 0.5 collective-permute-start.32
  103.2 0.7 collective-permute-done.31.refs_7_
  103.9 0.2 collective-permute-done.32.refs_8_
  104.0 1.0 collective-permute-done.24.refs_1_
  105.0 0.6 collective-permute-done.25.refs_2_
  105.6 1.3 %shard_map.167 = (bf16[256,128]{1,0:T(8,128)(2,1)}, f32[128,128]{1,0:T(8,128)}, f32[128,128]{1,0:T(8,128)}, f32[1,128]{1,0:T(1,128)}) custom-call(s32[2]{0:T(128)S(1)} %pad_add_fusion.1.ids_ref, bf16[128,256]{1,0:T(8,128)(2,1)S(1)} %get-tuple-element.50.refs_0_, bf16[128,256]{1,0:T(8,128)(2,1)S(1)} %collective-permute-done.24.refs_1_, ...), custom_call_target="tpu_custom_call" | custom-call | tf_op jit(solution)/shard_map/pallas_call | solution.py:96
  (43 shorter events, 0.5 us)
Async XLA Ops:
  1.3 6.5 %collective-permute-start.1 = (bf16[16,128]{1,0:T(8,128)(2,1)S(1)}, bf16[16,128]{1,0:T(8,128)(2,1)S(1)}, u32[]{:S(2)}, u32[]{:S(2)}) collective-permute-start(bf16[16,128]{1,0:T(8,128)(2,1)S(1)} %pad.8), channel_id=1, source_target_pairs={{5,0},{4,1},{6,2},{7,3},{0,4},{1,5},{3,6},{2,7},{13,8},{12,9},{14,... | collective-permute-start | bytes 12296 | tf_op jit(solution)/shard_map/ppermute | solution.py:56
  3.1 5.7 %collective-permute-start = (bf16[256,128]{1,0:T(8,128)(2,1)}, bf16[256,128]{1,0:T(8,128)(2,1)S(1)}, u32[]{:S(2)}, u32[]{:S(2)}) collective-permute-start(bf16[256,128]{1,0:T(8,128)(2,1)} %feat_ref.1), channel_id=1, source_target_pairs={{5,0},{4,1},{6,2},{7,3},{0,4},{1,5},{3,6},{2,7},{13,8},{12,9},{14,... | collective-permute-start | bytes 196616 | tf_op jit(solution)/shard_map/ppermute | solution.py:56
  9.6 11.3 %collective-permute-start.2 = (bf16[544,128]{1,0:T(8,128)(2,1)S(1)}, bf16[544,128]{1,0:T(8,128)(2,1)S(1)}, u32[]{:S(2)}, u32[]{:S(2)}) collective-permute-start(bf16[544,128]{1,0:T(8,128)(2,1)S(1)} %pad_maximum_fusion.refs_0_), channel_id=1, source_target_pairs={{120,0},{9,1},{122,2},{11,3},{124,4},{13,5},{126,6},{15,7},{0,8},{... | collective-permute-start | bytes 417800 | tf_op jit(solution)/shard_map/ppermute | solution.py:56
  11.6 10.3 %collective-permute-start.3 = (bf16[544,128]{1,0:T(8,128)(2,1)S(1)}, bf16[544,128]{1,0:T(8,128)(2,1)S(1)}, u32[]{:S(2)}, u32[]{:S(2)}) collective-permute-start(bf16[544,128]{1,0:T(8,128)(2,1)S(1)} %pad_maximum_fusion.refs_0_), channel_id=1, source_target_pairs={{112,0},{17,1},{114,2},{19,3},{116,4},{21,5},{118,6},{23,7},{120,8... | collective-permute-start | bytes 417800 | tf_op jit(solution)/shard_map/ppermute | solution.py:56
  15.2 7.5 %collective-permute-start.4 = (bf16[544,128]{1,0:T(8,128)(2,1)S(1)}, bf16[544,128]{1,0:T(8,128)(2,1)S(1)}, u32[]{:S(2)}, u32[]{:S(2)}) collective-permute-start(bf16[544,128]{1,0:T(8,128)(2,1)S(1)} %pad_maximum_fusion.refs_0_), channel_id=1, source_target_pairs={{104,0},{25,1},{106,2},{27,3},{108,4},{29,5},{110,6},{31,7},{112,8... | collective-permute-start | bytes 417800 | tf_op jit(solution)/shard_map/ppermute | solution.py:56
  17.1 6.3 %collective-permute-start.5 = (bf16[544,128]{1,0:T(8,128)(2,1)S(1)}, bf16[544,128]{1,0:T(8,128)(2,1)S(1)}, u32[]{:S(2)}, u32[]{:S(2)}) collective-permute-start(bf16[544,128]{1,0:T(8,128)(2,1)S(1)} %pad_maximum_fusion.refs_0_), channel_id=1, source_target_pairs={{96,0},{33,1},{98,2},{35,3},{100,4},{37,5},{102,6},{39,7},{104,8},... | collective-permute-start | bytes 417800 | tf_op jit(solution)/shard_map/ppermute | solution.py:56
  24.0 13.0 %collective-permute-start.6 = (bf16[2176,128]{1,0:T(8,128)(2,1)S(1)}, bf16[2176,128]{1,0:T(8,128)(2,1)S(1)}, u32[]{:S(2)}, u32[]{:S(2)}) collective-permute-start(bf16[2176,128]{1,0:T(8,128)(2,1)S(1)} %shard_map.155.refs_1_), channel_id=1, source_target_pairs={{96,0},{33,1},{98,2},{35,3},{100,4},{37,5},{102,6},{39,7},{104,8},... | collective-permute-start | bytes 1671176 | tf_op jit(solution)/shard_map/ppermute | solution.py:56
  24.3 23.7 %collective-permute-start.9 = (bf16[2176,128]{1,0:T(8,128)(2,1)S(1)}, bf16[2176,128]{1,0:T(8,128)(2,1)S(1)}, u32[]{:S(2)}, u32[]{:S(2)}) collective-permute-start(bf16[2176,128]{1,0:T(8,128)(2,1)S(1)} %shard_map.155.refs_1_), channel_id=1, source_target_pairs={{2,0},{3,1},{0,2},{1,3},{6,4},{7,5},{4,6},{5,7},{10,8},{11,9},{8,1... | collective-permute-start | bytes 1671176 | tf_op jit(solution)/shard_map/ppermute | solution.py:56
  37.0 12.7 %collective-permute-start.7 = (bf16[2176,128]{1,0:T(8,128)(2,1)S(1)}, bf16[2176,128]{1,0:T(8,128)(2,1)S(1)}, u32[]{:S(2)}, u32[]{:S(2)}) collective-permute-start(bf16[2176,128]{1,0:T(8,128)(2,1)S(1)} %collective-permute-done.6.refs_0_), channel_id=1, source_target_pairs={{2,0},{3,1},{0,2},{1,3},{6,4},{7,5},{4,6},{5,7},{10,8},{11,9},{8,1... | collective-permute-start | bytes 1671176 | tf_op jit(solution)/shard_map/ppermute | solution.py:56
  37.0 11.0 %collective-permute-start.8 = (bf16[544,128]{1,0:T(8,128)(2,1)S(1)}, bf16[544,128]{1,0:T(8,128)(2,1)S(1)}, u32[]{:S(2)}, u32[]{:S(2)}) collective-permute-start(bf16[544,128]{1,0:T(8,128)(2,1)S(1)} %pad_maximum_fusion.refs_0_), channel_id=1, source_target_pairs={{2,0},{3,1},{0,2},{1,3},{6,4},{7,5},{4,6},{5,7},{10,8},{11,9},{8,1... | collective-permute-start | bytes 417800 | tf_op jit(solution)/shard_map/ppermute | solution.py:56
  37.6 14.0 %collective-permute-start.11 = (bf16[528,128]{1,0:T(8,128)(2,1)S(1)}, bf16[528,128]{1,0:T(8,128)(2,1)S(1)}, u32[]{:S(2)}, u32[]{:S(2)}) collective-permute-start(bf16[528,128]{1,0:T(8,128)(2,1)S(1)} %pad_maximum_fusion.1), channel_id=1, source_target_pairs={{1,0},{0,1},{3,2},{2,3},{5,4},{4,5},{7,6},{6,7},{9,8},{8,9},{11,10... | collective-permute-start | bytes 405512 | tf_op jit(solution)/shard_map/ppermute | solution.py:56
  44.7 3.3 %copy-start = (bf16[64,16,256]{2,1,0:T(8,128)(2,1)S(1)}, bf16[64,16,256]{2,1,0:T(8,128)(2,1)}, u32[]{:S(2)}) copy-start(bf16[64,16,256]{2,1,0:T(8,128)(2,1)} %refs_3_.1) | copy-start | bytes 1572868
  49.7 7.5 %copy-start.1 = (bf16[256,128]{1,0:T(8,128)(2,1)S(1)}, bf16[256,128]{1,0:T(8,128)(2,1)}, u32[]{:S(2)}) copy-start(bf16[256,128]{1,0:T(8,128)(2,1)} %feat_ref.1) | copy-start | bytes 196612
  49.7 7.5 %copy-start.2 = (bf16[256,128]{1,0:T(8,128)(2,1)S(1)}, bf16[256,128]{1,0:T(8,128)(2,1)}, u32[]{:S(2)}) copy-start(bf16[256,128]{1,0:T(8,128)(2,1)} %ct_ref.1) | copy-start | bytes 196612
  49.8 7.5 %copy-start.3 = (bf16[128,128]{1,0:T(8,128)(2,1)S(1)}, bf16[128,128]{1,0:T(8,128)(2,1)}, u32[]{:S(2)}) copy-start(bf16[128,128]{1,0:T(8,128)(2,1)} %sw_ref.1) | copy-start | bytes 98308
  49.8 7.5 %copy-start.4 = (bf16[128,128]{1,0:T(8,128)(2,1)S(1)}, bf16[128,128]{1,0:T(8,128)(2,1)}, u32[]{:S(2)}) copy-start(bf16[128,128]{1,0:T(8,128)(2,1)} %nw_ref.1) | copy-start | bytes 98308
  49.8 7.5 %copy-start.5 = (f32[128]{0:T(128)S(1)}, f32[128]{0:T(128)}, u32[]{:S(2)}) copy-start(f32[128]{0:T(128)} %param.22) | copy-start | bytes 1540
  51.4 5.8 %collective-permute-start.10 = (bf16[256,128]{1,0:T(8,128)(2,1)S(1)}, bf16[256,128]{1,0:T(8,128)(2,1)S(1)}, u32[]{:S(2)}, u32[]{:S(2)}) collective-permute-start(bf16[256,128]{1,0:T(8,128)(2,1)S(1)} %get-tuple-element.35.mine_ref), channel_id=1, source_target_pairs={{1,0},{0,1},{3,2},{2,3},{5,4},{4,5},{7,6},{6,7},{9,8},{8,9},{11,10... | collective-permute-start | bytes 196616 | tf_op jit(solution)/shard_map/ppermute | solution.py:56
  59.9 9.3 %collective-permute-start.13 = (bf16[4,128,512]{2,1,0:T(8,128)(2,1)S(1)}, bf16[4,128,512]{2,1,0:T(8,128)(2,1)S(1)}, u32[]{:S(2)}, u32[]{:S(2)}) collective-permute-start(bf16[4,128,512]{2,1,0:T(8,128)(2,1)S(1)} %shard_map.163), channel_id=1, source_target_pairs={{2,0},{3,1},{0,2},{1,3},{6,4},{7,5},{4,6},{5,7},{10,8},{11,9},{8,1... | collective-permute-start | bytes 1572872 | tf_op jit(solution)/shard_map/ppermute | solution.py:56
  60.0 2.0 %collective-permute-start.15 = (f32[2,72,128]{2,1,0:T(8,128)S(1)}, f32[2,72,128]{2,1,0:T(8,128)S(1)}, u32[]{:S(2)}, u32[]{:S(2)}) collective-permute-start(f32[2,72,128]{2,1,0:T(8,128)S(1)} %get-tuple-element.44), channel_id=1, source_target_pairs={{2,0},{3,1},{0,2},{1,3},{6,4},{7,5},{4,6},{5,7},{10,8},{11,9},{8,1... | collective-permute-start | bytes 221192 | tf_op jit(solution)/shard_map/ppermute | solution.py:56
  61.8 20.6 %collective-permute-start.12 = (bf16[5,128,512]{2,1,0:T(8,128)(2,1)S(1)}, bf16[5,128,512]{2,1,0:T(8,128)(2,1)S(1)}, u32[]{:S(2)}, u32[]{:S(2)}) collective-permute-start(bf16[5,128,512]{2,1,0:T(8,128)(2,1)S(1)} %shard_map.161), channel_id=1, source_target_pairs={{2,0},{3,1},{0,2},{1,3},{6,4},{7,5},{4,6},{5,7},{10,8},{11,9},{8,1... | collective-permute-start | bytes 1966088 | tf_op jit(solution)/shard_map/ppermute | solution.py:56
  62.0 9.9 %collective-permute-start.16 = (f32[72,128]{1,0:T(8,128)S(1)}, f32[72,128]{1,0:T(8,128)S(1)}, u32[]{:S(2)}, u32[]{:S(2)}) collective-permute-start(f32[72,128]{1,0:T(8,128)S(1)} %slice_bitcast_fusion), channel_id=1, source_target_pairs={{4,0},{5,1},{6,2},{7,3},{0,4},{1,5},{2,6},{3,7},{12,8},{13,9},{14,... | collective-permute-start | bytes 110600 | tf_op jit(solution)/shard_map/ppermute | solution.py:56
  70.4 14.6 %collective-permute-start.14 = (bf16[4,128,512]{2,1,0:T(8,128)(2,1)S(1)}, bf16[4,128,512]{2,1,0:T(8,128)(2,1)S(1)}, u32[]{:S(2)}, u32[]{:S(2)}) collective-permute-start(bf16[4,128,512]{2,1,0:T(8,128)(2,1)S(1)} %shard_map.164), channel_id=1, source_target_pairs={{0,96},{1,33},{2,98},{3,35},{4,100},{5,37},{6,102},{7,39},{8,104},... | collective-permute-start | bytes 1572872 | tf_op jit(solution)/shard_map/ppermute | solution.py:56
  72.0 4.2 %collective-permute-start.17 = (f32[72,128]{1,0:T(8,128)S(1)}, f32[72,128]{1,0:T(8,128)S(1)}, u32[]{:S(2)}, u32[]{:S(2)}) collective-permute-start(f32[72,128]{1,0:T(8,128)S(1)} %fusion), channel_id=1, source_target_pairs={{8,0},{9,1},{10,2},{11,3},{12,4},{13,5},{14,6},{15,7},{0,8},{1,9},... | collective-permute-start | bytes 110600 | tf_op jit(solution)/shard_map/ppermute | solution.py:56
  72.6 5.2 %collective-permute-start.18 = (f32[72,128]{1,0:T(8,128)S(1)}, f32[72,128]{1,0:T(8,128)S(1)}, u32[]{:S(2)}, u32[]{:S(2)}) collective-permute-start(f32[72,128]{1,0:T(8,128)S(1)} %fusion), channel_id=1, source_target_pairs={{24,0},{25,1},{26,2},{27,3},{28,4},{29,5},{30,6},{31,7},{16,8},{17... | collective-permute-start | bytes 110600 | tf_op jit(solution)/shard_map/ppermute | solution.py:56
  72.6 5.6 %collective-permute-start.19 = (f32[72,128]{1,0:T(8,128)S(1)}, f32[72,128]{1,0:T(8,128)S(1)}, u32[]{:S(2)}, u32[]{:S(2)}) collective-permute-start(f32[72,128]{1,0:T(8,128)S(1)} %fusion), channel_id=1, source_target_pairs={{16,0},{17,1},{18,2},{19,3},{20,4},{21,5},{22,6},{23,7},{24,8},{25... | collective-permute-start | bytes 110600 | tf_op jit(solution)/shard_map/ppermute | solution.py:56
  78.2 12.2 %collective-permute-start.27 = (f32[72,128]{1,0:T(8,128)S(1)}, f32[72,128]{1,0:T(8,128)S(1)}, u32[]{:S(2)}, u32[]{:S(2)}) collective-permute-start(f32[72,128]{1,0:T(8,128)S(1)} %add_add_fusion.1), channel_id=1, source_target_pairs={{32,0},{33,1},{34,2},{35,3},{36,4},{37,5},{38,6},{39,7},{40,8},{41... | collective-permute-start | bytes 110600 | tf_op jit(solution)/shard_map/ppermute | solution.py:56
  78.7 11.7 %collective-permute-start.28 = (f32[72,128]{1,0:T(8,128)S(1)}, f32[72,128]{1,0:T(8,128)S(1)}, u32[]{:S(2)}, u32[]{:S(2)}) collective-permute-start(f32[72,128]{1,0:T(8,128)S(1)} %add_add_fusion.1), channel_id=1, source_target_pairs={{96,0},{97,1},{98,2},{99,3},{100,4},{101,5},{102,6},{103,7},{104,8... | collective-permute-start | bytes 110600 | tf_op jit(solution)/shard_map/ppermute | solution.py:56
  78.9 12.3 %collective-permute-start.29 = (f32[72,128]{1,0:T(8,128)S(1)}, f32[72,128]{1,0:T(8,128)S(1)}, u32[]{:S(2)}, u32[]{:S(2)}) collective-permute-start(f32[72,128]{1,0:T(8,128)S(1)} %add_add_fusion.1), channel_id=1, source_target_pairs={{64,0},{65,1},{66,2},{67,3},{68,4},{69,5},{70,6},{71,7},{72,8},{73... | collective-permute-start | bytes 110600 | tf_op jit(solution)/shard_map/ppermute | solution.py:56
  85.6 6.4 %collective-permute-start.20 = (bf16[128,512]{1,0:T(8,128)(2,1)S(1)}, bf16[128,512]{1,0:T(8,128)(2,1)S(1)}, u32[]{:S(2)}, u32[]{:S(2)}) collective-permute-start(bf16[128,512]{1,0:T(8,128)(2,1)S(1)} %get-tuple-element.46), channel_id=1, source_target_pairs={{0,120},{1,9},{2,122},{3,11},{4,124},{5,13},{6,126},{7,15},{8,0},{... | collective-permute-start | bytes 393224 | tf_op jit(solution)/shard_map/ppermute | solution.py:56
  87.5 6.8 %collective-permute-start.21 = (bf16[128,512]{1,0:T(8,128)(2,1)S(1)}, bf16[128,512]{1,0:T(8,128)(2,1)S(1)}, u32[]{:S(2)}, u32[]{:S(2)}) collective-permute-start(bf16[128,512]{1,0:T(8,128)(2,1)S(1)} %get-tuple-element.47), channel_id=1, source_target_pairs={{0,112},{1,17},{2,114},{3,19},{4,116},{5,21},{6,118},{7,23},{8,120... | collective-permute-start | bytes 393224 | tf_op jit(solution)/shard_map/ppermute | solution.py:56
  90.4 6.6 %collective-permute-start.22 = (bf16[128,512]{1,0:T(8,128)(2,1)S(1)}, bf16[128,512]{1,0:T(8,128)(2,1)S(1)}, u32[]{:S(2)}, u32[]{:S(2)}) collective-permute-start(bf16[128,512]{1,0:T(8,128)(2,1)S(1)} %get-tuple-element.48), channel_id=1, source_target_pairs={{0,104},{1,25},{2,106},{3,27},{4,108},{5,29},{6,110},{7,31},{8,112... | collective-permute-start | bytes 393224 | tf_op jit(solution)/shard_map/ppermute | solution.py:56
  90.4 8.0 %collective-permute-start.23 = (bf16[128,512]{1,0:T(8,128)(2,1)S(1)}, bf16[128,512]{1,0:T(8,128)(2,1)S(1)}, u32[]{:S(2)}, u32[]{:S(2)}) collective-permute-start(bf16[128,512]{1,0:T(8,128)(2,1)S(1)} %get-tuple-element.49), channel_id=1, source_target_pairs={{0,96},{1,33},{2,98},{3,35},{4,100},{5,37},{6,102},{7,39},{8,104},... | collective-permute-start | bytes 393224 | tf_op jit(solution)/shard_map/ppermute | solution.py:56
  91.3 11.4 %collective-permute-start.30 = (f32[72,128]{1,0:T(8,128)S(1)}, f32[72,128]{1,0:T(8,128)S(1)}, u32[]{:S(2)}, u32[]{:S(2)}) collective-permute-start(f32[72,128]{1,0:T(8,128)S(1)} %add_add_fusion.refs_5_), channel_id=1, source_target_pairs={{4,0},{5,1},{6,2},{7,3},{0,4},{1,5},{2,6},{3,7},{12,8},{13,9},{14,... | collective-permute-start | bytes 110600 | tf_op jit(solution)/shard_map/ppermute | solution.py:56
  99.1 6.0 %collective-permute-start.24 = (bf16[128,256]{1,0:T(8,128)(2,1)S(1)}, bf16[128,256]{1,0:T(8,128)(2,1)S(1)}, u32[]{:S(2)}, u32[]{:S(2)}) collective-permute-start(bf16[128,256]{1,0:T(8,128)(2,1)S(1)} %get-tuple-element.50.refs_0_), channel_id=1, source_target_pairs={{1,0},{0,1},{3,2},{2,3},{5,4},{4,5},{7,6},{6,7},{9,8},{8,9},{11,10... | collective-permute-start | bytes 196616 | tf_op jit(solution)/shard_map/ppermute | solution.py:56
  99.1 6.5 %collective-permute-start.25 = (bf16[128,256]{1,0:T(8,128)(2,1)S(1)}, bf16[128,256]{1,0:T(8,128)(2,1)S(1)}, u32[]{:S(2)}, u32[]{:S(2)}) collective-permute-start(bf16[128,256]{1,0:T(8,128)(2,1)S(1)} %get-tuple-element.51), channel_id=1, source_target_pairs={{5,0},{4,1},{7,2},{6,3},{0,4},{1,5},{2,6},{3,7},{13,8},{12,9},{15,... | collective-permute-start | bytes 196616 | tf_op jit(solution)/shard_map/ppermute | solution.py:56
  100.1 5.5 %collective-permute-start.26 = (bf16[128,256]{1,0:T(8,128)(2,1)S(1)}, bf16[128,256]{1,0:T(8,128)(2,1)S(1)}, u32[]{:S(2)}, u32[]{:S(2)}) collective-permute-start(bf16[128,256]{1,0:T(8,128)(2,1)S(1)} %get-tuple-element.51), channel_id=1, source_target_pairs={{4,0},{5,1},{6,2},{7,3},{1,4},{0,5},{3,6},{2,7},{12,8},{13,9},{14,... | collective-permute-start | bytes 196616 | tf_op jit(solution)/shard_map/ppermute | solution.py:56
  102.7 1.2 %collective-permute-start.31 = (f32[72,128]{1,0:T(8,128)S(1)}, f32[72,128]{1,0:T(8,128)S(1)}, u32[]{:S(2)}, u32[]{:S(2)}) collective-permute-start(f32[72,128]{1,0:T(8,128)S(1)} %add_add_fusion.refs_5_), channel_id=1, source_target_pairs={{2,0},{3,1},{0,2},{1,3},{6,4},{7,5},{4,6},{5,7},{10,8},{11,9},{8,1... | collective-permute-start | bytes 110600 | tf_op jit(solution)/shard_map/ppermute | solution.py:56
  102.7 1.4 %collective-permute-start.32 = (f32[72,128]{1,0:T(8,128)S(1)}, f32[72,128]{1,0:T(8,128)S(1)}, u32[]{:S(2)}, u32[]{:S(2)}) collective-permute-start(f32[72,128]{1,0:T(8,128)S(1)} %collective-permute-done.30.refs_6_), channel_id=1, source_target_pairs={{2,0},{3,1},{0,2},{1,3},{6,4},{7,5},{4,6},{5,7},{10,8},{11,9},{8,1... | collective-permute-start | bytes 110600 | tf_op jit(solution)/shard_map/ppermute | solution.py:56

commit v3 on v2

--- a/solution.py
+++ b/solution.py
@@ -190,12 +190,13 @@
 
 
 def join_kernel(ids_ref, *refs):
-    for i, ref in enumerate(refs[:-1]):
-        refs[-1][i * GROUP : (i + 1) * GROUP, :] = ref[...]
+    for i, ref in enumerate(refs[:4]):
+        for out in refs[4:] if i < 3 else refs[4:5]:
+            out[i * GROUP : (i + 1) * GROUP, :] = ref[...]
 
 
 def forward_kernel(columns, first, ids_ref, *refs):
-    groups, (mats_ref, hub_ref), refs = refs[: 4 if first else 2], refs[4 if first else 2 :][:2], refs[6 if first else 4 :]
+    groups, (mats_ref, hub_ref), refs = refs[:4], refs[4:6], refs[6:]
     before_ref, (out_ref, hot_ref, wts_ref, pick_ref) = (None, refs) if first else (refs[0], refs[1:])
     lane = lax.broadcasted_iota(jnp.int32, (2 * HEAD, 128), 1)
     column = lax.broadcasted_iota(jnp.int32, (2 * HEAD, 256), 1)
@@ -205,7 +206,7 @@
             if first:
                 ref, base = groups[cls * 2 + min(k, 1)], max(k - 1, 0) * GROUP
             else:
-                ref, base = groups[cls], i * GROUP
+                ref, base = groups[cls * 2 + i // 3], i % 3 * GROUP
             head = ref[base + 512 : base + GROUP, :].astype(jnp.float32)
             mine = jnp.sum(jnp.where(lane == ids_ref[0], head, 0.0), axis=1, keepdims=True)
             hot = (mine.astype(jnp.int32) == column).astype(jnp.float32).astype(jnp.bfloat16)
@@ -384,17 +385,24 @@
     other = permute(packed, SWAP_R)
     cols = [permute(col0, FROM_COL[k]) for k in range(1, 5)]
     oth0 = permute(col0, SWAP_C)
-    cols = kernel_call(join_kernel, 4, ((4 * GROUP, 128), bf16))(ids, *cols)
-    far = permute(cols, FROM_COL[4])
+    turn = permute(col0, inverse(FROM_COL[4]))
+    cols, sent = kernel_call(
+        join_kernel, 4, [((4 * GROUP, 128), bf16), ((3 * GROUP, 128), bf16)]
+    )(ids, *cols)
+    far = permute(sent, FROM_COL[4])
+    last = permute(turn, inverse(FROM_COL[4]))
     oth1 = permute(cols, SWAP_C)
     mats_near = densify(NEAR, ids, table, tile_values)
     mats_far = densify(FAR, ids, table, tile_values)
     oth2 = permute(far, SWAP_C)
+    oth3 = permute(last, SWAP_C)
 
     partial, hot_near, wts_near = forward(
         NEAR, True, ids, col0, cols, oth0, oth1, mats_near, hub_weight
     )
-    partial, hot_far, wts_far = forward(FAR, False, ids, far, oth2, mats_far, hub_weight, partial)
+    partial, hot_far, wts_far = forward(
+        FAR, False, ids, far, last, oth2, oth3, mats_far, hub_weight, partial
+    )
     theirs = permute(partial, SWAP_R)
     output, grad, self_grad, parts, give_parts = middle(
         ids,

time: 108 us -> 113 us (1.046)
  the two profiles are of different devices: /device:TPU:0 before, /device:TPU:120 now
where the time goes in v3:
time: 113 us
  waiting for transfers between devices  46.4 us (41%)
  starting transfers between devices  41 us (36%)
  Pallas kernels  19.7 us (17%)
  other arithmetic  4.58 us (4%)
    ppermute x36, waiting for transfers between devices, permute(): return lax.ppermute(x, AXES, pairs)  46.4 us
    ppermute x36, starting transfers between devices, permute(): return lax.ppermute(x, AXES, pairs)  41 us
    pallas_call x11, Pallas kernels, call(): pl.pallas_call(body, in_specs=[smem()] + [vmem()] * n_in, out_specs=vmem(...  12.8 us
    pallas_call x2, Pallas kernels, densify(): pl.pallas_call(functools.partial(densify_kernel, columns), in_specs=[smem...  6.9 us
  transfers between devices with their start and end apart: 36, of which 19 were waited for; matrix products, arithmetic and copies ran while one was open for 3% of the time, Pallas kernels for 13%

profile of v3, /device:TPU:120, one launch (start us, length us, event | category | flops | bytes accessed | tf_op | source)
XLA Modules:
  0.0 112.9 jit_solution(15442875228075283375)
XLA Ops:
  0.6 0.7 fusion.5
  1.3 0.3 collective-permute-start.1
  1.6 1.6 %collective-permute-start = (bf16[256,128]{1,0:T(8,128)(2,1)}, bf16[256,128]{1,0:T(8,128)(2,1)S(1)}, u32[]{:S(2)}, u32[]{:S(2)}) collective-permute-start(bf16[256,128]{1,0:T(8,128)(2,1)} %feat_ref.1), channel_id=1, source_target_pairs={{5,0},{4,1},{6,2},{7,3},{0,4},{1,5},{3,6},{2,7},{13,8},{12,9},{14,... | collective-permute-start | bytes 196616 | tf_op jit(solution)/shard_map/ppermute | solution.py:56
  3.2 0.7 fusion.8
  3.9 0.7 multiply_add_fusion
  4.7 0.1 add.36
  4.8 0.7 pad_add_fusion.table_ref
  5.4 0.9 pad_maximum_fusion.1
  6.4 0.9 pad_maximum_fusion.refs_0_
  7.2 0.5 collective-permute-start.2
  7.7 0.3 collective-permute-start.3
  8.0 4.8 %collective-permute-start.4 = (bf16[544,128]{1,0:T(8,128)(2,1)S(1)}, bf16[544,128]{1,0:T(8,128)(2,1)S(1)}, u32[]{:S(2)}, u32[]{:S(2)}) collective-permute-start(bf16[544,128]{1,0:T(8,128)(2,1)S(1)} %pad_maximum_fusion.refs_0_), channel_id=1, source_target_pairs={{104,0},{25,1},{106,2},{27,3},{108,4},{29,5},{110,6},{31,7},{112,8... | collective-permute-start | bytes 417800 | tf_op jit(solution)/shard_map/ppermute | solution.py:56
  12.7 0.8 collective-permute-start.5
  13.6 4.3 %collective-permute-done.2.refs_0_ = bf16[544,128]{1,0:T(8,128)(2,1)S(1)} collective-permute-done((bf16[544,128]{1,0:T(8,128)(2,1)S(1)}, bf16[544,128]{1,0:T(8,128)(2,1)S(1)}, u32[]{:S(2)}, u32[]{:S(2)}) %collective-permute-start.2) | collective-permute-done | bytes 139296 | tf_op jit(solution)/shard_map/ppermute | solution.py:56
  17.8 0.6 collective-permute-done.4.refs_2_
  18.4 0.7 shard_map.155
  19.1 3.4 %collective-permute-start.6 = (bf16[1632,128]{1,0:T(8,128)(2,1)S(1)}, bf16[1632,128]{1,0:T(8,128)(2,1)S(1)}, u32[]{:S(2)}, u32[]{:S(2)}) collective-permute-start(bf16[1632,128]{1,0:T(8,128)(2,1)S(1)} %get-tuple-element.35), channel_id=1, source_target_pairs={{96,0},{33,1},{98,2},{35,3},{100,4},{37,5},{102,6},{39,7},{104,8},... | collective-permute-start | bytes 1253384 | tf_op jit(solution)/shard_map/ppermute | solution.py:56
  22.6 6.6 %collective-permute-done.6.refs_0_ = bf16[1632,128]{1,0:T(8,128)(2,1)S(1)} collective-permute-done((bf16[1632,128]{1,0:T(8,128)(2,1)S(1)}, bf16[1632,128]{1,0:T(8,128)(2,1)S(1)}, u32[]{:S(2)}, u32[]{:S(2)}) %collective-permute-start.6) | collective-permute-done | bytes 417824 | tf_op jit(solution)/shard_map/ppermute | solution.py:56
  29.2 0.7 collective-permute-done.7
  29.9 7.4 %collective-permute-done.8.refs_1_ = bf16[544,128]{1,0:T(8,128)(2,1)S(1)} collective-permute-done((bf16[544,128]{1,0:T(8,128)(2,1)S(1)}, bf16[544,128]{1,0:T(8,128)(2,1)S(1)}, u32[]{:S(2)}, u32[]{:S(2)}) %collective-permute-start.8) | collective-permute-done | bytes 139296 | tf_op jit(solution)/shard_map/ppermute | solution.py:56
  37.2 6.7 %collective-permute-start.14 = (bf16[528,128]{1,0:T(8,128)(2,1)S(1)}, bf16[528,128]{1,0:T(8,128)(2,1)S(1)}, u32[]{:S(2)}, u32[]{:S(2)}) collective-permute-start(bf16[528,128]{1,0:T(8,128)(2,1)S(1)} %pad_maximum_fusion.1), channel_id=1, source_target_pairs={{1,0},{0,1},{3,2},{2,3},{5,4},{4,5},{7,6},{6,7},{9,8},{8,9},{11,10... | collective-permute-start | bytes 405512 | tf_op jit(solution)/shard_map/ppermute | solution.py:56
  43.9 3.5 %shard_map.157.refs_4_.mats_ref = bf16[20,256,256]{2,1,0:T(8,128)(2,1)S(1)} custom-call(s32[2]{0:T(128)S(1)} %pad_add_fusion.1.ids_ref, s32[544]{0:T(1024)S(1)} %pad_add_fusion.table_ref, bf16[1,32,16,128,128]{4,3,2,1,0:T(8,128)(2,1)} %tiles_ref.3), custom_call_target="tpu_custom_call" | custom-call | tf_op jit(solution)/shard_map/pallas_call | solution.py:178
  47.5 3.4 %shard_map.156.refs_4_.mats_ref = bf16[16,256,256]{2,1,0:T(8,128)(2,1)S(1)} custom-call(s32[2]{0:T(128)S(1)} %pad_add_fusion.1.ids_ref, s32[544]{0:T(1024)S(1)} %pad_add_fusion.table_ref, bf16[1,32,16,128,128]{4,3,2,1,0:T(8,128)(2,1)} %tiles_ref.3), custom_call_target="tpu_custom_call" | custom-call | tf_op jit(solution)/shard_map/pallas_call | solution.py:178
  50.9 1.7 %shard_map.158 = (f32[256,128]{1,0:T(8,128)S(1)}, bf16[320,256]{1,0:T(8,128)(2,1)S(1)}, bf16[320,256]{1,0:T(8,128)(2,1)S(1)}) custom-call(s32[2]{0:T(128)S(1)} %pad_add_fusion.1.ids_ref, bf16[544,128]{1,0:T(8,128)(2,1)S(1)} %pad_maximum_fusion.refs_0_, bf16[2176,128]{1,0:T(8,128)(2,1)S(1)} %get-tuple-element.37.refs_1_, ...), custom_call_target="tpu_custom_call" | custom-call | tf_op jit(solution)/shard_map/pallas_call | solution.py:96
  52.7 1.6 %shard_map.159 = (bf16[256,128]{1,0:T(8,128)(2,1)S(1)}, bf16[256,256]{1,0:T(8,128)(2,1)S(1)}, bf16[256,256]{1,0:T(8,128)(2,1)S(1)}) custom-call(s32[2]{0:T(128)S(1)} %pad_add_fusion.1.ids_ref, bf16[1632,128]{1,0:T(8,128)(2,1)S(1)} %collective-permute-done.6.refs_0_, bf16[544,128]{1,0:T(8,128)(2,1)S(1)} %collective-permute-done.8.refs_1_, ...), custom_call_target="tpu_custom_call" | custom-call | tf_op jit(solution)/shard_map/pallas_call | solution.py:96
  54.3 0.6 collective-permute-start.13
  54.8 5.3 %collective-permute-done.13.theirs_ref = bf16[256,128]{1,0:T(8,128)(2,1)S(1)} collective-permute-done((bf16[256,128]{1,0:T(8,128)(2,1)S(1)}, bf16[256,128]{1,0:T(8,128)(2,1)S(1)}, u32[]{:S(2)}, u32[]{:S(2)}) %collective-permute-start.13) | collective-permute-done | bytes 65568 | tf_op jit(solution)/shard_map/ppermute | solution.py:56
  60.1 1.5 %shard_map.160 = (bf16[256,128]{1,0:T(8,128)(2,1)}, bf16[128,256]{1,0:T(8,128)(2,1)S(1)}, f32[128,256]{1,0:T(8,128)S(1)}, f32[2,72,128]{2,1,0:T(8,128)S(1)}, f32[2,72,128]{2,1,0:T(8,128)S(1)}) custom-call(s32[2]{0:T(128)S(1)} %pad_add_fusion.1.ids_ref, bf16[256,128]{1,0:T(8,128)(2,1)S(1)} %get-tuple-element.39.mine_ref, ...), custom_call_target="tpu_custom_call" | custom-call | tf_op jit(solution)/shard_map/pallas_call | solution.py:96
  61.6 1.2 %shard_map.163 = bf16[4,128,512]{2,1,0:T(8,128)(2,1)S(1)} custom-call(s32[2]{0:T(128)S(1)} %pad_add_fusion.1.ids_ref, bf16[128,256]{1,0:T(8,128)(2,1)S(1)} %get-tuple-element.42.grad_ref, bf16[16,256,256]{2,1,0:T(8,128)(2,1)S(1)} %shard_map.156.refs_4_.mats_ref, bf16[256,256]{1,0:T(8,128)(2,1)S(1)} %get-tuple-element.45.hot_ref, ...), custom_call_target="tpu_custom_call" | custom-call | tf_op jit(solution)/shard_map/pallas_call | solution.py:96
  62.8 0.1 collective-permute-start.16
  62.9 0.5 collective-permute-start.18
  63.4 1.3 %shard_map.161 = bf16[5,128,512]{2,1,0:T(8,128)(2,1)S(1)} custom-call(s32[2]{0:T(128)S(1)} %pad_add_fusion.1.ids_ref, bf16[128,256]{1,0:T(8,128)(2,1)S(1)} %get-tuple-element.42.grad_ref, bf16[20,256,256]{2,1,0:T(8,128)(2,1)S(1)} %shard_map.157.refs_4_.mats_ref, bf16[320,256]{1,0:T(8,128)(2,1)S(1)} %get-tuple-element.43.hot_ref, ...), custom_call_target="tpu_custom_call" | custom-call | tf_op jit(solution)/shard_map/pallas_call | solution.py:96
  64.6 0.2 collective-permute-start.15
  64.9 0.1 collective-permute-start.19
  65.0 1.2 %shard_map.164 = bf16[4,128,512]{2,1,0:T(8,128)(2,1)S(1)} custom-call(s32[2]{0:T(128)S(1)} %pad_add_fusion.1.ids_ref, bf16[128,256]{1,0:T(8,128)(2,1)S(1)} %get-tuple-element.42.grad_ref, bf16[16,256,256]{2,1,0:T(8,128)(2,1)S(1)} %shard_map.156.refs_4_.mats_ref, bf16[256,256]{1,0:T(8,128)(2,1)S(1)} %get-tuple-element.45.hot_ref, ...), custom_call_target="tpu_custom_call" | custom-call | tf_op jit(solution)/shard_map/pallas_call | solution.py:96
  66.3 2.7 %collective-permute-done.19 = f32[72,128]{1,0:T(8,128)S(1)} collective-permute-done((f32[72,128]{1,0:T(8,128)S(1)}, f32[72,128]{1,0:T(8,128)S(1)}, u32[]{:S(2)}, u32[]{:S(2)}) %collective-permute-start.19) | collective-permute-done | bytes 36896 | tf_op jit(solution)/shard_map/ppermute | solution.py:56
  69.0 1.3 %collective-permute-start.20 = (f32[72,128]{1,0:T(8,128)S(1)}, f32[72,128]{1,0:T(8,128)S(1)}, u32[]{:S(2)}, u32[]{:S(2)}) collective-permute-start(f32[72,128]{1,0:T(8,128)S(1)} %fusion), channel_id=1, source_target_pairs={{8,0},{9,1},{10,2},{11,3},{12,4},{13,5},{14,6},{15,7},{0,8},{1,9},... | collective-permute-start | bytes 110600 | tf_op jit(solution)/shard_map/ppermute | solution.py:56
  70.2 3.7 %collective-permute-start.21 = (f32[72,128]{1,0:T(8,128)S(1)}, f32[72,128]{1,0:T(8,128)S(1)}, u32[]{:S(2)}, u32[]{:S(2)}) collective-permute-start(f32[72,128]{1,0:T(8,128)S(1)} %fusion), channel_id=1, source_target_pairs={{24,0},{25,1},{26,2},{27,3},{28,4},{29,5},{30,6},{31,7},{16,8},{17... | collective-permute-start | bytes 110600 | tf_op jit(solution)/shard_map/ppermute | solution.py:56
  73.9 1.4 %collective-permute-start.22 = (f32[72,128]{1,0:T(8,128)S(1)}, f32[72,128]{1,0:T(8,128)S(1)}, u32[]{:S(2)}, u32[]{:S(2)}) collective-permute-start(f32[72,128]{1,0:T(8,128)S(1)} %fusion), channel_id=1, source_target_pairs={{16,0},{17,1},{18,2},{19,3},{20,4},{21,5},{22,6},{23,7},{24,8},{25... | collective-permute-start | bytes 110600 | tf_op jit(solution)/shard_map/ppermute | solution.py:56
  75.3 0.6 collective-permute-done.21
  75.9 3.5 %collective-permute-done.22 = f32[72,128]{1,0:T(8,128)S(1)} collective-permute-done((f32[72,128]{1,0:T(8,128)S(1)}, f32[72,128]{1,0:T(8,128)S(1)}, u32[]{:S(2)}, u32[]{:S(2)}) %collective-permute-start.22) | collective-permute-done | bytes 36896 | tf_op jit(solution)/shard_map/ppermute | solution.py:56
  79.4 0.1 collective-permute-start.30
  79.5 0.7 collective-permute-start.31
  80.2 3.4 %collective-permute-start.32 = (f32[72,128]{1,0:T(8,128)S(1)}, f32[72,128]{1,0:T(8,128)S(1)}, u32[]{:S(2)}, u32[]{:S(2)}) collective-permute-start(f32[72,128]{1,0:T(8,128)S(1)} %add_add_fusion.1), channel_id=1, source_target_pairs={{64,0},{65,1},{66,2},{67,3},{68,4},{69,5},{70,6},{71,7},{72,8},{73... | collective-permute-start | bytes 110600 | tf_op jit(solution)/shard_map/ppermute | solution.py:56
  83.6 1.3 %shard_map.162.keep_ref = f32[5,128,512]{2,1,0:T(8,128)S(1)} custom-call(s32[2]{0:T(128)S(1)} %pad_add_fusion.1.ids_ref, bf16[128,256]{1,0:T(8,128)(2,1)S(1)} %get-tuple-element.42.grad_ref, bf16[20,256,256]{2,1,0:T(8,128)(2,1)S(1)} %shard_map.157.refs_4_.mats_ref, bf16[320,256]{1,0:T(8,128)(2,1)S(1)} %get-tuple-element.43.hot_ref, ...), custom_call_target="tpu_custom_call" | custom-call | tf_op jit(solution)/shard_map/pallas_call | solution.py:96
  84.9 0.6 shard_map.165
  85.5 0.6 collective-permute-start.23
  86.1 2.4 %collective-permute-start.24 = (bf16[128,512]{1,0:T(8,128)(2,1)S(1)}, bf16[128,512]{1,0:T(8,128)(2,1)S(1)}, u32[]{:S(2)}, u32[]{:S(2)}) collective-permute-start(bf16[128,512]{1,0:T(8,128)(2,1)S(1)} %get-tuple-element.51), channel_id=1, source_target_pairs={{0,112},{1,17},{2,114},{3,19},{4,116},{5,21},{6,118},{7,23},{8,120... | collective-permute-start | bytes 393224 | tf_op jit(solution)/shard_map/ppermute | solution.py:56
  88.5 0.8 collective-permute-start.26
  89.3 2.1 %collective-permute-start.33 = (f32[72,128]{1,0:T(8,128)S(1)}, f32[72,128]{1,0:T(8,128)S(1)}, u32[]{:S(2)}, u32[]{:S(2)}) collective-permute-start(f32[72,128]{1,0:T(8,128)S(1)} %add_add_fusion.refs_5_), channel_id=1, source_target_pairs={{4,0},{5,1},{6,2},{7,3},{0,4},{1,5},{2,6},{3,7},{12,8},{13,9},{14,... | collective-permute-start | bytes 110600 | tf_op jit(solution)/shard_map/ppermute | solution.py:56
  91.4 0.3 collective-permute-done.23.refs_0_
  91.7 1.1 collective-permute-done.24.refs_1_
  92.8 2.3 %collective-permute-done.25.refs_2_ = bf16[128,512]{1,0:T(8,128)(2,1)S(1)} collective-permute-done((bf16[128,512]{1,0:T(8,128)(2,1)S(1)}, bf16[128,512]{1,0:T(8,128)(2,1)S(1)}, u32[]{:S(2)}, u32[]{:S(2)}) %collective-permute-start.25) | collective-permute-done | bytes 131104 | tf_op jit(solution)/shard_map/ppermute | solution.py:56
  95.1 6.1 %collective-permute-done.26.refs_3_ = bf16[128,512]{1,0:T(8,128)(2,1)S(1)} collective-permute-done((bf16[128,512]{1,0:T(8,128)(2,1)S(1)}, bf16[128,512]{1,0:T(8,128)(2,1)S(1)}, u32[]{:S(2)}, u32[]{:S(2)}) %collective-permute-start.26) | collective-permute-done | bytes 131104 | tf_op jit(solution)/shard_map/ppermute | solution.py:56
  101.2 0.6 shard_map.166
  101.8 0.1 collective-permute-start.27
  101.9 4.1 %collective-permute-start.28 = (bf16[128,256]{1,0:T(8,128)(2,1)S(1)}, bf16[128,256]{1,0:T(8,128)(2,1)S(1)}, u32[]{:S(2)}, u32[]{:S(2)}) collective-permute-start(bf16[128,256]{1,0:T(8,128)(2,1)S(1)} %get-tuple-element.55), channel_id=1, source_target_pairs={{5,0},{4,1},{7,2},{6,3},{0,4},{1,5},{2,6},{3,7},{13,8},{12,9},{15,... | collective-permute-start | bytes 196616 | tf_op jit(solution)/shard_map/ppermute | solution.py:56
  106.1 0.5 collective-permute-start.35
  106.6 0.7 collective-permute-done.34.refs_7_
  107.3 0.2 collective-permute-done.35.refs_8_
  107.4 0.3 collective-permute-done.27.refs_1_
  107.8 0.2 collective-permute-done.28.refs_2_
  107.9 3.6 %collective-permute-done.29.refs_3_ = bf16[128,256]{1,0:T(8,128)(2,1)S(1)} collective-permute-done((bf16[128,256]{1,0:T(8,128)(2,1)S(1)}, bf16[128,256]{1,0:T(8,128)(2,1)S(1)}, u32[]{:S(2)}, u32[]{:S(2)}) %collective-permute-start.29) | collective-permute-done | bytes 65568 | tf_op jit(solution)/shard_map/ppermute | solution.py:56
  111.5 1.3 %shard_map.167 = (bf16[256,128]{1,0:T(8,128)(2,1)}, f32[128,128]{1,0:T(8,128)}, f32[128,128]{1,0:T(8,128)}, f32[1,128]{1,0:T(1,128)}) custom-call(s32[2]{0:T(128)S(1)} %pad_add_fusion.1.ids_ref, bf16[128,256]{1,0:T(8,128)(2,1)S(1)} %get-tuple-element.54.refs_0_, bf16[128,256]{1,0:T(8,128)(2,1)S(1)} %collective-permute-done.27.refs_1_, ...), custom_call_target="tpu_custom_call" | custom-call | tf_op jit(solution)/shard_map/pallas_call | solution.py:96
  (49 shorter events, 0.5 us)
Async XLA Ops:
  1.3 5.0 %collective-permute-start.1 = (bf16[16,128]{1,0:T(8,128)(2,1)S(1)}, bf16[16,128]{1,0:T(8,128)(2,1)S(1)}, u32[]{:S(2)}, u32[]{:S(2)}) collective-permute-start(bf16[16,128]{1,0:T(8,128)(2,1)S(1)} %pad.8), channel_id=1, source_target_pairs={{5,0},{4,1},{6,2},{7,3},{0,4},{1,5},{3,6},{2,7},{13,8},{12,9},{14,... | collective-permute-start | bytes 12296 | tf_op jit(solution)/shard_map/ppermute | solution.py:56
  1.6 4.7 %collective-permute-start = (bf16[256,128]{1,0:T(8,128)(2,1)}, bf16[256,128]{1,0:T(8,128)(2,1)S(1)}, u32[]{:S(2)}, u32[]{:S(2)}) collective-permute-start(bf16[256,128]{1,0:T(8,128)(2,1)} %feat_ref.1), channel_id=1, source_target_pairs={{5,0},{4,1},{6,2},{7,3},{0,4},{1,5},{3,6},{2,7},{13,8},{12,9},{14,... | collective-permute-start | bytes 196616 | tf_op jit(solution)/shard_map/ppermute | solution.py:56
  7.2 10.6 %collective-permute-start.2 = (bf16[544,128]{1,0:T(8,128)(2,1)S(1)}, bf16[544,128]{1,0:T(8,128)(2,1)S(1)}, u32[]{:S(2)}, u32[]{:S(2)}) collective-permute-start(bf16[544,128]{1,0:T(8,128)(2,1)S(1)} %pad_maximum_fusion.refs_0_), channel_id=1, source_target_pairs={{120,0},{9,1},{122,2},{11,3},{124,4},{13,5},{126,6},{15,7},{0,8},{... | collective-permute-start | bytes 417800 | tf_op jit(solution)/shard_map/ppermute | solution.py:56
  7.7 10.1 %collective-permute-start.3 = (bf16[544,128]{1,0:T(8,128)(2,1)S(1)}, bf16[544,128]{1,0:T(8,128)(2,1)S(1)}, u32[]{:S(2)}, u32[]{:S(2)}) collective-permute-start(bf16[544,128]{1,0:T(8,128)(2,1)S(1)} %pad_maximum_fusion.refs_0_), channel_id=1, source_target_pairs={{112,0},{17,1},{114,2},{19,3},{116,4},{21,5},{118,6},{23,7},{120,8... | collective-permute-start | bytes 417800 | tf_op jit(solution)/shard_map/ppermute | solution.py:56
  8.0 10.5 %collective-permute-start.4 = (bf16[544,128]{1,0:T(8,128)(2,1)S(1)}, bf16[544,128]{1,0:T(8,128)(2,1)S(1)}, u32[]{:S(2)}, u32[]{:S(2)}) collective-permute-start(bf16[544,128]{1,0:T(8,128)(2,1)S(1)} %pad_maximum_fusion.refs_0_), channel_id=1, source_target_pairs={{104,0},{25,1},{106,2},{27,3},{108,4},{29,5},{110,6},{31,7},{112,8... | collective-permute-start | bytes 417800 | tf_op jit(solution)/shard_map/ppermute | solution.py:56
  12.7 5.7 %collective-permute-start.5 = (bf16[544,128]{1,0:T(8,128)(2,1)S(1)}, bf16[544,128]{1,0:T(8,128)(2,1)S(1)}, u32[]{:S(2)}, u32[]{:S(2)}) collective-permute-start(bf16[544,128]{1,0:T(8,128)(2,1)S(1)} %pad_maximum_fusion.refs_0_), channel_id=1, source_target_pairs={{96,0},{33,1},{98,2},{35,3},{100,4},{37,5},{102,6},{39,7},{104,8},... | collective-permute-start | bytes 417800 | tf_op jit(solution)/shard_map/ppermute | solution.py:56
  19.1 10.1 %collective-permute-start.6 = (bf16[1632,128]{1,0:T(8,128)(2,1)S(1)}, bf16[1632,128]{1,0:T(8,128)(2,1)S(1)}, u32[]{:S(2)}, u32[]{:S(2)}) collective-permute-start(bf16[1632,128]{1,0:T(8,128)(2,1)S(1)} %get-tuple-element.35), channel_id=1, source_target_pairs={{96,0},{33,1},{98,2},{35,3},{100,4},{37,5},{102,6},{39,7},{104,8},... | collective-permute-start | bytes 1253384 | tf_op jit(solution)/shard_map/ppermute | solution.py:56
  22.6 28.3 %collective-permute-start.12 = (bf16[2176,128]{1,0:T(8,128)(2,1)S(1)}, bf16[2176,128]{1,0:T(8,128)(2,1)S(1)}, u32[]{:S(2)}, u32[]{:S(2)}) collective-permute-start(bf16[2176,128]{1,0:T(8,128)(2,1)S(1)} %get-tuple-element.37.refs_1_), channel_id=1, source_target_pairs={{2,0},{3,1},{0,2},{1,3},{6,4},{7,5},{4,6},{5,7},{10,8},{11,9},{8,1... | collective-permute-start | bytes 1671176 | tf_op jit(solution)/shard_map/ppermute | solution.py:56
  22.6 7.3 %collective-permute-start.7 = (bf16[544,128]{1,0:T(8,128)(2,1)S(1)}, bf16[544,128]{1,0:T(8,128)(2,1)S(1)}, u32[]{:S(2)}, u32[]{:S(2)}) collective-permute-start(bf16[544,128]{1,0:T(8,128)(2,1)S(1)} %pad_maximum_fusion.refs_0_), channel_id=1, source_target_pairs={{0,96},{1,33},{2,98},{3,35},{4,100},{5,37},{6,102},{7,39},{8,104},... | collective-permute-start | bytes 417800 | tf_op jit(solution)/shard_map/ppermute | solution.py:56
  29.2 23.5 %collective-permute-start.9 = (bf16[1632,128]{1,0:T(8,128)(2,1)S(1)}, bf16[1632,128]{1,0:T(8,128)(2,1)S(1)}, u32[]{:S(2)}, u32[]{:S(2)}) collective-permute-start(bf16[1632,128]{1,0:T(8,128)(2,1)S(1)} %collective-permute-done.6.refs_0_), channel_id=1, source_target_pairs={{2,0},{3,1},{0,2},{1,3},{6,4},{7,5},{4,6},{5,7},{10,8},{11,9},{8,1... | collective-permute-start | bytes 1253384 | tf_op jit(solution)/shard_map/ppermute | solution.py:56
  29.9 7.4 %collective-permute-start.8 = (bf16[544,128]{1,0:T(8,128)(2,1)S(1)}, bf16[544,128]{1,0:T(8,128)(2,1)S(1)}, u32[]{:S(2)}, u32[]{:S(2)}) collective-permute-start(bf16[544,128]{1,0:T(8,128)(2,1)S(1)} %collective-permute-done.7), channel_id=1, source_target_pairs={{0,96},{1,33},{2,98},{3,35},{4,100},{5,37},{6,102},{7,39},{8,104},... | collective-permute-start | bytes 417800 | tf_op jit(solution)/shard_map/ppermute | solution.py:56
  29.9 21.0 %collective-permute-start.11 = (bf16[544,128]{1,0:T(8,128)(2,1)S(1)}, bf16[544,128]{1,0:T(8,128)(2,1)S(1)}, u32[]{:S(2)}, u32[]{:S(2)}) collective-permute-start(bf16[544,128]{1,0:T(8,128)(2,1)S(1)} %pad_maximum_fusion.refs_0_), channel_id=1, source_target_pairs={{2,0},{3,1},{0,2},{1,3},{6,4},{7,5},{4,6},{5,7},{10,8},{11,9},{8,1... | collective-permute-start | bytes 417800 | tf_op jit(solution)/shard_map/ppermute | solution.py:56
  37.2 15.4 %collective-permute-start.10 = (bf16[544,128]{1,0:T(8,128)(2,1)S(1)}, bf16[544,128]{1,0:T(8,128)(2,1)S(1)}, u32[]{:S(2)}, u32[]{:S(2)}) collective-permute-start(bf16[544,128]{1,0:T(8,128)(2,1)S(1)} %collective-permute-done.8.refs_1_), channel_id=1, source_target_pairs={{2,0},{3,1},{0,2},{1,3},{6,4},{7,5},{4,6},{5,7},{10,8},{11,9},{8,1... | collective-permute-start | bytes 417800 | tf_op jit(solution)/shard_map/ppermute | solution.py:56
  37.2 17.6 %collective-permute-start.14 = (bf16[528,128]{1,0:T(8,128)(2,1)S(1)}, bf16[528,128]{1,0:T(8,128)(2,1)S(1)}, u32[]{:S(2)}, u32[]{:S(2)}) collective-permute-start(bf16[528,128]{1,0:T(8,128)(2,1)S(1)} %pad_maximum_fusion.1), channel_id=1, source_target_pairs={{1,0},{0,1},{3,2},{2,3},{5,4},{4,5},{7,6},{6,7},{9,8},{8,9},{11,10... | collective-permute-start | bytes 405512 | tf_op jit(solution)/shard_map/ppermute | solution.py:56
  47.5 3.4 %copy-start = (bf16[64,16,256]{2,1,0:T(8,128)(2,1)S(1)}, bf16[64,16,256]{2,1,0:T(8,128)(2,1)}, u32[]{:S(2)}) copy-start(bf16[64,16,256]{2,1,0:T(8,128)(2,1)} %refs_5_.3) | copy-start | bytes 1572868
  52.6 7.5 %copy-start.1 = (bf16[256,128]{1,0:T(8,128)(2,1)S(1)}, bf16[256,128]{1,0:T(8,128)(2,1)}, u32[]{:S(2)}) copy-start(bf16[256,128]{1,0:T(8,128)(2,1)} %feat_ref.1) | copy-start | bytes 196612
  52.6 7.5 %copy-start.2 = (bf16[256,128]{1,0:T(8,128)(2,1)S(1)}, bf16[256,128]{1,0:T(8,128)(2,1)}, u32[]{:S(2)}) copy-start(bf16[256,128]{1,0:T(8,128)(2,1)} %ct_ref.1) | copy-start | bytes 196612
  52.6 7.5 %copy-start.3 = (bf16[128,128]{1,0:T(8,128)(2,1)S(1)}, bf16[128,128]{1,0:T(8,128)(2,1)}, u32[]{:S(2)}) copy-start(bf16[128,128]{1,0:T(8,128)(2,1)} %sw_ref.1) | copy-start | bytes 98308
  52.6 7.5 %copy-start.4 = (bf16[128,128]{1,0:T(8,128)(2,1)S(1)}, bf16[128,128]{1,0:T(8,128)(2,1)}, u32[]{:S(2)}) copy-start(bf16[128,128]{1,0:T(8,128)(2,1)} %nw_ref.1) | copy-start | bytes 98308
  52.6 7.5 %copy-start.5 = (f32[128]{0:T(128)S(1)}, f32[128]{0:T(128)}, u32[]{:S(2)}) copy-start(f32[128]{0:T(128)} %param.22) | copy-start | bytes 1540
  54.3 5.8 %collective-permute-start.13 = (bf16[256,128]{1,0:T(8,128)(2,1)S(1)}, bf16[256,128]{1,0:T(8,128)(2,1)S(1)}, u32[]{:S(2)}, u32[]{:S(2)}) collective-permute-start(bf16[256,128]{1,0:T(8,128)(2,1)S(1)} %get-tuple-element.39.mine_ref), channel_id=1, source_target_pairs={{1,0},{0,1},{3,2},{2,3},{5,4},{4,5},{7,6},{6,7},{9,8},{8,9},{11,10... | collective-permute-start | bytes 196616 | tf_op jit(solution)/shard_map/ppermute | solution.py:56
  62.8 2.2 %collective-permute-start.16 = (bf16[4,128,512]{2,1,0:T(8,128)(2,1)S(1)}, bf16[4,128,512]{2,1,0:T(8,128)(2,1)S(1)}, u32[]{:S(2)}, u32[]{:S(2)}) collective-permute-start(bf16[4,128,512]{2,1,0:T(8,128)(2,1)S(1)} %shard_map.163), channel_id=1, source_target_pairs={{2,0},{3,1},{0,2},{1,3},{6,4},{7,5},{4,6},{5,7},{10,8},{11,9},{8,1... | collective-permute-start | bytes 1572872 | tf_op jit(solution)/shard_map/ppermute | solution.py:56
  62.9 2.0 %collective-permute-start.18 = (f32[2,72,128]{2,1,0:T(8,128)S(1)}, f32[2,72,128]{2,1,0:T(8,128)S(1)}, u32[]{:S(2)}, u32[]{:S(2)}) collective-permute-start(f32[2,72,128]{2,1,0:T(8,128)S(1)} %get-tuple-element.48), channel_id=1, source_target_pairs={{2,0},{3,1},{0,2},{1,3},{6,4},{7,5},{4,6},{5,7},{10,8},{11,9},{8,1... | collective-permute-start | bytes 221192 | tf_op jit(solution)/shard_map/ppermute | solution.py:56
  64.6 18.9 %collective-permute-start.15 = (bf16[5,128,512]{2,1,0:T(8,128)(2,1)S(1)}, bf16[5,128,512]{2,1,0:T(8,128)(2,1)S(1)}, u32[]{:S(2)}, u32[]{:S(2)}) collective-permute-start(bf16[5,128,512]{2,1,0:T(8,128)(2,1)S(1)} %shard_map.161), channel_id=1, source_target_pairs={{2,0},{3,1},{0,2},{1,3},{6,4},{7,5},{4,6},{5,7},{10,8},{11,9},{8,1... | collective-permute-start | bytes 1966088 | tf_op jit(solution)/shard_map/ppermute | solution.py:56
  64.9 4.0 %collective-permute-start.19 = (f32[72,128]{1,0:T(8,128)S(1)}, f32[72,128]{1,0:T(8,128)S(1)}, u32[]{:S(2)}, u32[]{:S(2)}) collective-permute-start(f32[72,128]{1,0:T(8,128)S(1)} %slice_bitcast_fusion), channel_id=1, source_target_pairs={{4,0},{5,1},{6,2},{7,3},{0,4},{1,5},{2,6},{3,7},{12,8},{13,9},{14,... | collective-permute-start | bytes 110600 | tf_op jit(solution)/shard_map/ppermute | solution.py:56
  66.2 18.7 %collective-permute-start.17 = (bf16[4,128,512]{2,1,0:T(8,128)(2,1)S(1)}, bf16[4,128,512]{2,1,0:T(8,128)(2,1)S(1)}, u32[]{:S(2)}, u32[]{:S(2)}) collective-permute-start(bf16[4,128,512]{2,1,0:T(8,128)(2,1)S(1)} %shard_map.164), channel_id=1, source_target_pairs={{0,96},{1,33},{2,98},{3,35},{4,100},{5,37},{6,102},{7,39},{8,104},... | collective-permute-start | bytes 1572872 | tf_op jit(solution)/shard_map/ppermute | solution.py:56
  69.0 6.4 %collective-permute-start.20 = (f32[72,128]{1,0:T(8,128)S(1)}, f32[72,128]{1,0:T(8,128)S(1)}, u32[]{:S(2)}, u32[]{:S(2)}) collective-permute-start(f32[72,128]{1,0:T(8,128)S(1)} %fusion), channel_id=1, source_target_pairs={{8,0},{9,1},{10,2},{11,3},{12,4},{13,5},{14,6},{15,7},{0,8},{1,9},... | collective-permute-start | bytes 110600 | tf_op jit(solution)/shard_map/ppermute | solution.py:56
  70.2 5.6 %collective-permute-start.21 = (f32[72,128]{1,0:T(8,128)S(1)}, f32[72,128]{1,0:T(8,128)S(1)}, u32[]{:S(2)}, u32[]{:S(2)}) collective-permute-start(f32[72,128]{1,0:T(8,128)S(1)} %fusion), channel_id=1, source_target_pairs={{24,0},{25,1},{26,2},{27,3},{28,4},{29,5},{30,6},{31,7},{16,8},{17... | collective-permute-start | bytes 110600 | tf_op jit(solution)/shard_map/ppermute | solution.py:56
  73.9 5.5 %collective-permute-start.22 = (f32[72,128]{1,0:T(8,128)S(1)}, f32[72,128]{1,0:T(8,128)S(1)}, u32[]{:S(2)}, u32[]{:S(2)}) collective-permute-start(f32[72,128]{1,0:T(8,128)S(1)} %fusion), channel_id=1, source_target_pairs={{16,0},{17,1},{18,2},{19,3},{20,4},{21,5},{22,6},{23,7},{24,8},{25... | collective-permute-start | bytes 110600 | tf_op jit(solution)/shard_map/ppermute | solution.py:56
  79.4 9.1 %collective-permute-start.30 = (f32[72,128]{1,0:T(8,128)S(1)}, f32[72,128]{1,0:T(8,128)S(1)}, u32[]{:S(2)}, u32[]{:S(2)}) collective-permute-start(f32[72,128]{1,0:T(8,128)S(1)} %add_add_fusion.1), channel_id=1, source_target_pairs={{32,0},{33,1},{34,2},{35,3},{36,4},{37,5},{38,6},{39,7},{40,8},{41... | collective-permute-start | bytes 110600 | tf_op jit(solution)/shard_map/ppermute | solution.py:56
  79.5 9.0 %collective-permute-start.31 = (f32[72,128]{1,0:T(8,128)S(1)}, f32[72,128]{1,0:T(8,128)S(1)}, u32[]{:S(2)}, u32[]{:S(2)}) collective-permute-start(f32[72,128]{1,0:T(8,128)S(1)} %add_add_fusion.1), channel_id=1, source_target_pairs={{96,0},{97,1},{98,2},{99,3},{100,4},{101,5},{102,6},{103,7},{104,8... | collective-permute-start | bytes 110600 | tf_op jit(solution)/shard_map/ppermute | solution.py:56
  80.2 9.1 %collective-permute-start.32 = (f32[72,128]{1,0:T(8,128)S(1)}, f32[72,128]{1,0:T(8,128)S(1)}, u32[]{:S(2)}, u32[]{:S(2)}) collective-permute-start(f32[72,128]{1,0:T(8,128)S(1)} %add_add_fusion.1), channel_id=1, source_target_pairs={{64,0},{65,1},{66,2},{67,3},{68,4},{69,5},{70,6},{71,7},{72,8},{73... | collective-permute-start | bytes 110600 | tf_op jit(solution)/shard_map/ppermute | solution.py:56
  85.5 6.2 %collective-permute-start.23 = (bf16[128,512]{1,0:T(8,128)(2,1)S(1)}, bf16[128,512]{1,0:T(8,128)(2,1)S(1)}, u32[]{:S(2)}, u32[]{:S(2)}) collective-permute-start(bf16[128,512]{1,0:T(8,128)(2,1)S(1)} %get-tuple-element.50), channel_id=1, source_target_pairs={{0,120},{1,9},{2,122},{3,11},{4,124},{5,13},{6,126},{7,15},{8,0},{... | collective-permute-start | bytes 393224 | tf_op jit(solution)/shard_map/ppermute | solution.py:56
  86.1 6.7 %collective-permute-start.24 = (bf16[128,512]{1,0:T(8,128)(2,1)S(1)}, bf16[128,512]{1,0:T(8,128)(2,1)S(1)}, u32[]{:S(2)}, u32[]{:S(2)}) collective-permute-start(bf16[128,512]{1,0:T(8,128)(2,1)S(1)} %get-tuple-element.51), channel_id=1, source_target_pairs={{0,112},{1,17},{2,114},{3,19},{4,116},{5,21},{6,118},{7,23},{8,120... | collective-permute-start | bytes 393224 | tf_op jit(solution)/shard_map/ppermute | solution.py:56
  88.5 6.6 %collective-permute-start.25 = (bf16[128,512]{1,0:T(8,128)(2,1)S(1)}, bf16[128,512]{1,0:T(8,128)(2,1)S(1)}, u32[]{:S(2)}, u32[]{:S(2)}) collective-permute-start(bf16[128,512]{1,0:T(8,128)(2,1)S(1)} %get-tuple-element.52), channel_id=1, source_target_pairs={{0,104},{1,25},{2,106},{3,27},{4,108},{5,29},{6,110},{7,31},{8,112... | collective-permute-start | bytes 393224 | tf_op jit(solution)/shard_map/ppermute | solution.py:56
  88.5 12.7 %collective-permute-start.26 = (bf16[128,512]{1,0:T(8,128)(2,1)S(1)}, bf16[128,512]{1,0:T(8,128)(2,1)S(1)}, u32[]{:S(2)}, u32[]{:S(2)}) collective-permute-start(bf16[128,512]{1,0:T(8,128)(2,1)S(1)} %get-tuple-element.53), channel_id=1, source_target_pairs={{0,96},{1,33},{2,98},{3,35},{4,100},{5,37},{6,102},{7,39},{8,104},... | collective-permute-start | bytes 393224 | tf_op jit(solution)/shard_map/ppermute | solution.py:56
  89.3 16.7 %collective-permute-start.33 = (f32[72,128]{1,0:T(8,128)S(1)}, f32[72,128]{1,0:T(8,128)S(1)}, u32[]{:S(2)}, u32[]{:S(2)}) collective-permute-start(f32[72,128]{1,0:T(8,128)S(1)} %add_add_fusion.refs_5_), channel_id=1, source_target_pairs={{4,0},{5,1},{6,2},{7,3},{0,4},{1,5},{2,6},{3,7},{12,8},{13,9},{14,... | collective-permute-start | bytes 110600 | tf_op jit(solution)/shard_map/ppermute | solution.py:56
  101.8 5.9 %collective-permute-start.27 = (bf16[128,256]{1,0:T(8,128)(2,1)S(1)}, bf16[128,256]{1,0:T(8,128)(2,1)S(1)}, u32[]{:S(2)}, u32[]{:S(2)}) collective-permute-start(bf16[128,256]{1,0:T(8,128)(2,1)S(1)} %get-tuple-element.54.refs_0_), channel_id=1, source_target_pairs={{1,0},{0,1},{3,2},{2,3},{5,4},{4,5},{7,6},{6,7},{9,8},{8,9},{11,10... | collective-permute-start | bytes 196616 | tf_op jit(solution)/shard_map/ppermute | solution.py:56
  101.9 6.0 %collective-permute-start.28 = (bf16[128,256]{1,0:T(8,128)(2,1)S(1)}, bf16[128,256]{1,0:T(8,128)(2,1)S(1)}, u32[]{:S(2)}, u32[]{:S(2)}) collective-permute-start(bf16[128,256]{1,0:T(8,128)(2,1)S(1)} %get-tuple-element.55), channel_id=1, source_target_pairs={{5,0},{4,1},{7,2},{6,3},{0,4},{1,5},{2,6},{3,7},{13,8},{12,9},{15,... | collective-permute-start | bytes 196616 | tf_op jit(solution)/shard_map/ppermute | solution.py:56
  106.0 5.5 %collective-permute-start.29 = (bf16[128,256]{1,0:T(8,128)(2,1)S(1)}, bf16[128,256]{1,0:T(8,128)(2,1)S(1)}, u32[]{:S(2)}, u32[]{:S(2)}) collective-permute-start(bf16[128,256]{1,0:T(8,128)(2,1)S(1)} %get-tuple-element.55), channel_id=1, source_target_pairs={{4,0},{5,1},{6,2},{7,3},{1,4},{0,5},{3,6},{2,7},{12,8},{13,9},{14,... | collective-permute-start | bytes 196616 | tf_op jit(solution)/shard_map/ppermute | solution.py:56
  106.0 1.2 %collective-permute-start.34 = (f32[72,128]{1,0:T(8,128)S(1)}, f32[72,128]{1,0:T(8,128)S(1)}, u32[]{:S(2)}, u32[]{:S(2)}) collective-permute-start(f32[72,128]{1,0:T(8,128)S(1)} %add_add_fusion.refs_5_), channel_id=1, source_target_pairs={{2,0},{3,1},{0,2},{1,3},{6,4},{7,5},{4,6},{5,7},{10,8},{11,9},{8,1... | collective-permute-start | bytes 110600 | tf_op jit(solution)/shard_map/ppermute | solution.py:56
  106.1 1.4 %collective-permute-start.35 = (f32[72,128]{1,0:T(8,128)S(1)}, f32[72,128]{1,0:T(8,128)S(1)}, u32[]{:S(2)}, u32[]{:S(2)}) collective-permute-start(f32[72,128]{1,0:T(8,128)S(1)} %collective-permute-done.33.refs_6_), channel_id=1, source_target_pairs={{2,0},{3,1},{0,2},{1,3},{6,4},{7,5},{4,6},{5,7},{10,8},{11,9},{8,1... | collective-permute-start | bytes 110600 | tf_op jit(solution)/shard_map/ppermute | solution.py:56

commit v4 on v3

--- a/solution.py
+++ b/solution.py
@@ -195,28 +195,29 @@
             out[i * GROUP : (i + 1) * GROUP, :] = ref[...]
 
 
-def forward_kernel(columns, first, ids_ref, *refs):
-    groups, (mats_ref, hub_ref), refs = refs[:4], refs[4:6], refs[6:]
+def forward_kernel(columns, classes, first, ids_ref, *refs):
+    split = 2 * len(classes)
+    groups, (mats_ref, hub_ref), refs = refs[:split], refs[split : split + 2], refs[split + 2 :]
     before_ref, (out_ref, hot_ref, wts_ref, pick_ref) = (None, refs) if first else (refs[0], refs[1:])
     lane = lax.broadcasted_iota(jnp.int32, (2 * HEAD, 128), 1)
     column = lax.broadcasted_iota(jnp.int32, (2 * HEAD, 256), 1)
     total = None if first else before_ref[...]
-    for cls in range(2):
+    for n, cls in enumerate(classes):
         for i, k in enumerate(columns):
             if first:
-                ref, base = groups[cls * 2 + min(k, 1)], max(k - 1, 0) * GROUP
+                ref, base = groups[n * 2 + min(k, 1)], max(k - 1, 0) * GROUP
             else:
-                ref, base = groups[cls * 2 + i // 3], i % 3 * GROUP
+                ref, base = groups[n * 2 + i // 3], i % 3 * GROUP
             head = ref[base + 512 : base + GROUP, :].astype(jnp.float32)
             mine = jnp.sum(jnp.where(lane == ids_ref[0], head, 0.0), axis=1, keepdims=True)
             hot = (mine.astype(jnp.int32) == column).astype(jnp.float32).astype(jnp.bfloat16)
             for lr in range(2):
-                slot = (cls * len(columns) + i) * 2 + lr
+                slot = (n * len(columns) + i) * 2 + lr
                 source, valid = slot_source(ids_ref, cls, k, lr)
                 at = slice(slot * HEAD, (slot + 1) * HEAD)
                 one = hot[lr * HEAD : (lr + 1) * HEAD, :]
                 block = ref[base + lr * 256 : base + (lr + 1) * 256, :]
-                both = dot(jnp.concatenate([mats_ref[slot], one], axis=0), block)
+                both = dot(jnp.concatenate([mats_ref[(cls * len(columns) + i) * 2 + lr], one], axis=0), block)
                 total = both[:256] if total is None else total + both[:256]
                 hot_ref[at, :] = one
                 pick_ref[at, :] = both[256:].astype(jnp.bfloat16)
@@ -225,16 +226,13 @@
     out_ref[...] = (total + dot_tn(wts_ref[...], pick_ref[...])).astype(out_ref.dtype)
 
 
-def forward(columns, first, *args):
-    rows = 4 * len(columns) * HEAD
+def forward(columns, classes, dtype, *args):
+    rows = 2 * len(classes) * len(columns) * HEAD
+    first = len(args) == 2 * len(classes) + 3
     return kernel_call(
-        functools.partial(forward_kernel, columns, first),
+        functools.partial(forward_kernel, columns, classes, first),
         len(args) - 1,
-        [
-            ((256, 128), jnp.float32 if first else jnp.bfloat16),
-            ((rows, 256), jnp.bfloat16),
-            ((rows, 256), jnp.bfloat16),
-        ],
+        [((256, 128), dtype), ((rows, 256), jnp.bfloat16), ((rows, 256), jnp.bfloat16)],
         scratch=[pltpu.VMEM((rows, 128), jnp.bfloat16)],
         limit=20 * MIB,
     )(*args)
@@ -293,14 +291,15 @@
     out_ref = refs[-1]
     grad = grad_ref[...]
     count = 2 * len(columns) * HEAD
-    backs = dot_nt(wts_ref[cls * count : (cls + 1) * count, :], grad).astype(jnp.bfloat16)
+    first = 0 if hot_ref.shape[0] == count else cls * count
+    backs = dot_nt(wts_ref[first : first + count, :], grad).astype(jnp.bfloat16)
     for i in range(len(columns)):
         for lr in range(2):
             slot = (cls * len(columns) + i) * 2 + lr
-            at = slice(slot * HEAD, (slot + 1) * HEAD)
+            row = (2 * i + lr) * HEAD
             lanes = slice(lr * 256, (lr + 1) * 256)
-            back = backs[(2 * i + lr) * HEAD : (2 * i + lr + 1) * HEAD]
-            part = dot(grad, mats_ref[slot]) + dot_tn(back, hot_ref[at, :])
+            back = dot_tn(backs[row : row + HEAD], hot_ref[first + row : first + row + HEAD, :])
+            part = dot(grad, mats_ref[slot]) + back
             if add:
                 part += refs[0][i, :, lanes].astype(jnp.float32)
             out_ref[i, :, lanes] = part.astype(out_ref.dtype)
@@ -398,11 +397,10 @@
     oth3 = permute(last, SWAP_C)
 
     partial, hot_near, wts_near = forward(
-        NEAR, True, ids, col0, cols, oth0, oth1, mats_near, hub_weight
+        NEAR, (0, 1), f32, ids, col0, cols, oth0, oth1, mats_near, hub_weight
     )
-    partial, hot_far, wts_far = forward(
-        FAR, False, ids, far, last, oth2, oth3, mats_far, hub_weight, partial
-    )
+    partial, *hub0 = forward(FAR, (0,), f32, ids, far, last, mats_far, hub_weight, partial)
+    partial, *hub1 = forward(FAR, (1,), bf16, ids, oth2, oth3, mats_far, hub_weight, partial)
     theirs = permute(partial, SWAP_R)
     output, grad, self_grad, parts, give_parts = middle(
         ids,
@@ -416,12 +414,11 @@
         other,
     )
 
-    with_far = (grad, mats_far, hot_far, wts_far)
     with_near = (grad, mats_near, hot_near, wts_near)
-    got_far = permute(backward(1, FAR, bf16, ids, *with_far), SWAP_C)
+    got_far = permute(backward(1, FAR, bf16, ids, grad, mats_far, *hub1), SWAP_C)
     got_near = permute(backward(1, NEAR, bf16, ids, *with_near), SWAP_C)
     got_parts = permute(give_parts, SWAP_C)
-    sent = backward(0, FAR, bf16, ids, *with_far, got_far)
+    sent = backward(0, FAR, bf16, ids, grad, mats_far, *hub0, got_far)
     far_sums = permute(sent, inverse(FROM_COL[4]))
     keep = backward(0, NEAR, f32, ids, *with_near, got_near)
 

time: 113 us -> 114 us (level)
  the two profiles are of different devices: /device:TPU:120 before, /device:TPU:0 now
where the time goes in v4:
time: 114 us; the launch traced here: 112 us
  starting transfers between devices  50.1 us (44%)
  waiting for transfers between devices  35.1 us (31%)
  Pallas kernels  21 us (18%)
  other arithmetic  4.58 us (4%)
    ppermute x36, starting transfers between devices, permute(): return lax.ppermute(x, AXES, pairs)  50.1 us
    ppermute x36, waiting for transfers between devices, permute(): return lax.ppermute(x, AXES, pairs)  35.1 us
    pallas_call x12, Pallas kernels, call(): pl.pallas_call(body, in_specs=[smem()] + [vmem()] * n_in, out_specs=vmem(...  13.6 us
    pallas_call x2, Pallas kernels, densify(): pl.pallas_call(functools.partial(densify_kernel, columns), in_specs=[smem...  7.4 us
  transfers between devices with their start and end apart: 36, of which 19 were waited for; matrix products, arithmetic and copies ran while one was open for 3% of the time, Pallas kernels for 15%

profile of v4, /device:TPU:0, one launch (start us, length us, event | category | flops | bytes accessed | tf_op | source)
XLA Modules:
  0.0 111.8 jit_solution(17221281274037884376)
XLA Ops:
  0.6 0.7 fusion.5
  1.3 1.8 %collective-permute-start.1 = (bf16[16,128]{1,0:T(8,128)(2,1)S(1)}, bf16[16,128]{1,0:T(8,128)(2,1)S(1)}, u32[]{:S(2)}, u32[]{:S(2)}) collective-permute-start(bf16[16,128]{1,0:T(8,128)(2,1)S(1)} %pad.8), channel_id=1, source_target_pairs={{5,0},{4,1},{6,2},{7,3},{0,4},{1,5},{3,6},{2,7},{13,8},{12,9},{14,... | collective-permute-start | bytes 12296 | tf_op jit(solution)/shard_map/ppermute | solution.py:56
  3.1 1.6 %collective-permute-start = (bf16[256,128]{1,0:T(8,128)(2,1)}, bf16[256,128]{1,0:T(8,128)(2,1)S(1)}, u32[]{:S(2)}, u32[]{:S(2)}) collective-permute-start(bf16[256,128]{1,0:T(8,128)(2,1)} %feat_ref.1), channel_id=1, source_target_pairs={{5,0},{4,1},{6,2},{7,3},{0,4},{1,5},{3,6},{2,7},{13,8},{12,9},{14,... | collective-permute-start | bytes 196616 | tf_op jit(solution)/shard_map/ppermute | solution.py:56
  4.7 0.7 fusion.8
  5.3 0.7 multiply_add_fusion
  6.2 0.7 pad_add_fusion.table_ref
  6.9 0.9 pad_maximum_fusion.1
  7.8 1.0 collective-permute-done
  8.8 0.8 pad_maximum_fusion.refs_0_
  9.6 2.0 %collective-permute-start.2 = (bf16[544,128]{1,0:T(8,128)(2,1)S(1)}, bf16[544,128]{1,0:T(8,128)(2,1)S(1)}, u32[]{:S(2)}, u32[]{:S(2)}) collective-permute-start(bf16[544,128]{1,0:T(8,128)(2,1)S(1)} %pad_maximum_fusion.refs_0_), channel_id=1, source_target_pairs={{120,0},{9,1},{122,2},{11,3},{124,4},{13,5},{126,6},{15,7},{0,8},{... | collective-permute-start | bytes 417800 | tf_op jit(solution)/shard_map/ppermute | solution.py:56
  11.6 3.6 %collective-permute-start.3 = (bf16[544,128]{1,0:T(8,128)(2,1)S(1)}, bf16[544,128]{1,0:T(8,128)(2,1)S(1)}, u32[]{:S(2)}, u32[]{:S(2)}) collective-permute-start(bf16[544,128]{1,0:T(8,128)(2,1)S(1)} %pad_maximum_fusion.refs_0_), channel_id=1, source_target_pairs={{112,0},{17,1},{114,2},{19,3},{116,4},{21,5},{118,6},{23,7},{120,8... | collective-permute-start | bytes 417800 | tf_op jit(solution)/shard_map/ppermute | solution.py:56
  15.2 1.9 %collective-permute-start.4 = (bf16[544,128]{1,0:T(8,128)(2,1)S(1)}, bf16[544,128]{1,0:T(8,128)(2,1)S(1)}, u32[]{:S(2)}, u32[]{:S(2)}) collective-permute-start(bf16[544,128]{1,0:T(8,128)(2,1)S(1)} %pad_maximum_fusion.refs_0_), channel_id=1, source_target_pairs={{104,0},{25,1},{106,2},{27,3},{108,4},{29,5},{110,6},{31,7},{112,8... | collective-permute-start | bytes 417800 | tf_op jit(solution)/shard_map/ppermute | solution.py:56
  17.1 1.5 %collective-permute-start.5 = (bf16[544,128]{1,0:T(8,128)(2,1)S(1)}, bf16[544,128]{1,0:T(8,128)(2,1)S(1)}, u32[]{:S(2)}, u32[]{:S(2)}) collective-permute-start(bf16[544,128]{1,0:T(8,128)(2,1)S(1)} %pad_maximum_fusion.refs_0_), channel_id=1, source_target_pairs={{96,0},{33,1},{98,2},{35,3},{100,4},{37,5},{102,6},{39,7},{104,8},... | collective-permute-start | bytes 417800 | tf_op jit(solution)/shard_map/ppermute | solution.py:56
  18.6 2.3 %collective-permute-done.2.refs_0_ = bf16[544,128]{1,0:T(8,128)(2,1)S(1)} collective-permute-done((bf16[544,128]{1,0:T(8,128)(2,1)S(1)}, bf16[544,128]{1,0:T(8,128)(2,1)S(1)}, u32[]{:S(2)}, u32[]{:S(2)}) %collective-permute-start.2) | collective-permute-done | bytes 139296 | tf_op jit(solution)/shard_map/ppermute | solution.py:56
  20.9 1.0 collective-permute-done.3.refs_1_
  21.9 0.8 collective-permute-done.4.refs_2_
  22.8 0.7 collective-permute-done.5.refs_3_
  23.4 0.7 shard_map.155
  24.1 0.3 collective-permute-start.6
  24.4 3.0 %collective-permute-start.8 = (bf16[544,128]{1,0:T(8,128)(2,1)S(1)}, bf16[544,128]{1,0:T(8,128)(2,1)S(1)}, u32[]{:S(2)}, u32[]{:S(2)}) collective-permute-start(bf16[544,128]{1,0:T(8,128)(2,1)S(1)} %pad_maximum_fusion.refs_0_), channel_id=1, source_target_pairs={{0,96},{1,33},{2,98},{3,35},{4,100},{5,37},{6,102},{7,39},{8,104},... | collective-permute-start | bytes 417800 | tf_op jit(solution)/shard_map/ppermute | solution.py:56
  27.4 6.8 %collective-permute-done.6.refs_0_ = bf16[1632,128]{1,0:T(8,128)(2,1)S(1)} collective-permute-done((bf16[1632,128]{1,0:T(8,128)(2,1)S(1)}, bf16[1632,128]{1,0:T(8,128)(2,1)S(1)}, u32[]{:S(2)}, u32[]{:S(2)}) %collective-permute-start.6) | collective-permute-done | bytes 417824 | tf_op jit(solution)/shard_map/ppermute | solution.py:56
  34.1 0.5 collective-permute-start.9
  34.7 5.5 %collective-permute-done.9.refs_1_ = bf16[544,128]{1,0:T(8,128)(2,1)S(1)} collective-permute-done((bf16[544,128]{1,0:T(8,128)(2,1)S(1)}, bf16[544,128]{1,0:T(8,128)(2,1)S(1)}, u32[]{:S(2)}, u32[]{:S(2)}) %collective-permute-start.9) | collective-permute-done | bytes 139296 | tf_op jit(solution)/shard_map/ppermute | solution.py:56
  40.2 5.2 %collective-permute-start.14 = (bf16[528,128]{1,0:T(8,128)(2,1)S(1)}, bf16[528,128]{1,0:T(8,128)(2,1)S(1)}, u32[]{:S(2)}, u32[]{:S(2)}) collective-permute-start(bf16[528,128]{1,0:T(8,128)(2,1)S(1)} %pad_maximum_fusion.1), channel_id=1, source_target_pairs={{1,0},{0,1},{3,2},{2,3},{5,4},{4,5},{7,6},{6,7},{9,8},{8,9},{11,10... | collective-permute-start | bytes 405512 | tf_op jit(solution)/shard_map/ppermute | solution.py:56
  45.4 4.1 %shard_map.157.refs_4_.mats_ref = bf16[20,256,256]{2,1,0:T(8,128)(2,1)S(1)} custom-call(s32[2]{0:T(128)S(1)} %pad_add_fusion.1.ids_ref, s32[544]{0:T(1024)S(1)} %pad_add_fusion.table_ref, bf16[1,32,16,128,128]{4,3,2,1,0:T(8,128)(2,1)} %tiles_ref.3), custom_call_target="tpu_custom_call" | custom-call | tf_op jit(solution)/shard_map/pallas_call | solution.py:178
  49.6 3.3 %shard_map.156.refs_2_.mats_ref = bf16[16,256,256]{2,1,0:T(8,128)(2,1)S(1)} custom-call(s32[2]{0:T(128)S(1)} %pad_add_fusion.1.ids_ref, s32[544]{0:T(1024)S(1)} %pad_add_fusion.table_ref, bf16[1,32,16,128,128]{4,3,2,1,0:T(8,128)(2,1)} %tiles_ref.3), custom_call_target="tpu_custom_call" | custom-call | tf_op jit(solution)/shard_map/pallas_call | solution.py:178
  52.9 1.7 %shard_map.158 = (f32[256,128]{1,0:T(8,128)S(1)}, bf16[320,256]{1,0:T(8,128)(2,1)S(1)}, bf16[320,256]{1,0:T(8,128)(2,1)S(1)}) custom-call(s32[2]{0:T(128)S(1)} %pad_add_fusion.1.ids_ref, bf16[544,128]{1,0:T(8,128)(2,1)S(1)} %pad_maximum_fusion.refs_0_, bf16[2176,128]{1,0:T(8,128)(2,1)S(1)} %get-tuple-element.40.refs_1_, ...), custom_call_target="tpu_custom_call" | custom-call | tf_op jit(solution)/shard_map/pallas_call | solution.py:96
  54.6 1.2 %shard_map.159 = (f32[256,128]{1,0:T(8,128)S(1)}, bf16[128,256]{1,0:T(8,128)(2,1)S(1)}, bf16[128,256]{1,0:T(8,128)(2,1)S(1)}) custom-call(s32[2]{0:T(128)S(1)} %pad_add_fusion.1.ids_ref, bf16[1632,128]{1,0:T(8,128)(2,1)S(1)} %collective-permute-done.6.refs_0_, bf16[544,128]{1,0:T(8,128)(2,1)S(1)} %collective-permute-done.9.refs_1_, ...), custom_call_target="tpu_custom_call" | custom-call | tf_op jit(solution)/shard_map/pallas_call | solution.py:96
  55.8 1.2 %shard_map.160 = (bf16[256,128]{1,0:T(8,128)(2,1)S(1)}, bf16[128,256]{1,0:T(8,128)(2,1)S(1)}, bf16[128,256]{1,0:T(8,128)(2,1)S(1)}) custom-call(s32[2]{0:T(128)S(1)} %pad_add_fusion.1.ids_ref, bf16[1632,128]{1,0:T(8,128)(2,1)S(1)} %collective-permute-done.7.refs_0_, bf16[544,128]{1,0:T(8,128)(2,1)S(1)} %collective-permute-done.10.refs_1_, ...), custom_call_target="tpu_custom_call" | custom-call | tf_op jit(solution)/shard_map/pallas_call | solution.py:96
  57.1 5.8 %collective-permute-done.13.theirs_ref = bf16[256,128]{1,0:T(8,128)(2,1)S(1)} collective-permute-done((bf16[256,128]{1,0:T(8,128)(2,1)S(1)}, bf16[256,128]{1,0:T(8,128)(2,1)S(1)}, u32[]{:S(2)}, u32[]{:S(2)}) %collective-permute-start.13) | collective-permute-done | bytes 65568 | tf_op jit(solution)/shard_map/ppermute | solution.py:56
  62.9 1.5 %shard_map.161 = (bf16[256,128]{1,0:T(8,128)(2,1)}, bf16[128,256]{1,0:T(8,128)(2,1)S(1)}, f32[128,256]{1,0:T(8,128)S(1)}, f32[2,72,128]{2,1,0:T(8,128)S(1)}, f32[2,72,128]{2,1,0:T(8,128)S(1)}) custom-call(s32[2]{0:T(128)S(1)} %pad_add_fusion.1.ids_ref, bf16[256,128]{1,0:T(8,128)(2,1)S(1)} %get-tuple-element.43.mine_ref, ...), custom_call_target="tpu_custom_call" | custom-call | tf_op jit(solution)/shard_map/pallas_call | solution.py:96
  64.3 1.2 %shard_map.164 = bf16[4,128,512]{2,1,0:T(8,128)(2,1)S(1)} custom-call(s32[2]{0:T(128)S(1)} %pad_add_fusion.1.ids_ref, bf16[128,256]{1,0:T(8,128)(2,1)S(1)} %get-tuple-element.46.grad_ref, bf16[16,256,256]{2,1,0:T(8,128)(2,1)S(1)} %shard_map.156.refs_2_.mats_ref, bf16[128,256]{1,0:T(8,128)(2,1)S(1)} %get-tuple-element.51.hot_ref, ...), custom_call_target="tpu_custom_call" | custom-call | tf_op jit(solution)/shard_map/pallas_call | solution.py:96
  65.6 0.5 collective-permute-start.18
  66.1 1.3 %shard_map.162 = bf16[5,128,512]{2,1,0:T(8,128)(2,1)S(1)} custom-call(s32[2]{0:T(128)S(1)} %pad_add_fusion.1.ids_ref, bf16[128,256]{1,0:T(8,128)(2,1)S(1)} %get-tuple-element.46.grad_ref, bf16[20,256,256]{2,1,0:T(8,128)(2,1)S(1)} %shard_map.157.refs_4_.mats_ref, bf16[320,256]{1,0:T(8,128)(2,1)S(1)} %get-tuple-element.47.hot_ref, ...), custom_call_target="tpu_custom_call" | custom-call | tf_op jit(solution)/shard_map/pallas_call | solution.py:96
  67.4 0.2 collective-permute-start.15
  67.6 7.5 %collective-permute-start.19 = (f32[72,128]{1,0:T(8,128)S(1)}, f32[72,128]{1,0:T(8,128)S(1)}, u32[]{:S(2)}, u32[]{:S(2)}) collective-permute-start(f32[72,128]{1,0:T(8,128)S(1)} %slice_bitcast_fusion), channel_id=1, source_target_pairs={{4,0},{5,1},{6,2},{7,3},{0,4},{1,5},{2,6},{3,7},{12,8},{13,9},{14,... | collective-permute-start | bytes 110600 | tf_op jit(solution)/shard_map/ppermute | solution.py:56
  75.1 1.2 %shard_map.165 = bf16[4,128,512]{2,1,0:T(8,128)(2,1)S(1)} custom-call(s32[2]{0:T(128)S(1)} %pad_add_fusion.1.ids_ref, bf16[128,256]{1,0:T(8,128)(2,1)S(1)} %get-tuple-element.46.grad_ref, bf16[16,256,256]{2,1,0:T(8,128)(2,1)S(1)} %shard_map.156.refs_2_.mats_ref, bf16[128,256]{1,0:T(8,128)(2,1)S(1)} %get-tuple-element.49.hot_ref, ...), custom_call_target="tpu_custom_call" | custom-call | tf_op jit(solution)/shard_map/pallas_call | solution.py:96
  76.4 0.7 collective-permute-done.19
  77.1 0.1 collective-permute-start.21
  77.2 4.0 %collective-permute-start.22 = (f32[72,128]{1,0:T(8,128)S(1)}, f32[72,128]{1,0:T(8,128)S(1)}, u32[]{:S(2)}, u32[]{:S(2)}) collective-permute-start(f32[72,128]{1,0:T(8,128)S(1)} %fusion), channel_id=1, source_target_pairs={{16,0},{17,1},{18,2},{19,3},{20,4},{21,5},{22,6},{23,7},{24,8},{25... | collective-permute-start | bytes 110600 | tf_op jit(solution)/shard_map/ppermute | solution.py:56
  81.2 1.2 %collective-permute-done.21 = f32[72,128]{1,0:T(8,128)S(1)} collective-permute-done((f32[72,128]{1,0:T(8,128)S(1)}, f32[72,128]{1,0:T(8,128)S(1)}, u32[]{:S(2)}, u32[]{:S(2)}) %collective-permute-start.21) | collective-permute-done | bytes 36896 | tf_op jit(solution)/shard_map/ppermute | solution.py:56
  82.3 0.8 collective-permute-done.22
  83.1 1.7 %collective-permute-start.30 = (f32[72,128]{1,0:T(8,128)S(1)}, f32[72,128]{1,0:T(8,128)S(1)}, u32[]{:S(2)}, u32[]{:S(2)}) collective-permute-start(f32[72,128]{1,0:T(8,128)S(1)} %add_add_fusion.1), channel_id=1, source_target_pairs={{32,0},{33,1},{34,2},{35,3},{36,4},{37,5},{38,6},{39,7},{40,8},{41... | collective-permute-start | bytes 110600 | tf_op jit(solution)/shard_map/ppermute | solution.py:56
  84.8 2.7 %collective-permute-start.32 = (f32[72,128]{1,0:T(8,128)S(1)}, f32[72,128]{1,0:T(8,128)S(1)}, u32[]{:S(2)}, u32[]{:S(2)}) collective-permute-start(f32[72,128]{1,0:T(8,128)S(1)} %add_add_fusion.1), channel_id=1, source_target_pairs={{64,0},{65,1},{66,2},{67,3},{68,4},{69,5},{70,6},{71,7},{72,8},{73... | collective-permute-start | bytes 110600 | tf_op jit(solution)/shard_map/ppermute | solution.py:56
  87.5 1.3 %shard_map.163.keep_ref = f32[5,128,512]{2,1,0:T(8,128)S(1)} custom-call(s32[2]{0:T(128)S(1)} %pad_add_fusion.1.ids_ref, bf16[128,256]{1,0:T(8,128)(2,1)S(1)} %get-tuple-element.46.grad_ref, bf16[20,256,256]{2,1,0:T(8,128)(2,1)S(1)} %shard_map.157.refs_4_.mats_ref, bf16[320,256]{1,0:T(8,128)(2,1)S(1)} %get-tuple-element.47.hot_ref, ...), custom_call_target="tpu_custom_call" | custom-call | tf_op jit(solution)/shard_map/pallas_call | solution.py:96
  88.8 2.1 %collective-permute-done.17.far_ref = bf16[4,128,512]{2,1,0:T(8,128)(2,1)S(1)} collective-permute-done((bf16[4,128,512]{2,1,0:T(8,128)(2,1)S(1)}, bf16[4,128,512]{2,1,0:T(8,128)(2,1)S(1)}, u32[]{:S(2)}, u32[]{:S(2)}) %collective-permute-start.17) | collective-permute-done | bytes 524320 | tf_op jit(solution)/shard_map/ppermute | solution.py:56
  90.9 0.6 shard_map.166
  91.5 0.8 collective-permute-start.23
  92.3 2.1 %collective-permute-start.24 = (bf16[128,512]{1,0:T(8,128)(2,1)S(1)}, bf16[128,512]{1,0:T(8,128)(2,1)S(1)}, u32[]{:S(2)}, u32[]{:S(2)}) collective-permute-start(bf16[128,512]{1,0:T(8,128)(2,1)S(1)} %get-tuple-element.57), channel_id=1, source_target_pairs={{0,112},{1,17},{2,114},{3,19},{4,116},{5,21},{6,118},{7,23},{8,120... | collective-permute-start | bytes 393224 | tf_op jit(solution)/shard_map/ppermute | solution.py:56
  94.4 0.4 collective-permute-start.25
  94.7 2.6 %collective-permute-start.26 = (bf16[128,512]{1,0:T(8,128)(2,1)S(1)}, bf16[128,512]{1,0:T(8,128)(2,1)S(1)}, u32[]{:S(2)}, u32[]{:S(2)}) collective-permute-start(bf16[128,512]{1,0:T(8,128)(2,1)S(1)} %get-tuple-element.59), channel_id=1, source_target_pairs={{0,96},{1,33},{2,98},{3,35},{4,100},{5,37},{6,102},{7,39},{8,104},... | collective-permute-start | bytes 393224 | tf_op jit(solution)/shard_map/ppermute | solution.py:56
  97.4 0.8 collective-permute-start.33
  98.1 1.6 %collective-permute-done.24.refs_1_ = bf16[128,512]{1,0:T(8,128)(2,1)S(1)} collective-permute-done((bf16[128,512]{1,0:T(8,128)(2,1)S(1)}, bf16[128,512]{1,0:T(8,128)(2,1)S(1)}, u32[]{:S(2)}, u32[]{:S(2)}) %collective-permute-start.24) | collective-permute-done | bytes 131104 | tf_op jit(solution)/shard_map/ppermute | solution.py:56
  99.8 1.3 %collective-permute-done.25.refs_2_ = bf16[128,512]{1,0:T(8,128)(2,1)S(1)} collective-permute-done((bf16[128,512]{1,0:T(8,128)(2,1)S(1)}, bf16[128,512]{1,0:T(8,128)(2,1)S(1)}, u32[]{:S(2)}, u32[]{:S(2)}) %collective-permute-start.25) | collective-permute-done | bytes 131104 | tf_op jit(solution)/shard_map/ppermute | solution.py:56
  101.1 1.8 %collective-permute-done.26.refs_3_ = bf16[128,512]{1,0:T(8,128)(2,1)S(1)} collective-permute-done((bf16[128,512]{1,0:T(8,128)(2,1)S(1)}, bf16[128,512]{1,0:T(8,128)(2,1)S(1)}, u32[]{:S(2)}, u32[]{:S(2)}) %collective-permute-start.26) | collective-permute-done | bytes 131104 | tf_op jit(solution)/shard_map/ppermute | solution.py:56
  102.9 0.6 shard_map.167
  103.5 1.3 %collective-permute-start.27 = (bf16[128,256]{1,0:T(8,128)(2,1)S(1)}, bf16[128,256]{1,0:T(8,128)(2,1)S(1)}, u32[]{:S(2)}, u32[]{:S(2)}) collective-permute-start(bf16[128,256]{1,0:T(8,128)(2,1)S(1)} %get-tuple-element.60.refs_0_), channel_id=1, source_target_pairs={{1,0},{0,1},{3,2},{2,3},{5,4},{4,5},{7,6},{6,7},{9,8},{8,9},{11,10... | collective-permute-start | bytes 196616 | tf_op jit(solution)/shard_map/ppermute | solution.py:56
  104.9 0.8 collective-permute-start.28
  105.7 2.6 %collective-permute-start.29 = (bf16[128,256]{1,0:T(8,128)(2,1)S(1)}, bf16[128,256]{1,0:T(8,128)(2,1)S(1)}, u32[]{:S(2)}, u32[]{:S(2)}) collective-permute-start(bf16[128,256]{1,0:T(8,128)(2,1)S(1)} %get-tuple-element.61), channel_id=1, source_target_pairs={{4,0},{5,1},{6,2},{7,3},{1,4},{0,5},{3,6},{2,7},{12,8},{13,9},{14,... | collective-permute-start | bytes 196616 | tf_op jit(solution)/shard_map/ppermute | solution.py:56
  108.3 0.5 collective-permute-start.35
  108.8 0.7 collective-permute-done.34.refs_7_
  109.5 0.2 collective-permute-done.35.refs_8_
  109.7 0.9 collective-permute-done.28.refs_2_
  110.5 1.3 %shard_map.168 = (bf16[256,128]{1,0:T(8,128)(2,1)}, f32[128,128]{1,0:T(8,128)}, f32[128,128]{1,0:T(8,128)}, f32[1,128]{1,0:T(1,128)}) custom-call(s32[2]{0:T(128)S(1)} %pad_add_fusion.1.ids_ref, bf16[128,256]{1,0:T(8,128)(2,1)S(1)} %get-tuple-element.60.refs_0_, bf16[128,256]{1,0:T(8,128)(2,1)S(1)} %collective-permute-done.27.refs_1_, ...), custom_call_target="tpu_custom_call" | custom-call | tf_op jit(solution)/shard_map/pallas_call | solution.py:96
  (50 shorter events, 0.7 us)
Async XLA Ops:
  1.3 6.5 %collective-permute-start.1 = (bf16[16,128]{1,0:T(8,128)(2,1)S(1)}, bf16[16,128]{1,0:T(8,128)(2,1)S(1)}, u32[]{:S(2)}, u32[]{:S(2)}) collective-permute-start(bf16[16,128]{1,0:T(8,128)(2,1)S(1)} %pad.8), channel_id=1, source_target_pairs={{5,0},{4,1},{6,2},{7,3},{0,4},{1,5},{3,6},{2,7},{13,8},{12,9},{14,... | collective-permute-start | bytes 12296 | tf_op jit(solution)/shard_map/ppermute | solution.py:56
  3.1 5.7 %collective-permute-start = (bf16[256,128]{1,0:T(8,128)(2,1)}, bf16[256,128]{1,0:T(8,128)(2,1)S(1)}, u32[]{:S(2)}, u32[]{:S(2)}) collective-permute-start(bf16[256,128]{1,0:T(8,128)(2,1)} %feat_ref.1), channel_id=1, source_target_pairs={{5,0},{4,1},{6,2},{7,3},{0,4},{1,5},{3,6},{2,7},{13,8},{12,9},{14,... | collective-permute-start | bytes 196616 | tf_op jit(solution)/shard_map/ppermute | solution.py:56
  9.6 11.3 %collective-permute-start.2 = (bf16[544,128]{1,0:T(8,128)(2,1)S(1)}, bf16[544,128]{1,0:T(8,128)(2,1)S(1)}, u32[]{:S(2)}, u32[]{:S(2)}) collective-permute-start(bf16[544,128]{1,0:T(8,128)(2,1)S(1)} %pad_maximum_fusion.refs_0_), channel_id=1, source_target_pairs={{120,0},{9,1},{122,2},{11,3},{124,4},{13,5},{126,6},{15,7},{0,8},{... | collective-permute-start | bytes 417800 | tf_op jit(solution)/shard_map/ppermute | solution.py:56
  11.6 10.3 %collective-permute-start.3 = (bf16[544,128]{1,0:T(8,128)(2,1)S(1)}, bf16[544,128]{1,0:T(8,128)(2,1)S(1)}, u32[]{:S(2)}, u32[]{:S(2)}) collective-permute-start(bf16[544,128]{1,0:T(8,128)(2,1)S(1)} %pad_maximum_fusion.refs_0_), channel_id=1, source_target_pairs={{112,0},{17,1},{114,2},{19,3},{116,4},{21,5},{118,6},{23,7},{120,8... | collective-permute-start | bytes 417800 | tf_op jit(solution)/shard_map/ppermute | solution.py:56
  15.2 7.5 %collective-permute-start.4 = (bf16[544,128]{1,0:T(8,128)(2,1)S(1)}, bf16[544,128]{1,0:T(8,128)(2,1)S(1)}, u32[]{:S(2)}, u32[]{:S(2)}) collective-permute-start(bf16[544,128]{1,0:T(8,128)(2,1)S(1)} %pad_maximum_fusion.refs_0_), channel_id=1, source_target_pairs={{104,0},{25,1},{106,2},{27,3},{108,4},{29,5},{110,6},{31,7},{112,8... | collective-permute-start | bytes 417800 | tf_op jit(solution)/shard_map/ppermute | solution.py:56
  17.1 6.3 %collective-permute-start.5 = (bf16[544,128]{1,0:T(8,128)(2,1)S(1)}, bf16[544,128]{1,0:T(8,128)(2,1)S(1)}, u32[]{:S(2)}, u32[]{:S(2)}) collective-permute-start(bf16[544,128]{1,0:T(8,128)(2,1)S(1)} %pad_maximum_fusion.refs_0_), channel_id=1, source_target_pairs={{96,0},{33,1},{98,2},{35,3},{100,4},{37,5},{102,6},{39,7},{104,8},... | collective-permute-start | bytes 417800 | tf_op jit(solution)/shard_map/ppermute | solution.py:56
  24.1 10.1 %collective-permute-start.6 = (bf16[1632,128]{1,0:T(8,128)(2,1)S(1)}, bf16[1632,128]{1,0:T(8,128)(2,1)S(1)}, u32[]{:S(2)}, u32[]{:S(2)}) collective-permute-start(bf16[1632,128]{1,0:T(8,128)(2,1)S(1)} %get-tuple-element.38), channel_id=1, source_target_pairs={{96,0},{33,1},{98,2},{35,3},{100,4},{37,5},{102,6},{39,7},{104,8},... | collective-permute-start | bytes 1253384 | tf_op jit(solution)/shard_map/ppermute | solution.py:56
  24.4 28.4 %collective-permute-start.12 = (bf16[2176,128]{1,0:T(8,128)(2,1)S(1)}, bf16[2176,128]{1,0:T(8,128)(2,1)S(1)}, u32[]{:S(2)}, u32[]{:S(2)}) collective-permute-start(bf16[2176,128]{1,0:T(8,128)(2,1)S(1)} %get-tuple-element.40.refs_1_), channel_id=1, source_target_pairs={{2,0},{3,1},{0,2},{1,3},{6,4},{7,5},{4,6},{5,7},{10,8},{11,9},{8,1... | collective-permute-start | bytes 1671176 | tf_op jit(solution)/shard_map/ppermute | solution.py:56
  24.4 9.7 %collective-permute-start.8 = (bf16[544,128]{1,0:T(8,128)(2,1)S(1)}, bf16[544,128]{1,0:T(8,128)(2,1)S(1)}, u32[]{:S(2)}, u32[]{:S(2)}) collective-permute-start(bf16[544,128]{1,0:T(8,128)(2,1)S(1)} %pad_maximum_fusion.refs_0_), channel_id=1, source_target_pairs={{0,96},{1,33},{2,98},{3,35},{4,100},{5,37},{6,102},{7,39},{8,104},... | collective-permute-start | bytes 417800 | tf_op jit(solution)/shard_map/ppermute | solution.py:56
  34.1 21.7 %collective-permute-start.7 = (bf16[1632,128]{1,0:T(8,128)(2,1)S(1)}, bf16[1632,128]{1,0:T(8,128)(2,1)S(1)}, u32[]{:S(2)}, u32[]{:S(2)}) collective-permute-start(bf16[1632,128]{1,0:T(8,128)(2,1)S(1)} %collective-permute-done.6.refs_0_), channel_id=1, source_target_pairs={{2,0},{3,1},{0,2},{1,3},{6,4},{7,5},{4,6},{5,7},{10,8},{11,9},{8,1... | collective-permute-start | bytes 1253384 | tf_op jit(solution)/shard_map/ppermute | solution.py:56
  34.1 6.1 %collective-permute-start.9 = (bf16[544,128]{1,0:T(8,128)(2,1)S(1)}, bf16[544,128]{1,0:T(8,128)(2,1)S(1)}, u32[]{:S(2)}, u32[]{:S(2)}) collective-permute-start(bf16[544,128]{1,0:T(8,128)(2,1)S(1)} %collective-permute-done.8), channel_id=1, source_target_pairs={{0,96},{1,33},{2,98},{3,35},{4,100},{5,37},{6,102},{7,39},{8,104},... | collective-permute-start | bytes 417800 | tf_op jit(solution)/shard_map/ppermute | solution.py:56
  34.7 18.2 %collective-permute-start.11 = (bf16[544,128]{1,0:T(8,128)(2,1)S(1)}, bf16[544,128]{1,0:T(8,128)(2,1)S(1)}, u32[]{:S(2)}, u32[]{:S(2)}) collective-permute-start(bf16[544,128]{1,0:T(8,128)(2,1)S(1)} %pad_maximum_fusion.refs_0_), channel_id=1, source_target_pairs={{2,0},{3,1},{0,2},{1,3},{6,4},{7,5},{4,6},{5,7},{10,8},{11,9},{8,1... | collective-permute-start | bytes 417800 | tf_op jit(solution)/shard_map/ppermute | solution.py:56
  40.2 15.6 %collective-permute-start.10 = (bf16[544,128]{1,0:T(8,128)(2,1)S(1)}, bf16[544,128]{1,0:T(8,128)(2,1)S(1)}, u32[]{:S(2)}, u32[]{:S(2)}) collective-permute-start(bf16[544,128]{1,0:T(8,128)(2,1)S(1)} %collective-permute-done.9.refs_1_), channel_id=1, source_target_pairs={{2,0},{3,1},{0,2},{1,3},{6,4},{7,5},{4,6},{5,7},{10,8},{11,9},{8,1... | collective-permute-start | bytes 417800 | tf_op jit(solution)/shard_map/ppermute | solution.py:56
  40.2 16.8 %collective-permute-start.14 = (bf16[528,128]{1,0:T(8,128)(2,1)S(1)}, bf16[528,128]{1,0:T(8,128)(2,1)S(1)}, u32[]{:S(2)}, u32[]{:S(2)}) collective-permute-start(bf16[528,128]{1,0:T(8,128)(2,1)S(1)} %pad_maximum_fusion.1), channel_id=1, source_target_pairs={{1,0},{0,1},{3,2},{2,3},{5,4},{4,5},{7,6},{6,7},{9,8},{8,9},{11,10... | collective-permute-start | bytes 405512 | tf_op jit(solution)/shard_map/ppermute | solution.py:56
  49.5 3.3 %copy-start = (bf16[64,16,256]{2,1,0:T(8,128)(2,1)S(1)}, bf16[64,16,256]{2,1,0:T(8,128)(2,1)}, u32[]{:S(2)}) copy-start(bf16[64,16,256]{2,1,0:T(8,128)(2,1)} %refs_3_.3) | copy-start | bytes 1572868
  54.6 8.3 %copy-start.1 = (bf16[256,128]{1,0:T(8,128)(2,1)S(1)}, bf16[256,128]{1,0:T(8,128)(2,1)}, u32[]{:S(2)}) copy-start(bf16[256,128]{1,0:T(8,128)(2,1)} %feat_ref.1) | copy-start | bytes 196612
  54.6 8.3 %copy-start.2 = (bf16[256,128]{1,0:T(8,128)(2,1)S(1)}, bf16[256,128]{1,0:T(8,128)(2,1)}, u32[]{:S(2)}) copy-start(bf16[256,128]{1,0:T(8,128)(2,1)} %ct_ref.1) | copy-start | bytes 196612
  54.6 8.3 %copy-start.3 = (bf16[128,128]{1,0:T(8,128)(2,1)S(1)}, bf16[128,128]{1,0:T(8,128)(2,1)}, u32[]{:S(2)}) copy-start(bf16[128,128]{1,0:T(8,128)(2,1)} %sw_ref.1) | copy-start | bytes 98308
  54.6 8.3 %copy-start.4 = (bf16[128,128]{1,0:T(8,128)(2,1)S(1)}, bf16[128,128]{1,0:T(8,128)(2,1)}, u32[]{:S(2)}) copy-start(bf16[128,128]{1,0:T(8,128)(2,1)} %nw_ref.1) | copy-start | bytes 98308
  54.6 8.3 %copy-start.5 = (f32[128]{0:T(128)S(1)}, f32[128]{0:T(128)}, u32[]{:S(2)}) copy-start(f32[128]{0:T(128)} %param.22) | copy-start | bytes 1540
  57.0 5.9 %collective-permute-start.13 = (bf16[256,128]{1,0:T(8,128)(2,1)S(1)}, bf16[256,128]{1,0:T(8,128)(2,1)S(1)}, u32[]{:S(2)}, u32[]{:S(2)}) collective-permute-start(bf16[256,128]{1,0:T(8,128)(2,1)S(1)} %get-tuple-element.43.mine_ref), channel_id=1, source_target_pairs={{1,0},{0,1},{3,2},{2,3},{5,4},{4,5},{7,6},{6,7},{9,8},{8,9},{11,10... | collective-permute-start | bytes 196616 | tf_op jit(solution)/shard_map/ppermute | solution.py:56
  65.5 9.6 %collective-permute-start.16 = (bf16[4,128,512]{2,1,0:T(8,128)(2,1)S(1)}, bf16[4,128,512]{2,1,0:T(8,128)(2,1)S(1)}, u32[]{:S(2)}, u32[]{:S(2)}) collective-permute-start(bf16[4,128,512]{2,1,0:T(8,128)(2,1)S(1)} %shard_map.164), channel_id=1, source_target_pairs={{2,0},{3,1},{0,2},{1,3},{6,4},{7,5},{4,6},{5,7},{10,8},{11,9},{8,1... | collective-permute-start | bytes 1572872 | tf_op jit(solution)/shard_map/ppermute | solution.py:56
  65.6 2.0 %collective-permute-start.18 = (f32[2,72,128]{2,1,0:T(8,128)S(1)}, f32[2,72,128]{2,1,0:T(8,128)S(1)}, u32[]{:S(2)}, u32[]{:S(2)}) collective-permute-start(f32[2,72,128]{2,1,0:T(8,128)S(1)} %get-tuple-element.54), channel_id=1, source_target_pairs={{2,0},{3,1},{0,2},{1,3},{6,4},{7,5},{4,6},{5,7},{10,8},{11,9},{8,1... | collective-permute-start | bytes 221192 | tf_op jit(solution)/shard_map/ppermute | solution.py:56
  67.4 20.1 %collective-permute-start.15 = (bf16[5,128,512]{2,1,0:T(8,128)(2,1)S(1)}, bf16[5,128,512]{2,1,0:T(8,128)(2,1)S(1)}, u32[]{:S(2)}, u32[]{:S(2)}) collective-permute-start(bf16[5,128,512]{2,1,0:T(8,128)(2,1)S(1)} %shard_map.162), channel_id=1, source_target_pairs={{2,0},{3,1},{0,2},{1,3},{6,4},{7,5},{4,6},{5,7},{10,8},{11,9},{8,1... | collective-permute-start | bytes 1966088 | tf_op jit(solution)/shard_map/ppermute | solution.py:56
  67.6 9.4 %collective-permute-start.19 = (f32[72,128]{1,0:T(8,128)S(1)}, f32[72,128]{1,0:T(8,128)S(1)}, u32[]{:S(2)}, u32[]{:S(2)}) collective-permute-start(f32[72,128]{1,0:T(8,128)S(1)} %slice_bitcast_fusion), channel_id=1, source_target_pairs={{4,0},{5,1},{6,2},{7,3},{0,4},{1,5},{2,6},{3,7},{12,8},{13,9},{14,... | collective-permute-start | bytes 110600 | tf_op jit(solution)/shard_map/ppermute | solution.py:56
  76.3 14.6 %collective-permute-start.17 = (bf16[4,128,512]{2,1,0:T(8,128)(2,1)S(1)}, bf16[4,128,512]{2,1,0:T(8,128)(2,1)S(1)}, u32[]{:S(2)}, u32[]{:S(2)}) collective-permute-start(bf16[4,128,512]{2,1,0:T(8,128)(2,1)S(1)} %shard_map.165), channel_id=1, source_target_pairs={{0,96},{1,33},{2,98},{3,35},{4,100},{5,37},{6,102},{7,39},{8,104},... | collective-permute-start | bytes 1572872 | tf_op jit(solution)/shard_map/ppermute | solution.py:56
  77.1 4.1 %collective-permute-start.20 = (f32[72,128]{1,0:T(8,128)S(1)}, f32[72,128]{1,0:T(8,128)S(1)}, u32[]{:S(2)}, u32[]{:S(2)}) collective-permute-start(f32[72,128]{1,0:T(8,128)S(1)} %fusion), channel_id=1, source_target_pairs={{8,0},{9,1},{10,2},{11,3},{12,4},{13,5},{14,6},{15,7},{0,8},{1,9},... | collective-permute-start | bytes 110600 | tf_op jit(solution)/shard_map/ppermute | solution.py:56
  77.1 5.2 %collective-permute-start.21 = (f32[72,128]{1,0:T(8,128)S(1)}, f32[72,128]{1,0:T(8,128)S(1)}, u32[]{:S(2)}, u32[]{:S(2)}) collective-permute-start(f32[72,128]{1,0:T(8,128)S(1)} %fusion), channel_id=1, source_target_pairs={{24,0},{25,1},{26,2},{27,3},{28,4},{29,5},{30,6},{31,7},{16,8},{17... | collective-permute-start | bytes 110600 | tf_op jit(solution)/shard_map/ppermute | solution.py:56
  77.2 5.9 %collective-permute-start.22 = (f32[72,128]{1,0:T(8,128)S(1)}, f32[72,128]{1,0:T(8,128)S(1)}, u32[]{:S(2)}, u32[]{:S(2)}) collective-permute-start(f32[72,128]{1,0:T(8,128)S(1)} %fusion), channel_id=1, source_target_pairs={{16,0},{17,1},{18,2},{19,3},{20,4},{21,5},{22,6},{23,7},{24,8},{25... | collective-permute-start | bytes 110600 | tf_op jit(solution)/shard_map/ppermute | solution.py:56
  83.1 11.2 %collective-permute-start.30 = (f32[72,128]{1,0:T(8,128)S(1)}, f32[72,128]{1,0:T(8,128)S(1)}, u32[]{:S(2)}, u32[]{:S(2)}) collective-permute-start(f32[72,128]{1,0:T(8,128)S(1)} %add_add_fusion.1), channel_id=1, source_target_pairs={{32,0},{33,1},{34,2},{35,3},{36,4},{37,5},{38,6},{39,7},{40,8},{41... | collective-permute-start | bytes 110600 | tf_op jit(solution)/shard_map/ppermute | solution.py:56
  84.8 9.9 %collective-permute-start.31 = (f32[72,128]{1,0:T(8,128)S(1)}, f32[72,128]{1,0:T(8,128)S(1)}, u32[]{:S(2)}, u32[]{:S(2)}) collective-permute-start(f32[72,128]{1,0:T(8,128)S(1)} %add_add_fusion.1), channel_id=1, source_target_pairs={{96,0},{97,1},{98,2},{99,3},{100,4},{101,5},{102,6},{103,7},{104,8... | collective-permute-start | bytes 110600 | tf_op jit(solution)/shard_map/ppermute | solution.py:56
  84.8 12.6 %collective-permute-start.32 = (f32[72,128]{1,0:T(8,128)S(1)}, f32[72,128]{1,0:T(8,128)S(1)}, u32[]{:S(2)}, u32[]{:S(2)}) collective-permute-start(f32[72,128]{1,0:T(8,128)S(1)} %add_add_fusion.1), channel_id=1, source_target_pairs={{64,0},{65,1},{66,2},{67,3},{68,4},{69,5},{70,6},{71,7},{72,8},{73... | collective-permute-start | bytes 110600 | tf_op jit(solution)/shard_map/ppermute | solution.py:56
  91.5 6.6 %collective-permute-start.23 = (bf16[128,512]{1,0:T(8,128)(2,1)S(1)}, bf16[128,512]{1,0:T(8,128)(2,1)S(1)}, u32[]{:S(2)}, u32[]{:S(2)}) collective-permute-start(bf16[128,512]{1,0:T(8,128)(2,1)S(1)} %get-tuple-element.56), channel_id=1, source_target_pairs={{0,120},{1,9},{2,122},{3,11},{4,124},{5,13},{6,126},{7,15},{8,0},{... | collective-permute-start | bytes 393224 | tf_op jit(solution)/shard_map/ppermute | solution.py:56
  92.3 7.5 %collective-permute-start.24 = (bf16[128,512]{1,0:T(8,128)(2,1)S(1)}, bf16[128,512]{1,0:T(8,128)(2,1)S(1)}, u32[]{:S(2)}, u32[]{:S(2)}) collective-permute-start(bf16[128,512]{1,0:T(8,128)(2,1)S(1)} %get-tuple-element.57), channel_id=1, source_target_pairs={{0,112},{1,17},{2,114},{3,19},{4,116},{5,21},{6,118},{7,23},{8,120... | collective-permute-start | bytes 393224 | tf_op jit(solution)/shard_map/ppermute | solution.py:56
  94.4 6.8 %collective-permute-start.25 = (bf16[128,512]{1,0:T(8,128)(2,1)S(1)}, bf16[128,512]{1,0:T(8,128)(2,1)S(1)}, u32[]{:S(2)}, u32[]{:S(2)}) collective-permute-start(bf16[128,512]{1,0:T(8,128)(2,1)S(1)} %get-tuple-element.58), channel_id=1, source_target_pairs={{0,104},{1,25},{2,106},{3,27},{4,108},{5,29},{6,110},{7,31},{8,112... | collective-permute-start | bytes 393224 | tf_op jit(solution)/shard_map/ppermute | solution.py:56
  94.7 8.2 %collective-permute-start.26 = (bf16[128,512]{1,0:T(8,128)(2,1)S(1)}, bf16[128,512]{1,0:T(8,128)(2,1)S(1)}, u32[]{:S(2)}, u32[]{:S(2)}) collective-permute-start(bf16[128,512]{1,0:T(8,128)(2,1)S(1)} %get-tuple-element.59), channel_id=1, source_target_pairs={{0,96},{1,33},{2,98},{3,35},{4,100},{5,37},{6,102},{7,39},{8,104},... | collective-permute-start | bytes 393224 | tf_op jit(solution)/shard_map/ppermute | solution.py:56
  97.4 10.9 %collective-permute-start.33 = (f32[72,128]{1,0:T(8,128)S(1)}, f32[72,128]{1,0:T(8,128)S(1)}, u32[]{:S(2)}, u32[]{:S(2)}) collective-permute-start(f32[72,128]{1,0:T(8,128)S(1)} %add_add_fusion.refs_5_), channel_id=1, source_target_pairs={{4,0},{5,1},{6,2},{7,3},{0,4},{1,5},{2,6},{3,7},{12,8},{13,9},{14,... | collective-permute-start | bytes 110600 | tf_op jit(solution)/shard_map/ppermute | solution.py:56
  103.5 6.1 %collective-permute-start.27 = (bf16[128,256]{1,0:T(8,128)(2,1)S(1)}, bf16[128,256]{1,0:T(8,128)(2,1)S(1)}, u32[]{:S(2)}, u32[]{:S(2)}) collective-permute-start(bf16[128,256]{1,0:T(8,128)(2,1)S(1)} %get-tuple-element.60.refs_0_), channel_id=1, source_target_pairs={{1,0},{0,1},{3,2},{2,3},{5,4},{4,5},{7,6},{6,7},{9,8},{8,9},{11,10... | collective-permute-start | bytes 196616 | tf_op jit(solution)/shard_map/ppermute | solution.py:56
  104.9 5.7 %collective-permute-start.28 = (bf16[128,256]{1,0:T(8,128)(2,1)S(1)}, bf16[128,256]{1,0:T(8,128)(2,1)S(1)}, u32[]{:S(2)}, u32[]{:S(2)}) collective-permute-start(bf16[128,256]{1,0:T(8,128)(2,1)S(1)} %get-tuple-element.61), channel_id=1, source_target_pairs={{5,0},{4,1},{7,2},{6,3},{0,4},{1,5},{2,6},{3,7},{13,8},{12,9},{15,... | collective-permute-start | bytes 196616 | tf_op jit(solution)/shard_map/ppermute | solution.py:56
  105.7 4.8 %collective-permute-start.29 = (bf16[128,256]{1,0:T(8,128)(2,1)S(1)}, bf16[128,256]{1,0:T(8,128)(2,1)S(1)}, u32[]{:S(2)}, u32[]{:S(2)}) collective-permute-start(bf16[128,256]{1,0:T(8,128)(2,1)S(1)} %get-tuple-element.61), channel_id=1, source_target_pairs={{4,0},{5,1},{6,2},{7,3},{1,4},{0,5},{3,6},{2,7},{12,8},{13,9},{14,... | collective-permute-start | bytes 196616 | tf_op jit(solution)/shard_map/ppermute | solution.py:56
  108.3 1.2 %collective-permute-start.34 = (f32[72,128]{1,0:T(8,128)S(1)}, f32[72,128]{1,0:T(8,128)S(1)}, u32[]{:S(2)}, u32[]{:S(2)}) collective-permute-start(f32[72,128]{1,0:T(8,128)S(1)} %add_add_fusion.refs_5_), channel_id=1, source_target_pairs={{2,0},{3,1},{0,2},{1,3},{6,4},{7,5},{4,6},{5,7},{10,8},{11,9},{8,1... | collective-permute-start | bytes 110600 | tf_op jit(solution)/shard_map/ppermute | solution.py:56
  108.3 1.4 %collective-permute-start.35 = (f32[72,128]{1,0:T(8,128)S(1)}, f32[72,128]{1,0:T(8,128)S(1)}, u32[]{:S(2)}, u32[]{:S(2)}) collective-permute-start(f32[72,128]{1,0:T(8,128)S(1)} %collective-permute-done.33.refs_6_), channel_id=1, source_target_pairs={{2,0},{3,1},{0,2},{1,3},{6,4},{7,5},{4,6},{5,7},{10,8},{11,9},{8,1... | collective-permute-start | bytes 110600 | tf_op jit(solution)/shard_map/ppermute | solution.py:56
